TPU v7x, 512 devices: a whole 4x8x8 slice. The times are simulated.
512 devices in a mesh: curve: 64 (over z, x, core), split: 8 (over y).
Axes of the slice: x: 4, y: 8, z: 8, core: 2. Of those that a mesh axis runs over, the one named last changes fastest.
Arguments:
- rhs_load: float32 [8192, 512], P(('curve', 'split')), may hold values from -6 to 6
- stretch: float32 [3, 8192], P(None, ('curve', 'split')), may hold values from 0.5 to 4
- helm_shift: float32 [8192], P(('curve', 'split')), may hold values from 100 to 1000
- local_slot: int32 [8192, 512], P(('curve', 'split')), may hold values from 0 to 5487, as said below
- share_curve: int32 [64, 8, 4, 128], P('curve', 'split'), may hold values from 0 to 5488, as said below
- share_split: int32 [64, 8, 2, 128], P('curve', 'split'), may hold values from 0 to 5488, as said below
- coarse_slot: int32 [8, 8192], P(None, ('curve', 'split')), may hold values from 0 to 15
- x_vals: float32 [16, 8192], P(None, ('curve', 'split')), may hold values from -4 to 4
- x_cols: int32 [16, 8192], P(None, ('curve', 'split')), may hold values from 0 to 8191, as said below
- x_count: int32 [8192], P(('curve', 'split')), may hold values from 1 to 16, as said below
Outputs:
- solution: float32 [8192, 512], P(('curve', 'split'))
- residual: float32 [8192, 512], P(('curve', 'split'))
Inputs may be any that keep to these rules, and one draw needn't show every extreme that they name: `local_slot`: every slot 0 to 5487 of a device's node vector is named by one or more of its points. `share_curve`: each entry is a node slot of the device, or 5488 for an empty entry; the slots of one list are distinct; the list of device (c, s) for offset o and the partner's list for offset -o name shared nodes entry by entry and have equal numbers of filled entries, which come first; lists towards partitions that do not exist are empty; some list is full in every draw. `share_split`: as for share_curve, with partner (c, s + o) for the offsets -1 and 1. `x_cols`: entry 0 of row i is i; entries 1 to 7 lie within 32 of i; the later entries lie among the coarse unknowns of separator devices of a nested dissection of the device numbers, one level an entry. `x_count`: some rows use all 16 entries.
All inputs are finite; a program needn't handle non-finite values.
Results may differ from a plain program's by a relative error of at most 0.0009.
Values sent between devices are 32-bit elements; how exact they have to be, the bound alone decides.
No kernel may reach another device: no remote copies, remote signals or barrier semaphores. Data moves between devices by JAX's collectives and lax.ppermute only.
A program may use at most 64 MiB of HBM per device.

v0:
```python
import jax
import jax.numpy as jnp
import numpy as np
from jax import lax
from jax.sharding import PartitionSpec as P

ITERS = 4


def from_behind(block, axis, distance):
    devices = range(lax.axis_size(axis))
    route = [(i - distance, i) for i in devices if i - distance in devices]
    return lax.ppermute(block, axis, route)


def element_tables():
    poly_order = 7
    node_count = poly_order + 1
    gll_nodes = -np.cos(np.pi * np.arange(node_count) / poly_order)
    legendre = np.zeros((node_count, node_count))
    for sweep in range(60):
        legendre[:, 0] = 1.0
        legendre[:, 1] = gll_nodes
        for degree in range(2, node_count):
            legendre[:, degree] = (
                (2 * degree - 1) * gll_nodes * legendre[:, degree - 1]
                - (degree - 1) * legendre[:, degree - 2]
            ) / degree
        gll_nodes = gll_nodes - (
            gll_nodes * legendre[:, poly_order] - legendre[:, poly_order - 1]
        ) / (node_count * legendre[:, poly_order])
    for degree in range(2, node_count):
        legendre[:, degree] = (
            (2 * degree - 1) * gll_nodes * legendre[:, degree - 1]
            - (degree - 1) * legendre[:, degree - 2]
        ) / degree
    top_poly = legendre[:, poly_order]
    quad_weights = 2.0 / (poly_order * node_count * top_poly * top_poly)
    deriv_matrix = np.zeros((node_count, node_count))
    for row_index in range(node_count):
        for col_index in range(node_count):
            if row_index != col_index:
                deriv_matrix[row_index, col_index] = top_poly[row_index] / (
                    top_poly[col_index] * (gll_nodes[row_index] - gll_nodes[col_index])
                )
    deriv_matrix[0, 0] = -poly_order * node_count / 4.0
    deriv_matrix[poly_order, poly_order] = poly_order * node_count / 4.0
    identity = np.eye(node_count)
    mass_diag = (
        quad_weights[:, None, None] * quad_weights[None, :, None] * quad_weights[None, None, :]
    ).reshape(-1)
    stiff_list = []
    for deriv_kron in (
        np.kron(np.kron(deriv_matrix, identity), identity),
        np.kron(np.kron(identity, deriv_matrix), identity),
        np.kron(identity, np.kron(identity, deriv_matrix)),
    ):
        stiff_list.append(deriv_kron.T @ (mass_diag[:, None] * deriv_kron))
    stiffness = np.concatenate(stiff_list, axis=1)
    diag_index = np.arange(stiff_list[0].shape[0])
    stiff_diag = np.stack([block[diag_index, diag_index] for block in stiff_list])
    hat_values = np.stack([(1.0 - gll_nodes) / 2.0, (1.0 + gll_nodes) / 2.0])
    coarse_table = (
        hat_values[:, None, None, :, None, None]
        * hat_values[None, :, None, None, :, None]
        * hat_values[None, None, :, None, None, :]
    ).reshape(8, -1)
    return (mass_diag, stiffness, stiff_diag, coarse_table)


def local_operator(element_field, stiffness, mass_diag, stretch, helm_shift):
    products = jnp.dot(
        element_field,
        stiffness,
        precision=lax.Precision.HIGHEST,
        preferred_element_type=jnp.float32,
    )
    point_count = element_field.shape[1]
    result = stretch[0][:, None] * products[:, :point_count]
    result = result + stretch[1][:, None] * products[:, point_count : 2 * point_count]
    result = result + stretch[2][:, None] * products[:, 2 * point_count :]
    return result + helm_shift[:, None] * mass_diag[None, :] * element_field


def assemble(fields, point_slots, curve_lists, split_lists, node_count):
    batch_count = fields.shape[0]
    flattened = fields.reshape(batch_count, -1)
    node_sums = jax.vmap(
        lambda values: jax.ops.segment_sum(values, point_slots, num_segments=node_count + 1)
    )(flattened)
    assembled = node_sums
    for list_index, offset in enumerate((-1, 1)):
        outgoing = node_sums[:, split_lists[1 - list_index]]
        incoming = from_behind(outgoing, "split", -offset)
        assembled = assembled.at[:, split_lists[list_index]].add(incoming)
    reach = curve_lists.shape[0] // 2
    curve_offsets = list(range(-reach, 0)) + list(range(1, reach + 1))
    for list_index, offset in enumerate(curve_offsets):
        outgoing = node_sums[:, curve_lists[2 * reach - 1 - list_index]]
        incoming = from_behind(outgoing, "curve", -offset)
        assembled = assembled.at[:, curve_lists[list_index]].add(incoming)
    return assembled[:, point_slots].reshape(fields.shape)


def local(
    rhs_load,
    stretch,
    helm_shift,
    local_slot,
    share_curve,
    share_split,
    coarse_slot,
    x_vals,
    x_cols,
    x_count,
):
    mass_np, stiff_np, sdiag_np, coarse_np = element_tables()
    mass_diag = jnp.asarray(mass_np, dtype=jnp.float32)
    stiffness = jnp.asarray(stiff_np, dtype=jnp.float32)
    stiff_diag = jnp.asarray(sdiag_np, dtype=jnp.float32)
    coarse_table = jnp.asarray(coarse_np, dtype=jnp.float32)
    element_count = rhs_load.shape[0]
    node_count = 343 * element_count
    point_slots = local_slot.reshape(-1)
    curve_lists = share_curve.reshape(share_curve.shape[2], share_curve.shape[3])
    split_lists = share_split.reshape(share_split.shape[2], share_split.shape[3])
    coarse_rows = x_vals.shape[1]
    total_coarse = coarse_rows * lax.axis_size("curve") * lax.axis_size("split")
    diag_local = (
        stretch[0][:, None] * stiff_diag[0][None, :] + stretch[1][:, None] * stiff_diag[1][None, :]
    )
    diag_local = (
        diag_local
        + stretch[2][:, None] * stiff_diag[2][None, :]
        + helm_shift[:, None] * mass_diag[None, :]
    )
    setup = assemble(
        jnp.stack([jnp.ones_like(rhs_load), diag_local, rhs_load]),
        point_slots,
        curve_lists,
        split_lists,
        node_count,
    )
    multiplicity = setup[0]
    diag_a = setup[1]
    right = setup[2]
    live_entry = jnp.arange(x_vals.shape[0])[:, None] < x_count[None, :]
    factor = jnp.where(live_entry, x_vals, jnp.zeros_like(x_vals))

    def global_dot(left_field, right_field):
        return lax.psum(jnp.sum(left_field * right_field / multiplicity), ("curve", "split"))

    def coarse_partial(scaled):
        restricted = lax.dot_general(
            coarse_table,
            scaled,
            (((1,), (1,)), ((), ())),
            precision=lax.Precision.HIGHEST,
            preferred_element_type=jnp.float32,
        )
        loads = jax.ops.segment_sum(
            restricted.reshape(-1), coarse_slot.reshape(-1), num_segments=coarse_rows
        )
        return jax.ops.segment_sum(
            (factor * loads[None, :]).reshape(-1), x_cols.reshape(-1), num_segments=total_coarse
        )

    def coarse_correction(coarse_image):
        coarse_values = jnp.sum(factor * coarse_image[x_cols], axis=0)
        vertex_values = coarse_values[coarse_slot]
        return lax.dot_general(
            vertex_values,
            coarse_table,
            (((0,), (0,)), ((), ())),
            precision=lax.Precision.HIGHEST,
            preferred_element_type=jnp.float32,
        )

    def precondition(residual_field):
        scaled = residual_field / multiplicity
        partial_image = coarse_partial(scaled)
        jacobi_part = residual_field / diag_a
        coarse_image = lax.psum(partial_image, ("curve", "split"))
        precond_field = jacobi_part + coarse_correction(coarse_image)
        precond_norm = global_dot(residual_field, precond_field)
        return (precond_field, precond_norm)

    solution = jnp.zeros_like(rhs_load)
    residual = right
    precond, rz_value = precondition(residual)
    direction = precond
    for iteration in range(ITERS):
        image = assemble(
            local_operator(direction, stiffness, mass_diag, stretch, helm_shift)[None],
            point_slots,
            curve_lists,
            split_lists,
            node_count,
        )[0]
        step_size = rz_value / global_dot(direction, image)
        solution = solution + step_size * direction
        residual = residual - step_size * image
        if iteration < ITERS - 1:
            precond, rz_next = precondition(residual)
            direction = precond + rz_next / rz_value * direction
            rz_value = rz_next
    return (solution, residual)


def solution(mesh):
    in_specs = (
        P(("curve", "split"), None),
        P(None, ("curve", "split")),
        P(("curve", "split")),
        P(("curve", "split"), None),
        P("curve", "split", None, None),
        P("curve", "split", None, None),
        P(None, ("curve", "split")),
        P(None, ("curve", "split")),
        P(None, ("curve", "split")),
        P(("curve", "split")),
    )
    out_specs = (P(("curve", "split"), None), P(("curve", "split"), None))
    return jax.shard_map(local, mesh=mesh, in_specs=in_specs, out_specs=out_specs, check_vma=False)
```

profile of v0, /device:TPU:1, one launch (start us, length us, event | category | flops | bytes accessed | tf_op | source)
XLA Modules:
  0.0 1746.0 jit_solution(16968491514519512765)
XLA Ops:
  9.2 45.0 %scatter_custom_fusion = f32[3,5489]{0,1:T(8,128)S(1)} fusion(s32[8192]{0:T(1024)S(1)} %bitcast.195, f32[8192,3]{1,0:T(8,128)} %copy.18, f32[]{:T(128)} %constant.10.clone.1), kind=kCustom, calls=%fused_computation.89 | custom fusion | flops 24576 | bytes 66380 | tf_op jit(solution)/shard_map/vmap()/scatter-add | solution.py:89
  55.4 4.0 collective-permute-start
  66.4 4.2 collective-permute-start.3
  91.3 27.7 %gather_fusion.6 = f32[8192,3]{1,0:T(8,128)} fusion(f32[3,5489]{0,1:T(8,128)S(1)} %scatter_custom_fusion.6, s32[8192]{0:T(1024)S(1)} %broadcast_clamp_fusion), kind=kCustom, calls=%fused_computation.6 | custom fusion | bytes 229376 | tf_op jit(solution)/shard_map/gather | solution.py:102
  119.0 10.2 slice_reduce_fusion.1
  133.3 107.6 %psum.84 = f32[8192]{0:T(1024)S(1)} all-reduce(f32[8192]{0:T(1024)S(1)} %scatter_custom_fusion.8), channel_id=1, replica_groups=mesh['curve'=64,'split'=8] {'curve','split'}, use_global_device_ids=true, to_apply=%region_9.10 | all-reduce | flops 8192 | bytes 65536 | tf_op jit(solution)/shard_map/psum | solution.py:183
  246.2 43.4 %scatter_custom_fusion.9 = f32[5489]{0:T(1024)S(1)} fusion(s32[8192]{0:T(1024)S(1)} %bitcast.196, f32[8192]{0:T(1024)S(1)} %bitcast.201, f32[]{:T(128)} %constant.10.clone.1), kind=kCustom, calls=%fused_computation.198 | custom fusion | flops 8192 | bytes 21960 | tf_op jit(solution)/shard_map/vmap()/scatter-add | solution.py:89
  294.8 3.7 collective-permute-start.6
  302.3 3.7 collective-permute-start.8
  320.3 45.5 %gather_fusion.15 = f32[8192]{0:T(1024)S(1)} fusion(f32[5489]{0:T(1024)S(1)} %scatter_fusion.5, s32[8192]{0:T(1024)S(1)} %broadcast_clamp_fusion), kind=kCustom, calls=%fused_computation.15 | custom fusion | bytes 98304 | tf_op jit(solution)/shard_map/gather | solution.py:102
  366.5 100.7 %all-reduce = (f32[]{:T(128)}, f32[]{:T(128)}) all-reduce(f32[]{:T(128)} %get-tuple-element.6, f32[]{:T(128)} %get-tuple-element.5), channel_id=1, replica_groups=mesh['curve'=64,'split'=8] {'curve','split'}, use_global_device_ids=true, to_apply=%region_12.13 | all-reduce | flops 2 | bytes 16 | tf_op jit(solution)/shard_map/psum | solution.py:151
  473.0 95.6 %psum.87 = f32[8192]{0:T(1024)S(1)} all-reduce(f32[8192]{0:T(1024)S(1)} %scatter_custom_fusion.17), channel_id=1, replica_groups=mesh['curve'=64,'split'=8] {'curve','split'}, use_global_device_ids=true, to_apply=%region_24.25 | all-reduce | flops 8192 | bytes 65536 | tf_op jit(solution)/shard_map/psum | solution.py:183
  572.6 95.4 %psum.88 = f32[]{:T(128)} all-reduce(f32[]{:T(128)} %get-tuple-element.18), channel_id=1, replica_groups=mesh['curve'=64,'split'=8] {'curve','split'}, use_global_device_ids=true, to_apply=%region_27.28 | all-reduce | flops 1 | bytes 8 | tf_op jit(solution)/shard_map/psum | solution.py:151
  671.0 43.2 %scatter_custom_fusion.18 = f32[5489]{0:T(1024)S(1)} fusion(s32[8192]{0:T(1024)S(1)} %bitcast.197, f32[8192]{0:T(1024)S(1)} %bitcast.202, f32[]{:T(128)} %constant.10.clone.1), kind=kCustom, calls=%fused_computation.196 | custom fusion | flops 8192 | bytes 21960 | tf_op jit(solution)/shard_map/vmap()/scatter-add | solution.py:89
  719.3 4.2 collective-permute-start.12
  727.4 3.7 collective-permute-start.14
  745.3 45.5 %gather_fusion.24 = f32[8192]{0:T(1024)S(1)} fusion(f32[5489]{0:T(1024)S(1)} %scatter_fusion.11, s32[8192]{0:T(1024)S(1)} %broadcast_clamp_fusion), kind=kCustom, calls=%fused_computation.24 | custom fusion | bytes 98304 | tf_op jit(solution)/shard_map/gather | solution.py:102
  791.5 101.1 %psum.89 = f32[]{:T(128)} all-reduce(f32[]{:T(128)} %fusion.33), channel_id=1, replica_groups=mesh['curve'=64,'split'=8] {'curve','split'}, use_global_device_ids=true, to_apply=%region_36.37 | all-reduce | flops 1 | bytes 8 | tf_op jit(solution)/shard_map/psum | solution.py:151
  898.5 95.7 %psum.90 = f32[8192]{0:T(1024)S(1)} all-reduce(f32[8192]{0:T(1024)S(1)} %scatter_custom_fusion.26), channel_id=1, replica_groups=mesh['curve'=64,'split'=8] {'curve','split'}, use_global_device_ids=true, to_apply=%region_39.40 | all-reduce | flops 8192 | bytes 65536 | tf_op jit(solution)/shard_map/psum | solution.py:183
  998.2 95.0 %psum.91 = f32[]{:T(128)} all-reduce(f32[]{:T(128)} %get-tuple-element.20), channel_id=1, replica_groups=mesh['curve'=64,'split'=8] {'curve','split'}, use_global_device_ids=true, to_apply=%region_42.43 | all-reduce | flops 1 | bytes 8 | tf_op jit(solution)/shard_map/psum | solution.py:151
  1096.2 43.2 %scatter_custom_fusion.27 = f32[5489]{0:T(1024)S(1)} fusion(s32[8192]{0:T(1024)S(1)} %bitcast.198, f32[8192]{0:T(1024)S(1)} %bitcast.203, f32[]{:T(128)} %constant.10.clone.1), kind=kCustom, calls=%fused_computation.194 | custom fusion | flops 8192 | bytes 21960 | tf_op jit(solution)/shard_map/vmap()/scatter-add | solution.py:89
  1144.5 4.2 collective-permute-start.18
  1152.6 3.7 collective-permute-start.20
  1170.7 45.5 %gather_fusion.33 = f32[8192]{0:T(1024)S(1)} fusion(f32[5489]{0:T(1024)S(1)} %scatter_fusion.17, s32[8192]{0:T(1024)S(1)} %broadcast_clamp_fusion), kind=kCustom, calls=%fused_computation.33 | custom fusion | bytes 98304 | tf_op jit(solution)/shard_map/gather | solution.py:102
  1216.9 101.1 %psum.92 = f32[]{:T(128)} all-reduce(f32[]{:T(128)} %fusion.35), channel_id=1, replica_groups=mesh['curve'=64,'split'=8] {'curve','split'}, use_global_device_ids=true, to_apply=%region_51.52 | all-reduce | flops 1 | bytes 8 | tf_op jit(solution)/shard_map/psum | solution.py:151
  1323.7 95.6 %psum.93 = f32[8192]{0:T(1024)S(1)} all-reduce(f32[8192]{0:T(1024)S(1)} %scatter_custom_fusion.35), channel_id=1, replica_groups=mesh['curve'=64,'split'=8] {'curve','split'}, use_global_device_ids=true, to_apply=%region_54.55 | all-reduce | flops 8192 | bytes 65536 | tf_op jit(solution)/shard_map/psum | solution.py:183
  1423.3 94.9 %psum.94 = f32[]{:T(128)} all-reduce(f32[]{:T(128)} %get-tuple-element.22), channel_id=1, replica_groups=mesh['curve'=64,'split'=8] {'curve','split'}, use_global_device_ids=true, to_apply=%region_57.58 | all-reduce | flops 1 | bytes 8 | tf_op jit(solution)/shard_map/psum | solution.py:151
  1521.3 43.2 %scatter_custom_fusion.36 = f32[5489]{0:T(1024)S(1)} fusion(s32[8192]{0:T(1024)S(1)} %bitcast.199, f32[8192]{0:T(1024)S(1)} %bitcast.200, f32[]{:T(128)} %constant.10.clone.1), kind=kCustom, calls=%fused_computation.192 | custom fusion | flops 8192 | bytes 21960 | tf_op jit(solution)/shard_map/vmap()/scatter-add | solution.py:89
  1569.6 4.2 collective-permute-start.24
  1577.6 3.7 collective-permute-start.26
  1595.8 45.5 %gather_fusion.42 = f32[8192]{0:T(1024)S(1)} fusion(f32[5489]{0:T(1024)S(1)} %scatter_fusion.23, s32[8192]{0:T(1024)S(1)} %broadcast_clamp_fusion), kind=kCustom, calls=%fused_computation.42 | custom fusion | bytes 98304 | tf_op jit(solution)/shard_map/gather | solution.py:102
  1642.0 101.1 %psum.95 = f32[]{:T(128)} all-reduce(f32[]{:T(128)} %fusion.37), channel_id=1, replica_groups=mesh['curve'=64,'split'=8] {'curve','split'}, use_global_device_ids=true, to_apply=%region_66.67 | all-reduce | flops 1 | bytes 8 | tf_op jit(solution)/shard_map/psum | solution.py:151
  (281 shorter events, 173.2 us)
Async XLA Ops:
  1.4 1094.7 %copy-start.8 = (f32[16]{0:T(128)}, f32[16]{0:T(128)S(1)}, u32[]{:S(2)}) copy-start(f32[16]{0:T(128)S(1)} %get-tuple-element.14) | copy-start | bytes 196
  1.4 1094.7 %copy-start.10 = (f32[16]{0:T(128)}, f32[16]{0:T(128)S(1)}, u32[]{:S(2)}) copy-start(f32[16]{0:T(128)S(1)} %get-tuple-element.15) | copy-start | bytes 196
  55.4 20.0 %collective-permute-start = (f32[3,128]{0,1:T(8,128)}, f32[3,128]{0,1:T(8,128)S(1)}, u32[]{:S(2)}, u32[]{:S(2)}) collective-permute-start(f32[3,128]{0,1:T(8,128)} %bitcast.8), channel_id=1, source_target_pairs={{0,1},{1,2},{2,3},{3,4},{4,5},{5,6},{6,7},{8,9},{9,10},{10,11},{11... | collective-permute-start | bytes 4616 | tf_op jit(solution)/shard_map/ppermute | solution.py:13
  60.1 19.3 %collective-permute-start.1 = (f32[3,128]{0,1:T(8,128)S(1)}, f32[3,128]{0,1:T(8,128)S(1)}, u32[]{:S(2)}, u32[]{:S(2)}) collective-permute-start(f32[3,128]{0,1:T(8,128)S(1)} %bitcast.252), channel_id=1, source_target_pairs={{1,0},{2,1},{3,2},{4,3},{5,4},{6,5},{7,6},{9,8},{10,9},{11,10},{12... | collective-permute-start | bytes 4616 | tf_op jit(solution)/shard_map/ppermute | solution.py:13
  62.7 19.0 %collective-permute-start.2 = (f32[3,128]{0,1:T(8,128)}, f32[3,128]{0,1:T(8,128)S(1)}, u32[]{:S(2)}, u32[]{:S(2)}) collective-permute-start(f32[3,128]{0,1:T(8,128)} %bitcast.16), channel_id=1, source_target_pairs={{0,16},{8,24},{16,32},{24,40},{32,48},{40,56},{48,64},{56,72},{64,... | collective-permute-start | bytes 4616 | tf_op jit(solution)/shard_map/ppermute | solution.py:13
  66.4 17.8 %collective-permute-start.3 = (f32[3,128]{0,1:T(8,128)S(1)}, f32[3,128]{0,1:T(8,128)S(1)}, u32[]{:S(2)}, u32[]{:S(2)}) collective-permute-start(f32[3,128]{0,1:T(8,128)S(1)} %bitcast.253), channel_id=1, source_target_pairs={{0,8},{8,16},{16,24},{24,32},{32,40},{40,48},{48,56},{56,64},{64,7... | collective-permute-start | bytes 4616 | tf_op jit(solution)/shard_map/ppermute | solution.py:13
  71.9 14.5 collective-permute-start.4
  75.4 13.4 collective-permute-start.5
  294.8 16.0 collective-permute-start.6
  301.0 12.5 collective-permute-start.7
  302.3 12.5 collective-permute-start.8
  306.0 10.4 collective-permute-start.9
  308.9 8.8 collective-permute-start.10
  310.8 8.2 collective-permute-start.11
  719.3 16.4 collective-permute-start.12
  726.1 12.5 collective-permute-start.13
  727.4 12.5 collective-permute-start.14
  731.0 10.3 collective-permute-start.15
  733.8 8.8 collective-permute-start.16
  735.7 8.2 collective-permute-start.17
  1144.5 16.4 collective-permute-start.18
  1151.3 12.5 collective-permute-start.19
  1152.6 12.5 collective-permute-start.20
  1156.2 10.3 collective-permute-start.21
  1159.0 8.8 collective-permute-start.22
  1160.9 8.4 collective-permute-start.23
  1569.6 16.7 collective-permute-start.24
  1576.3 12.7 collective-permute-start.25
  1577.6 12.7 collective-permute-start.26
  1581.3 10.6 collective-permute-start.27
  1584.1 9.1 collective-permute-start.28
  1586.3 8.2 collective-permute-start.29
  (25 other events, 2192.2 us)
where the time goes:
time: 1760 us; the launch traced here: 1750 us
  blocking collectives  1080 us (61%)
  other arithmetic  286 us (16%)
  local copies, waits for them, and re-layouts  279 us (16%)
  starting transfers between devices  76.1 us (4%)
    psum x7, blocking collectives, global_dot(): lax.psum(jnp.sum(left_field * right_field / multiplicity), ('curve', 'spl...  689 us
    psum x4, blocking collectives, precondition(): coarse_image = lax.psum(partial_image, ('curve', 'split'))  394 us
    scatter-add x5, other arithmetic, assemble(): jax.ops.segment_sum(values, point_slots, num_segments=node_count + 1)  218 us
    gather x5, local copies, waits for them, and re-layouts, assemble(): return assembled[:, point_slots].reshape(fields.shape)  210 us
    ppermute x30, starting transfers between devices, from_behind(): return lax.ppermute(block, axis, route)  76.1 us
  transfers between devices with their start and end apart: 30, of which 0 were waited for; matrix products, arithmetic and copies ran while one was open for 3% of the time, Pallas kernels for 0%

commit v1 on v0

v1 whole, which is shorter than its diff:
```python
import functools

import jax
import jax.numpy as jnp
import ml_dtypes
import numpy as np
from jax import lax
from jax.experimental import pallas as pl
from jax.experimental.pallas import tpu as pltpu
from jax.sharding import PartitionSpec as P

ITERS = 4
HI = 48
LO = 128
ELEMS = 16
POINTS = 512
LISTS = 6
WIDE = ELEMS * POINTS
ENTRIES = 256
ROWS = 64
F32 = jnp.float32
BF16 = jnp.bfloat16
VMEM_LIMIT = 48 << 20


def element_tables():
    poly_order = 7
    node_count = poly_order + 1
    nodes = -np.cos(np.pi * np.arange(node_count) / poly_order)
    legendre = np.zeros((node_count, node_count))

    def fill():
        legendre[:, 0] = 1.0
        legendre[:, 1] = nodes
        for degree in range(2, node_count):
            legendre[:, degree] = (
                (2 * degree - 1) * nodes * legendre[:, degree - 1] - (degree - 1) * legendre[:, degree - 2]
            ) / degree

    for _ in range(60):
        fill()
        nodes = nodes - (nodes * legendre[:, poly_order] - legendre[:, poly_order - 1]) / (
            node_count * legendre[:, poly_order]
        )
    fill()
    top = legendre[:, poly_order]
    weights = 2.0 / (poly_order * node_count * top * top)
    deriv = np.zeros((node_count, node_count))
    for i in range(node_count):
        for j in range(node_count):
            if i != j:
                deriv[i, j] = top[i] / (top[j] * (nodes[i] - nodes[j]))
    deriv[0, 0] = -poly_order * node_count / 4.0
    deriv[poly_order, poly_order] = poly_order * node_count / 4.0
    mass = (weights[:, None, None] * weights[None, :, None] * weights[None, None, :]).reshape(-1)
    line = deriv.T @ (weights[:, None] * deriv)
    scaled = line / weights[None, :]
    eye = np.eye(node_count)
    first = np.kron(scaled, np.eye(64))
    second = np.kron(np.eye(4), np.kron(scaled, eye))
    third = np.kron(np.eye(4), np.kron(eye, scaled))
    diag = np.diag(scaled)
    ones = np.ones(node_count)
    diags = np.stack(
        [
            mass * np.kron(diag, np.kron(ones, ones)),
            mass * np.kron(ones, np.kron(diag, ones)),
            mass * np.kron(ones, np.kron(ones, diag)),
        ]
    )
    hats = np.stack([(1.0 - nodes) / 2.0, (1.0 + nodes) / 2.0])
    coarse = (
        hats[:, None, None, :, None, None]
        * hats[None, :, None, None, :, None]
        * hats[None, None, :, None, None, :]
    ).reshape(8, -1)
    return mass, first, np.concatenate([second, third], axis=1), diags, coarse


def halves(table):
    table = np.asarray(table, np.float32)
    upper = table.astype(ml_dtypes.bfloat16)
    lower = (table - upper.astype(np.float32)).astype(ml_dtypes.bfloat16)
    return upper, lower


def two_parts(value):
    upper = value.astype(BF16)
    return upper, (value - upper.astype(F32)).astype(BF16)


def row_mask(slots, height):
    high = lax.shift_right_logical(slots, 7)
    width = slots.shape[1]
    return jnp.broadcast_to(high, (height, width)) == lax.broadcasted_iota(jnp.int32, (height, width), 0)


def lane_hot(slots):
    low = lax.bitwise_and(slots, LO - 1)
    width = slots.shape[1]
    hot = jnp.broadcast_to(low, (LO, width)) == lax.broadcasted_iota(jnp.int32, (LO, width), 0)
    return jnp.where(hot, 1.0, 0.0).astype(BF16)


def spread(values, mask):
    parts = []
    for value in values:
        wide = jnp.where(mask, jnp.broadcast_to(value, mask.shape), 0.0)
        upper, lower = two_parts(wide)
        parts += [upper, lower]
    return jnp.concatenate(parts, axis=0)


def put(left, hot):
    return lax.dot_general(left, hot, (((1,), (1,)), ((), ())), preferred_element_type=F32)


def table_parts(table):
    upper, lower = two_parts(table)
    return jnp.concatenate([upper, lower], axis=1)


def take(parts, hot, mask):
    both = jnp.concatenate([hot, hot], axis=0)
    found = jnp.dot(parts, both, preferred_element_type=F32)
    return jnp.sum(jnp.where(mask, found, 0.0), axis=0, keepdims=True)


def fold(stacked, height):
    return stacked[:height] + stacked[height : 2 * height]


def total(value):
    return jnp.sum(jnp.sum(value, axis=1, keepdims=True), axis=0, keepdims=True)


def place(scalars):
    lane = lax.broadcasted_iota(jnp.int32, (1, LO), 1)
    row = jnp.zeros((1, LO), F32)
    for index, scalar in enumerate(scalars):
        row = jnp.where(lane == index, scalar, row)
    return row


def coarse_image(scaled, phi_ref, pick_ref, xcols, xhot):
    line = jnp.zeros((1, ENTRIES), F32)
    acc = jnp.zeros((ELEMS, ENTRIES), F32)
    for v in range(8):
        restricted = jnp.sum(scaled * phi_ref[v : v + 1, :], axis=1, keepdims=True)
        acc = acc + restricted * pick_ref[v]
    line = jnp.sum(acc, axis=0, keepdims=True)
    return fold(put(spread([line], row_mask(xcols, ROWS)), xhot), ROWS)


def coarse_correction(image, phi_ref, pick_ref, xcols, xhot):
    line = take(table_parts(image), xhot, row_mask(xcols, ROWS))
    result = jnp.zeros((ELEMS, POINTS), F32)
    for v in range(8):
        vertex = jnp.sum(pick_ref[v] * line, axis=1, keepdims=True)
        result = result + vertex * phi_ref[v : v + 1, :]
    return result


def write_payload(out_ref, image, scalars):
    row = place(scalars)
    for part in range(8):
        out_ref[part, 0:8, :] = image[8 * part : 8 * part + 8, :]
        out_ref[part, 8:9, :] = row


def setup_scatter(rhs_ref, slot_ref, list_ref, stretch_ref, helm_ref, mass_ref, diag_ref, hot_ref, sums_ref, *out_refs):
    diag = helm_ref[...] * mass_ref[...]
    for d in range(3):
        diag = diag + stretch_ref[:, d : d + 1] * diag_ref[d : d + 1, :]
    acc = jnp.zeros((6 * HI, LO), F32)
    for e in range(ELEMS):
        slots = slot_ref[e : e + 1, :]
        hot = lane_hot(slots)
        hot_ref[:, e * POINTS : (e + 1) * POINTS] = hot
        mask = row_mask(slots, HI)
        left = spread([jnp.ones((1, POINTS), F32), diag[e : e + 1, :], rhs_ref[e : e + 1, :]], mask)
        acc = acc + put(left, hot)
    tables = []
    for field in range(3):
        table = fold(acc[2 * HI * field : 2 * HI * (field + 1)], HI)
        sums_ref[field] = table
        tables.append(table_parts(table))
    for t in range(LISTS):
        slots = list_ref[t : t + 1, :]
        hot = lane_hot(slots)
        hot_ref[:, WIDE + t * LO : WIDE + (t + 1) * LO] = hot
        mask = row_mask(slots, HI)
        for field in range(3):
            out_refs[t][field : field + 1, :] = take(tables[field], hot, mask)


def incoming_table(list_ref, hot_ref, in_refs, field):
    acc = jnp.zeros((2 * HI, LO), F32)
    for t in range(LISTS):
        mask = row_mask(list_ref[t : t + 1, :], HI)
        left = spread([in_refs[t][field : field + 1, :]], mask)
        acc = acc + put(left, hot_ref[:, WIDE + t * LO : WIDE + (t + 1) * LO])
    return fold(acc, HI)


def setup_gather(
    slot_ref, list_ref, hot_ref, sums_ref, phi_ref, corner_ref, xvals_ref, xcols_ref, *refs
):
    in_refs = refs[:LISTS]
    minv_ref, dinv_ref, right_ref, pick_ref, xhot_ref, pay_ref = refs[LISTS:]
    tables = [
        table_parts(sums_ref[field] + incoming_table(list_ref, hot_ref, in_refs, field)) for field in range(3)
    ]
    for e in range(ELEMS):
        mask = row_mask(slot_ref[e : e + 1, :], HI)
        hot = hot_ref[:, e * POINTS : (e + 1) * POINTS]
        minv_ref[e : e + 1, :] = 1.0 / take(tables[0], hot, mask)
        dinv_ref[e : e + 1, :] = 1.0 / take(tables[1], hot, mask)
        right_ref[e : e + 1, :] = take(tables[2], hot, mask)
    xcols = xcols_ref[...]
    xhot_ref[...] = lane_hot(xcols)
    row_of = lax.bitwise_and(lax.broadcasted_iota(jnp.int32, (ELEMS, ENTRIES), 1), 15)
    for v in range(8):
        pick_ref[v] = jnp.where(corner_ref[:, v : v + 1] == row_of, xvals_ref[...], 0.0)
    scaled = right_ref[...] * minv_ref[...]
    image = coarse_image(scaled, phi_ref, pick_ref, xcols, xhot_ref[...])
    write_payload(pay_ref, image, [total(scaled * right_ref[...] * dinv_ref[...])])


def operator(u, stretch_ref, helm_ref, mass_ref, first_ref, second_ref):
    upper, lower = two_parts(u)

    def product(left_upper, left_lower, ref):
        rows = left_upper.shape[0]
        big = jnp.dot(
            jnp.concatenate([left_upper, left_lower], axis=0), ref[0], preferred_element_type=F32
        )
        return big[:rows] + big[rows:] + jnp.dot(left_upper, ref[1], preferred_element_type=F32)

    half = POINTS // 2
    along = product(upper, lower, first_ref)
    inside = product(
        jnp.concatenate([upper[:, :half], upper[:, half:]], axis=0),
        jnp.concatenate([lower[:, :half], lower[:, half:]], axis=0),
        second_ref,
    )
    second = jnp.concatenate([inside[:ELEMS, :half], inside[ELEMS:, :half]], axis=1)
    third = jnp.concatenate([inside[:ELEMS, half:], inside[ELEMS:, half:]], axis=1)
    result = stretch_ref[:, 0:1] * along + stretch_ref[:, 1:2] * second + stretch_ref[:, 2:3] * third
    return mass_ref[...] * (result + helm_ref[...] * u)


def apply_and_scatter(
    direction, slot_ref, list_ref, hot_ref, stretch_ref, helm_ref, mass_ref, first_ref, second_ref, field_ref, sums_ref, out_refs
):
    field_ref[...] = operator(direction, stretch_ref, helm_ref, mass_ref, first_ref, second_ref)
    acc = jnp.zeros((2 * HI, LO), F32)
    for e in range(ELEMS):
        mask = row_mask(slot_ref[e : e + 1, :], HI)
        left = spread([field_ref[e : e + 1, :]], mask)
        acc = acc + put(left, hot_ref[:, e * POINTS : (e + 1) * POINTS])
    table = fold(acc, HI)
    sums_ref[...] = table
    parts = table_parts(table)
    for t in range(LISTS):
        mask = row_mask(list_ref[t : t + 1, :], HI)
        out_refs[t][...] = take(parts, hot_ref[:, WIDE + t * LO : WIDE + (t + 1) * LO], mask)


def first_direction(
    slot_ref, list_ref, hot_ref, stretch_ref, helm_ref, mass_ref, first_ref, second_ref,
    phi_ref, pick_ref, xcols_ref, xhot_ref, dinv_ref, right_ref, pay_ref, *refs
):
    image_ref, state_ref, direction_ref, sums_ref = refs[:4]
    out_refs, field_ref = refs[4 : 4 + LISTS], refs[-1]
    for part in range(8):
        image_ref[8 * part : 8 * part + 8, :] = pay_ref[part, 0:8, :]
    image = image_ref[...]
    correction = coarse_correction(image, phi_ref, pick_ref, xcols_ref[...], xhot_ref[...])
    direction = right_ref[...] * dinv_ref[...] + correction
    direction_ref[...] = direction
    jacobi = pay_ref[0, 8:9, 0:1]
    state_ref[...] = place([jacobi, jacobi + total(image * image)])
    apply_and_scatter(
        direction, slot_ref, list_ref, hot_ref, stretch_ref, helm_ref, mass_ref, first_ref, second_ref, field_ref, sums_ref, out_refs
    )


def next_direction(
    slot_ref, list_ref, hot_ref, stretch_ref, helm_ref, mass_ref, first_ref, second_ref,
    phi_ref, pick_ref, xcols_ref, xhot_ref, dinv_ref, solution_ref, residual_ref, olddir_ref, force_ref,
    oldimage_ref, oldstate_ref, pay_ref, *refs
):
    newsol_ref, newres_ref, image_ref, state_ref, direction_ref, sums_ref = refs[:6]
    out_refs, field_ref = refs[6 : 6 + LISTS], refs[-1]
    jacobi = oldstate_ref[0:1, 0:1]
    rz_old = oldstate_ref[0:1, 1:2]
    alpha = rz_old / pay_ref[0, 8:9, 0:1]
    newsol_ref[...] = solution_ref[...] + alpha * olddir_ref[...]
    residual = residual_ref[...] - alpha * force_ref[...]
    newres_ref[...] = residual
    for part in range(8):
        rows = slice(8 * part, 8 * part + 8)
        image_ref[rows, :] = oldimage_ref[rows, :] - alpha * pay_ref[part, 0:8, :]
    image = image_ref[...]
    correction = coarse_correction(image, phi_ref, pick_ref, xcols_ref[...], xhot_ref[...])
    jacobi = jacobi - alpha * (2.0 * pay_ref[0, 8:9, 1:2] - alpha * pay_ref[0, 8:9, 2:3])
    rz_new = jacobi + total(image * image)
    direction = residual * dinv_ref[...] + correction + (rz_new / rz_old) * olddir_ref[...]
    direction_ref[...] = direction
    state_ref[...] = place([jacobi, rz_new])
    apply_and_scatter(
        direction, slot_ref, list_ref, hot_ref, stretch_ref, helm_ref, mass_ref, first_ref, second_ref, field_ref, sums_ref, out_refs
    )


def gather_image(slot_ref, list_ref, hot_ref, sums_ref, in_refs, force_ref):
    parts = table_parts(sums_ref[...] + incoming_table(list_ref, hot_ref, in_refs, 0))
    for e in range(ELEMS):
        mask = row_mask(slot_ref[e : e + 1, :], HI)
        force_ref[e : e + 1, :] = take(parts, hot_ref[:, e * POINTS : (e + 1) * POINTS], mask)


def assemble_reduce(
    slot_ref, list_ref, hot_ref, sums_ref, phi_ref, pick_ref, xcols_ref, xhot_ref, minv_ref, dinv_ref,
    residual_ref, direction_ref, *refs
):
    in_refs = refs[:LISTS]
    force_ref, pay_ref = refs[LISTS:]
    gather_image(slot_ref, list_ref, hot_ref, sums_ref, in_refs, force_ref)
    force = force_ref[...]
    scaled = force * minv_ref[...]
    smooth = scaled * dinv_ref[...]
    image = coarse_image(scaled, phi_ref, pick_ref, xcols_ref[...], xhot_ref[...])
    write_payload(
        pay_ref,
        image,
        [total(scaled * direction_ref[...]), total(smooth * residual_ref[...]), total(smooth * force)],
    )


def assemble_last(slot_ref, list_ref, hot_ref, sums_ref, minv_ref, direction_ref, *refs):
    in_refs = refs[:LISTS]
    force_ref, pay_ref = refs[LISTS:]
    gather_image(slot_ref, list_ref, hot_ref, sums_ref, in_refs, force_ref)
    pay_ref[...] = place([total(force_ref[...] * minv_ref[...] * direction_ref[...])])


def finish(solution_ref, residual_ref, direction_ref, force_ref, state_ref, pay_ref, newsol_ref, newres_ref):
    alpha = state_ref[0:1, 1:2] / jnp.sum(pay_ref[...], axis=0, keepdims=True)[:, 0:1]
    newsol_ref[...] = solution_ref[...] + alpha * direction_ref[...]
    newres_ref[...] = residual_ref[...] - alpha * force_ref[...]


def run(body, name, args, outs, scratch=()):
    return pl.pallas_call(
        body,
        name=name,
        out_shape=[jax.ShapeDtypeStruct(shape, dtype) for shape, dtype in outs],
        in_specs=[pl.BlockSpec(memory_space=pltpu.VMEM) for _ in args],
        out_specs=[pl.BlockSpec(memory_space=pltpu.VMEM) for _ in outs],
        scratch_shapes=list(scratch),
        compiler_params=pltpu.CompilerParams(vmem_limit_bytes=VMEM_LIMIT),
    )(*args)


def shift(block, axis, offset):
    size = lax.axis_size(axis)
    route = [(i, i + offset) for i in range(size) if 0 <= i + offset < size]
    return lax.ppermute(block, axis, route)


WAYS = (("split", -1), ("split", 1), ("curve", -2), ("curve", -1), ("curve", 1), ("curve", 2))


def exchange(outgoing):
    arrived = [None] * LISTS
    for t, (axis, offset) in enumerate(WAYS):
        back = WAYS.index((axis, -offset))
        arrived[back] = shift(outgoing[t], axis, offset)
    return arrived


def swap(block, axis):
    return lax.all_to_all(block, axis, 0, 0)


def reduce_all(payload):
    part = jnp.sum(swap(payload, "split"), axis=0)
    size = lax.axis_size("curve")
    part = jnp.sum(swap(jnp.broadcast_to(part[None], (size,) + part.shape), "curve"), axis=0)
    return swap(jnp.broadcast_to(part[None], payload.shape), "split")


def local(rhs_load, stretch, helm_shift, local_slot, share_curve, share_split, coarse_slot, x_vals, x_cols, x_count):
    mass, first, second, diags, coarse = element_tables()
    mass = jnp.asarray(mass.reshape(1, -1), F32)
    diags = jnp.asarray(diags, F32)
    phi = jnp.asarray(coarse, F32)
    first = jnp.asarray(np.stack(halves(first)))
    second = jnp.asarray(np.stack(halves(second)))
    stretch_t = stretch.T
    helm = helm_shift.reshape(-1, 1)
    corner = coarse_slot.T
    lists = jnp.concatenate([share_split.reshape(2, LO), share_curve.reshape(4, LO)], axis=0)
    factor = jnp.where(jnp.arange(x_vals.shape[0])[:, None] < x_count[None, :], x_vals, 0.0)
    xvals = factor.reshape(1, ENTRIES)
    xcols = x_cols.reshape(1, ENTRIES)
    field = ((ELEMS, POINTS), F32)
    table = ((HI, LO), F32)
    line = ((1, LO), F32)
    payload = ((8, 9, LO), F32)
    image_shape = ((ROWS, LO), F32)

    hot, sums3, *outgoing = run(
        setup_scatter,
        "setup_scatter",
        (rhs_load, local_slot, lists, stretch_t, helm, mass, diags),
        [((LO, WIDE + LISTS * LO), BF16), ((3, HI, LO), F32)] + [((3, LO), F32)] * LISTS,
    )
    arrived = exchange(outgoing)
    minv, dinv, right, pick, xhot, pay = run(
        setup_gather,
        "setup_gather",
        (local_slot, lists, hot, sums3, phi, corner, xvals, xcols, *arrived),
        [field, field, field, ((8, ELEMS, ENTRIES), F32), ((LO, ENTRIES), BF16), payload],
    )
    pay = reduce_all(pay)
    shape = (local_slot, lists, hot)
    elements = (stretch_t, helm, mass, first, second)
    grid = (phi, pick, xcols, xhot)
    scratch = [pltpu.VMEM((ELEMS, POINTS), F32)]
    solution = jnp.zeros_like(rhs_load)
    residual = right
    image, state, direction, sums, *outgoing = run(
        first_direction,
        "first_direction",
        (*shape, *elements, *grid, dinv, right, pay),
        [image_shape, line, field, table] + [line] * LISTS,
        scratch,
    )
    for iteration in range(ITERS):
        arrived = exchange(outgoing)
        if iteration < ITERS - 1:
            force, pay = run(
                assemble_reduce,
                "assemble_reduce",
                (*shape, sums, *grid, minv, dinv, residual, direction, *arrived),
                [field, payload],
            )
            pay = reduce_all(pay)
            solution, residual, image, state, direction, sums, *outgoing = run(
                next_direction,
                "next_direction",
                (*shape, *elements, *grid, dinv, solution, residual, direction, force, image, state, pay),
                [field, field, image_shape, line, field, table] + [line] * LISTS,
                scratch,
            )
        else:
            force, pay = run(
                assemble_last,
                "assemble_last",
                (*shape, sums, minv, direction, *arrived),
                [field, line],
            )
            devices = lax.axis_size("curve") * lax.axis_size("split")
            pay = lax.all_to_all(jnp.broadcast_to(pay[None], (devices, 1, LO)), ("curve", "split"), 0, 0)
            solution, residual = run(
                finish,
                "finish",
                (solution, residual, direction, force, state, pay.reshape(devices, LO)),
                [field, field],
            )
    return solution, residual


def solution(mesh):
    in_specs = (
        P(("curve", "split"), None),
        P(None, ("curve", "split")),
        P(("curve", "split")),
        P(("curve", "split"), None),
        P("curve", "split", None, None),
        P("curve", "split", None, None),
        P(None, ("curve", "split")),
        P(None, ("curve", "split")),
        P(None, ("curve", "split")),
        P(("curve", "split")),
    )
    out_specs = (P(("curve", "split"), None), P(("curve", "split"), None))
    return jax.shard_map(local, mesh=mesh, in_specs=in_specs, out_specs=out_specs, check_vma=False)
```

time: 1760 us -> 443 us (0.25)
  blocking collectives: 1080 us -> 250 us
  other arithmetic: 286 us -> 14 us
  local copies, waits for them, and re-layouts: 279 us -> 64.8 us
  Pallas kernels: 0 us -> 20.3 us
    psum x11 -> x0, blocking collectives: 1080 us -> none  [the longest x7 689 us: global_dot(): lax.psum(jnp.sum(left_field * right_field / multiplicity), ('curve', 'spl...]
    scatter-add x43 -> x0, other arithmetic: 281 us -> none  [the longest x5 218 us: assemble(): jax.ops.segment_sum(values, point_slots, num_segments=node_count + 1)]
    gather x51 -> x0, local copies, waits for them, and re-layouts: 259 us -> none  [the longest x5 210 us: assemble(): return assembled[:, point_slots].reshape(fields.shape)]
    all_to_all x0 -> x13, blocking collectives: none -> 250 us  [the longest x12 216 us: swap(): return lax.all_to_all(block, axis, 0, 0)]
    unnamed x76 -> x204, local copies, waits for them, and re-layouts: 5.11 us -> 56.1 us
    pallas_call x0 -> x11, Pallas kernels: none -> 20.3 us  [run(): pl.pallas_call(body, name=name, out_shape=[jax.ShapeDtypeStruct(shape, dt...]
  transfers between devices with their start and end apart: 30 -> 30, of which waited for: 0 -> 8; matrix products, arithmetic and copies ran while one was open for 3% -> 1% of each run, Pallas kernels for 0% -> 0%
where the time goes in v1:
time: 443 us; the launch traced here: 438 us
  blocking collectives  250 us (56%)
  starting transfers between devices  75.8 us (17%)
  local copies, waits for them, and re-layouts  64.8 us (15%)
  Pallas kernels  20.3 us (5%)
  other arithmetic  14 us (3%)
  waiting for transfers between devices  11.9 us (3%)
    all_to_all x12, blocking collectives, swap(): return lax.all_to_all(block, axis, 0, 0)  216 us
    ppermute x30, starting transfers between devices, shift(): return lax.ppermute(block, axis, route)  75.8 us
    unnamed x204, local copies, waits for them, and re-layouts  56.1 us
    all_to_all x1, blocking collectives, local(): lax.all_to_all(jnp.broadcast_to(pay[None], (devices, 1, LO)), ('curve', '...  33.6 us
    pallas_call x11, Pallas kernels, run(): pl.pallas_call(body, name=name, out_shape=[jax.ShapeDtypeStruct(shape, dt...  20.3 us
    ppermute x30, waiting for transfers between devices, shift(): return lax.ppermute(block, axis, route)  11.9 us
  transfers between devices with their start and end apart: 30, of which 8 were waited for; matrix products, arithmetic and copies ran while one was open for 1% of the time, Pallas kernels for 0%

profile of v1, /device:TPU:1, one launch (start us, length us, event | category | flops | bytes accessed | tf_op | source)
XLA Modules:
  0.0 438.0 jit_solution(14207362728967392795)
XLA Ops:
  5.7 2.4 setup_scatter.1
  8.8 4.0 collective-permute-start
  14.1 3.1 collective-permute-start.2
  17.3 4.2 collective-permute-start.3
  40.9 3.1 setup_gather.1
  45.9 16.2 %all_to_all.65 = f32[8,9,128]{2,1,0:T(8,128)} all-to-all(f32[8,9,128]{2,1,0:T(8,128)S(1)} %get-tuple-element.81), channel_id=1, replica_groups=mesh['curve'=64,'split'=8] {'split'}, dimensions={0} | all-to-all | bytes 73728 | tf_op jit(solution)/shard_map/all_to_all | solution.py:385
  64.3 35.9 %all_to_all.66 = f32[64,9,128]{2,1,0:T(8,128)} all-to-all(f32[64,9,128]{2,1,0:T(8,128)S(1)} %broadcast_in_dim.28), channel_id=1, replica_groups=mesh['curve'=64,'split'=8] {'curve'}, dimensions={0} | all-to-all | bytes 589824 | tf_op jit(solution)/shard_map/all_to_all | solution.py:385
  102.6 9.5 %all_to_all.67.pay_ref = f32[8,9,128]{2,1,0:T(8,128)S(1)} all-to-all(f32[8,9,128]{2,1,0:T(8,128)S(1)} %broadcast_in_dim.29), channel_id=1, replica_groups=mesh['curve'=64,'split'=8] {'split'}, dimensions={0} | all-to-all | bytes 73728 | tf_op jit(solution)/shard_map/all_to_all | solution.py:385
  120.2 2.3 collective-permute-start.6
  123.8 3.0 collective-permute-start.8
  126.8 5.2 %collective-permute-start.9 = (f32[1,128]{1,0:T(1,128)S(1)}, f32[1,128]{1,0:T(1,128)S(1)}, u32[]{:S(2)}, u32[]{:S(2)}) collective-permute-start(f32[1,128]{1,0:T(1,128)S(1)} %get-tuple-element.88), channel_id=1, source_target_pairs={{0,8},{8,16},{16,24},{24,32},{32,40},{40,48},{48,56},{56,64},{64,7... | collective-permute-start | bytes 1544 | tf_op jit(solution)/shard_map/ppermute | solution.py:370
  140.4 11.9 %all_to_all.68 = f32[8,9,128]{2,1,0:T(8,128)} all-to-all(f32[8,9,128]{2,1,0:T(8,128)S(1)} %get-tuple-element.94), channel_id=1, replica_groups=mesh['curve'=64,'split'=8] {'split'}, dimensions={0} | all-to-all | bytes 73728 | tf_op jit(solution)/shard_map/all_to_all | solution.py:385
  154.4 30.0 %all_to_all.69 = f32[64,9,128]{2,1,0:T(8,128)} all-to-all(f32[64,9,128]{2,1,0:T(8,128)S(1)} %broadcast_in_dim.30), channel_id=1, replica_groups=mesh['curve'=64,'split'=8] {'curve'}, dimensions={0} | all-to-all | bytes 589824 | tf_op jit(solution)/shard_map/all_to_all | solution.py:385
  186.8 9.6 %all_to_all.70.pay_ref = f32[8,9,128]{2,1,0:T(8,128)S(1)} all-to-all(f32[8,9,128]{2,1,0:T(8,128)S(1)} %broadcast_in_dim.31), channel_id=1, replica_groups=mesh['curve'=64,'split'=8] {'split'}, dimensions={0} | all-to-all | bytes 73728 | tf_op jit(solution)/shard_map/all_to_all | solution.py:385
  205.5 2.1 next_direction.3
  207.7 2.3 collective-permute-start.12
  211.3 3.0 collective-permute-start.14
  214.3 5.2 %collective-permute-start.15 = (f32[1,128]{1,0:T(1,128)S(1)}, f32[1,128]{1,0:T(1,128)S(1)}, u32[]{:S(2)}, u32[]{:S(2)}) collective-permute-start(f32[1,128]{1,0:T(1,128)S(1)} %get-tuple-element.102), channel_id=1, source_target_pairs={{0,8},{8,16},{16,24},{24,32},{32,40},{40,48},{48,56},{56,64},{64,7... | collective-permute-start | bytes 1544 | tf_op jit(solution)/shard_map/ppermute | solution.py:370
  227.8 11.9 %all_to_all.71 = f32[8,9,128]{2,1,0:T(8,128)} all-to-all(f32[8,9,128]{2,1,0:T(8,128)S(1)} %get-tuple-element.108), channel_id=1, replica_groups=mesh['curve'=64,'split'=8] {'split'}, dimensions={0} | all-to-all | bytes 73728 | tf_op jit(solution)/shard_map/all_to_all | solution.py:385
  241.9 30.0 %all_to_all.72 = f32[64,9,128]{2,1,0:T(8,128)} all-to-all(f32[64,9,128]{2,1,0:T(8,128)S(1)} %broadcast_in_dim.32), channel_id=1, replica_groups=mesh['curve'=64,'split'=8] {'curve'}, dimensions={0} | all-to-all | bytes 589824 | tf_op jit(solution)/shard_map/all_to_all | solution.py:385
  274.3 9.6 %all_to_all.73.pay_ref = f32[8,9,128]{2,1,0:T(8,128)S(1)} all-to-all(f32[8,9,128]{2,1,0:T(8,128)S(1)} %broadcast_in_dim.33), channel_id=1, replica_groups=mesh['curve'=64,'split'=8] {'split'}, dimensions={0} | all-to-all | bytes 73728 | tf_op jit(solution)/shard_map/all_to_all | solution.py:385
  293.8 2.1 next_direction.4
  296.0 2.3 collective-permute-start.18
  299.5 3.0 collective-permute-start.20
  302.6 5.2 %collective-permute-start.21 = (f32[1,128]{1,0:T(1,128)S(1)}, f32[1,128]{1,0:T(1,128)S(1)}, u32[]{:S(2)}, u32[]{:S(2)}) collective-permute-start(f32[1,128]{1,0:T(1,128)S(1)} %get-tuple-element.116), channel_id=1, source_target_pairs={{0,8},{8,16},{16,24},{24,32},{32,40},{40,48},{48,56},{56,64},{64,7... | collective-permute-start | bytes 1544 | tf_op jit(solution)/shard_map/ppermute | solution.py:370
  316.1 11.9 %all_to_all.74 = f32[8,9,128]{2,1,0:T(8,128)} all-to-all(f32[8,9,128]{2,1,0:T(8,128)S(1)} %get-tuple-element.122), channel_id=1, replica_groups=mesh['curve'=64,'split'=8] {'split'}, dimensions={0} | all-to-all | bytes 73728 | tf_op jit(solution)/shard_map/all_to_all | solution.py:385
  330.1 30.0 %all_to_all.75 = f32[64,9,128]{2,1,0:T(8,128)} all-to-all(f32[64,9,128]{2,1,0:T(8,128)S(1)} %broadcast_in_dim.34), channel_id=1, replica_groups=mesh['curve'=64,'split'=8] {'curve'}, dimensions={0} | all-to-all | bytes 589824 | tf_op jit(solution)/shard_map/all_to_all | solution.py:385
  362.6 9.6 %all_to_all.76.pay_ref = f32[8,9,128]{2,1,0:T(8,128)S(1)} all-to-all(f32[8,9,128]{2,1,0:T(8,128)S(1)} %broadcast_in_dim.35), channel_id=1, replica_groups=mesh['curve'=64,'split'=8] {'split'}, dimensions={0} | all-to-all | bytes 73728 | tf_op jit(solution)/shard_map/all_to_all | solution.py:385
  384.1 2.3 collective-permute-start.24
  387.7 3.0 collective-permute-start.26
  390.7 5.2 %collective-permute-start.27 = (f32[1,128]{1,0:T(1,128)S(1)}, f32[1,128]{1,0:T(1,128)S(1)}, u32[]{:S(2)}, u32[]{:S(2)}) collective-permute-start(f32[1,128]{1,0:T(1,128)S(1)} %get-tuple-element.130), channel_id=1, source_target_pairs={{0,8},{8,16},{16,24},{24,32},{32,40},{40,48},{48,56},{56,64},{64,7... | collective-permute-start | bytes 1544 | tf_op jit(solution)/shard_map/ppermute | solution.py:370
  403.6 33.6 %all_to_all.77 = f32[512,1,128]{2,1,0:T(1,128)S(1)} all-to-all(f32[512,1,128]{2,1,0:T(1,128)S(1)} %broadcast_in_dim.37), channel_id=1, replica_groups=mesh['curve'=64,'split'=8] {'curve','split'}, dimensions={0} | all-to-all | bytes 524288 | tf_op jit(solution)/shard_map/all_to_all | solution.py:467
  (279 shorter events, 123.8 us)
Async XLA Ops:
  8.8 14.6 %collective-permute-start = (f32[3,128]{1,0:T(4,128)S(1)}, f32[3,128]{1,0:T(4,128)S(1)}, u32[]{:S(2)}, u32[]{:S(2)}) collective-permute-start(f32[3,128]{1,0:T(4,128)S(1)} %get-tuple-element.71), channel_id=1, source_target_pairs={{0,1},{1,2},{2,3},{3,4},{4,5},{5,6},{6,7},{8,9},{9,10},{10,11},{11... | collective-permute-start | bytes 4616 | tf_op jit(solution)/shard_map/ppermute | solution.py:370
  12.8 16.6 %collective-permute-start.1 = (f32[3,128]{1,0:T(4,128)S(1)}, f32[3,128]{1,0:T(4,128)S(1)}, u32[]{:S(2)}, u32[]{:S(2)}) collective-permute-start(f32[3,128]{1,0:T(4,128)S(1)} %get-tuple-element.72), channel_id=1, source_target_pairs={{1,0},{2,1},{3,2},{4,3},{5,4},{6,5},{7,6},{9,8},{10,9},{11,10},{12... | collective-permute-start | bytes 4616 | tf_op jit(solution)/shard_map/ppermute | solution.py:370
  14.1 15.3 %collective-permute-start.2 = (f32[3,128]{1,0:T(4,128)S(1)}, f32[3,128]{1,0:T(4,128)S(1)}, u32[]{:S(2)}, u32[]{:S(2)}) collective-permute-start(f32[3,128]{1,0:T(4,128)S(1)} %get-tuple-element.73), channel_id=1, source_target_pairs={{0,16},{8,24},{16,32},{24,40},{32,48},{40,56},{48,64},{56,72},{64,... | collective-permute-start | bytes 4616 | tf_op jit(solution)/shard_map/ppermute | solution.py:370
  17.3 12.8 %collective-permute-start.3 = (f32[3,128]{1,0:T(4,128)S(1)}, f32[3,128]{1,0:T(4,128)S(1)}, u32[]{:S(2)}, u32[]{:S(2)}) collective-permute-start(f32[3,128]{1,0:T(4,128)S(1)} %get-tuple-element.74), channel_id=1, source_target_pairs={{0,8},{8,16},{16,24},{24,32},{32,40},{40,48},{48,56},{56,64},{64,7... | collective-permute-start | bytes 4616 | tf_op jit(solution)/shard_map/ppermute | solution.py:370
  21.5 9.1 %collective-permute-start.4 = (f32[3,128]{1,0:T(4,128)S(1)}, f32[3,128]{1,0:T(4,128)S(1)}, u32[]{:S(2)}, u32[]{:S(2)}) collective-permute-start(f32[3,128]{1,0:T(4,128)S(1)} %get-tuple-element.75), channel_id=1, source_target_pairs={{8,0},{16,8},{24,16},{32,24},{40,32},{48,40},{56,48},{64,56},{72,6... | collective-permute-start | bytes 4616 | tf_op jit(solution)/shard_map/ppermute | solution.py:370
  24.0 7.2 %collective-permute-start.5 = (f32[3,128]{1,0:T(4,128)S(1)}, f32[3,128]{1,0:T(4,128)S(1)}, u32[]{:S(2)}, u32[]{:S(2)}) collective-permute-start(f32[3,128]{1,0:T(4,128)S(1)} %get-tuple-element.76), channel_id=1, source_target_pairs={{16,0},{24,8},{32,16},{40,24},{48,32},{56,40},{64,48},{72,56},{80,... | collective-permute-start | bytes 4616 | tf_op jit(solution)/shard_map/ppermute | solution.py:370
  40.9 71.2 %copy-start.7 = (s32[16,512]{1,0:T(8,128)S(1)}, s32[16,512]{1,0:T(8,128)}, u32[]{:S(2)}) copy-start(s32[16,512]{1,0:T(8,128)} %slot_ref.19) | copy-start | bytes 98308
  40.9 71.2 %copy-start.16 = (f32[8,512]{1,0:T(8,128)S(1)}, f32[8,512]{1,0:T(8,128)}, u32[]{:S(2)}) copy-start(f32[8,512]{1,0:T(8,128)} %constant.15.clone.phi_ref) | copy-start | bytes 49156
  120.2 13.7 %collective-permute-start.6 = (f32[1,128]{1,0:T(1,128)S(1)}, f32[1,128]{1,0:T(1,128)S(1)}, u32[]{:S(2)}, u32[]{:S(2)}) collective-permute-start(f32[1,128]{1,0:T(1,128)S(1)} %get-tuple-element.85), channel_id=1, source_target_pairs={{0,1},{1,2},{2,3},{3,4},{4,5},{5,6},{6,7},{8,9},{9,10},{10,11},{11... | collective-permute-start | bytes 1544 | tf_op jit(solution)/shard_map/ppermute | solution.py:370
  122.5 12.7 %collective-permute-start.7 = (f32[1,128]{1,0:T(1,128)S(1)}, f32[1,128]{1,0:T(1,128)S(1)}, u32[]{:S(2)}, u32[]{:S(2)}) collective-permute-start(f32[1,128]{1,0:T(1,128)S(1)} %get-tuple-element.86), channel_id=1, source_target_pairs={{1,0},{2,1},{3,2},{4,3},{5,4},{6,5},{7,6},{9,8},{10,9},{11,10},{12... | collective-permute-start | bytes 1544 | tf_op jit(solution)/shard_map/ppermute | solution.py:370
  123.8 11.5 %collective-permute-start.8 = (f32[1,128]{1,0:T(1,128)S(1)}, f32[1,128]{1,0:T(1,128)S(1)}, u32[]{:S(2)}, u32[]{:S(2)}) collective-permute-start(f32[1,128]{1,0:T(1,128)S(1)} %get-tuple-element.87), channel_id=1, source_target_pairs={{0,16},{8,24},{16,32},{24,40},{32,48},{40,56},{48,64},{56,72},{64,... | collective-permute-start | bytes 1544 | tf_op jit(solution)/shard_map/ppermute | solution.py:370
  126.8 8.5 %collective-permute-start.9 = (f32[1,128]{1,0:T(1,128)S(1)}, f32[1,128]{1,0:T(1,128)S(1)}, u32[]{:S(2)}, u32[]{:S(2)}) collective-permute-start(f32[1,128]{1,0:T(1,128)S(1)} %get-tuple-element.88), channel_id=1, source_target_pairs={{0,8},{8,16},{16,24},{24,32},{32,40},{40,48},{48,56},{56,64},{64,7... | collective-permute-start | bytes 1544 | tf_op jit(solution)/shard_map/ppermute | solution.py:370
  132.0 4.9 %collective-permute-start.10 = (f32[1,128]{1,0:T(1,128)S(1)}, f32[1,128]{1,0:T(1,128)S(1)}, u32[]{:S(2)}, u32[]{:S(2)}) collective-permute-start(f32[1,128]{1,0:T(1,128)S(1)} %get-tuple-element.89), channel_id=1, source_target_pairs={{8,0},{16,8},{24,16},{32,24},{40,32},{48,40},{56,48},{64,56},{72,6... | collective-permute-start | bytes 1544 | tf_op jit(solution)/shard_map/ppermute | solution.py:370
  134.0 4.3 collective-permute-start.11
  207.7 13.7 %collective-permute-start.12 = (f32[1,128]{1,0:T(1,128)S(1)}, f32[1,128]{1,0:T(1,128)S(1)}, u32[]{:S(2)}, u32[]{:S(2)}) collective-permute-start(f32[1,128]{1,0:T(1,128)S(1)} %get-tuple-element.99), channel_id=1, source_target_pairs={{0,1},{1,2},{2,3},{3,4},{4,5},{5,6},{6,7},{8,9},{9,10},{10,11},{11... | collective-permute-start | bytes 1544 | tf_op jit(solution)/shard_map/ppermute | solution.py:370
  210.0 12.8 %collective-permute-start.13 = (f32[1,128]{1,0:T(1,128)S(1)}, f32[1,128]{1,0:T(1,128)S(1)}, u32[]{:S(2)}, u32[]{:S(2)}) collective-permute-start(f32[1,128]{1,0:T(1,128)S(1)} %get-tuple-element.100), channel_id=1, source_target_pairs={{1,0},{2,1},{3,2},{4,3},{5,4},{6,5},{7,6},{9,8},{10,9},{11,10},{12... | collective-permute-start | bytes 1544 | tf_op jit(solution)/shard_map/ppermute | solution.py:370
  211.3 11.5 %collective-permute-start.14 = (f32[1,128]{1,0:T(1,128)S(1)}, f32[1,128]{1,0:T(1,128)S(1)}, u32[]{:S(2)}, u32[]{:S(2)}) collective-permute-start(f32[1,128]{1,0:T(1,128)S(1)} %get-tuple-element.101), channel_id=1, source_target_pairs={{0,16},{8,24},{16,32},{24,40},{32,48},{40,56},{48,64},{56,72},{64,... | collective-permute-start | bytes 1544 | tf_op jit(solution)/shard_map/ppermute | solution.py:370
  214.3 8.5 %collective-permute-start.15 = (f32[1,128]{1,0:T(1,128)S(1)}, f32[1,128]{1,0:T(1,128)S(1)}, u32[]{:S(2)}, u32[]{:S(2)}) collective-permute-start(f32[1,128]{1,0:T(1,128)S(1)} %get-tuple-element.102), channel_id=1, source_target_pairs={{0,8},{8,16},{16,24},{24,32},{32,40},{40,48},{48,56},{56,64},{64,7... | collective-permute-start | bytes 1544 | tf_op jit(solution)/shard_map/ppermute | solution.py:370
  219.5 4.9 %collective-permute-start.16 = (f32[1,128]{1,0:T(1,128)S(1)}, f32[1,128]{1,0:T(1,128)S(1)}, u32[]{:S(2)}, u32[]{:S(2)}) collective-permute-start(f32[1,128]{1,0:T(1,128)S(1)} %get-tuple-element.103), channel_id=1, source_target_pairs={{8,0},{16,8},{24,16},{32,24},{40,32},{48,40},{56,48},{64,56},{72,6... | collective-permute-start | bytes 1544 | tf_op jit(solution)/shard_map/ppermute | solution.py:370
  221.4 4.3 collective-permute-start.17
  296.0 13.7 %collective-permute-start.18 = (f32[1,128]{1,0:T(1,128)S(1)}, f32[1,128]{1,0:T(1,128)S(1)}, u32[]{:S(2)}, u32[]{:S(2)}) collective-permute-start(f32[1,128]{1,0:T(1,128)S(1)} %get-tuple-element.113), channel_id=1, source_target_pairs={{0,1},{1,2},{2,3},{3,4},{4,5},{5,6},{6,7},{8,9},{9,10},{10,11},{11... | collective-permute-start | bytes 1544 | tf_op jit(solution)/shard_map/ppermute | solution.py:370
  298.2 12.7 %collective-permute-start.19 = (f32[1,128]{1,0:T(1,128)S(1)}, f32[1,128]{1,0:T(1,128)S(1)}, u32[]{:S(2)}, u32[]{:S(2)}) collective-permute-start(f32[1,128]{1,0:T(1,128)S(1)} %get-tuple-element.114), channel_id=1, source_target_pairs={{1,0},{2,1},{3,2},{4,3},{5,4},{6,5},{7,6},{9,8},{10,9},{11,10},{12... | collective-permute-start | bytes 1544 | tf_op jit(solution)/shard_map/ppermute | solution.py:370
  299.5 11.5 %collective-permute-start.20 = (f32[1,128]{1,0:T(1,128)S(1)}, f32[1,128]{1,0:T(1,128)S(1)}, u32[]{:S(2)}, u32[]{:S(2)}) collective-permute-start(f32[1,128]{1,0:T(1,128)S(1)} %get-tuple-element.115), channel_id=1, source_target_pairs={{0,16},{8,24},{16,32},{24,40},{32,48},{40,56},{48,64},{56,72},{64,... | collective-permute-start | bytes 1544 | tf_op jit(solution)/shard_map/ppermute | solution.py:370
  302.6 8.5 %collective-permute-start.21 = (f32[1,128]{1,0:T(1,128)S(1)}, f32[1,128]{1,0:T(1,128)S(1)}, u32[]{:S(2)}, u32[]{:S(2)}) collective-permute-start(f32[1,128]{1,0:T(1,128)S(1)} %get-tuple-element.116), channel_id=1, source_target_pairs={{0,8},{8,16},{16,24},{24,32},{32,40},{40,48},{48,56},{56,64},{64,7... | collective-permute-start | bytes 1544 | tf_op jit(solution)/shard_map/ppermute | solution.py:370
  307.7 4.9 %collective-permute-start.22 = (f32[1,128]{1,0:T(1,128)S(1)}, f32[1,128]{1,0:T(1,128)S(1)}, u32[]{:S(2)}, u32[]{:S(2)}) collective-permute-start(f32[1,128]{1,0:T(1,128)S(1)} %get-tuple-element.117), channel_id=1, source_target_pairs={{8,0},{16,8},{24,16},{32,24},{40,32},{48,40},{56,48},{64,56},{72,6... | collective-permute-start | bytes 1544 | tf_op jit(solution)/shard_map/ppermute | solution.py:370
  309.7 4.3 collective-permute-start.23
  384.1 13.7 %collective-permute-start.24 = (f32[1,128]{1,0:T(1,128)S(1)}, f32[1,128]{1,0:T(1,128)S(1)}, u32[]{:S(2)}, u32[]{:S(2)}) collective-permute-start(f32[1,128]{1,0:T(1,128)S(1)} %get-tuple-element.127), channel_id=1, source_target_pairs={{0,1},{1,2},{2,3},{3,4},{4,5},{5,6},{6,7},{8,9},{9,10},{10,11},{11... | collective-permute-start | bytes 1544 | tf_op jit(solution)/shard_map/ppermute | solution.py:370
  386.4 12.7 %collective-permute-start.25 = (f32[1,128]{1,0:T(1,128)S(1)}, f32[1,128]{1,0:T(1,128)S(1)}, u32[]{:S(2)}, u32[]{:S(2)}) collective-permute-start(f32[1,128]{1,0:T(1,128)S(1)} %get-tuple-element.128), channel_id=1, source_target_pairs={{1,0},{2,1},{3,2},{4,3},{5,4},{6,5},{7,6},{9,8},{10,9},{11,10},{12... | collective-permute-start | bytes 1544 | tf_op jit(solution)/shard_map/ppermute | solution.py:370
  387.7 11.5 %collective-permute-start.26 = (f32[1,128]{1,0:T(1,128)S(1)}, f32[1,128]{1,0:T(1,128)S(1)}, u32[]{:S(2)}, u32[]{:S(2)}) collective-permute-start(f32[1,128]{1,0:T(1,128)S(1)} %get-tuple-element.129), channel_id=1, source_target_pairs={{0,16},{8,24},{16,32},{24,40},{32,48},{40,56},{48,64},{56,72},{64,... | collective-permute-start | bytes 1544 | tf_op jit(solution)/shard_map/ppermute | solution.py:370
  390.7 8.5 %collective-permute-start.27 = (f32[1,128]{1,0:T(1,128)S(1)}, f32[1,128]{1,0:T(1,128)S(1)}, u32[]{:S(2)}, u32[]{:S(2)}) collective-permute-start(f32[1,128]{1,0:T(1,128)S(1)} %get-tuple-element.130), channel_id=1, source_target_pairs={{0,8},{8,16},{16,24},{24,32},{32,40},{40,48},{48,56},{56,64},{64,7... | collective-permute-start | bytes 1544 | tf_op jit(solution)/shard_map/ppermute | solution.py:370
  395.9 4.9 %collective-permute-start.28 = (f32[1,128]{1,0:T(1,128)S(1)}, f32[1,128]{1,0:T(1,128)S(1)}, u32[]{:S(2)}, u32[]{:S(2)}) collective-permute-start(f32[1,128]{1,0:T(1,128)S(1)} %get-tuple-element.131), channel_id=1, source_target_pairs={{8,0},{16,8},{24,16},{32,24},{40,32},{48,40},{56,48},{64,56},{72,6... | collective-permute-start | bytes 1544 | tf_op jit(solution)/shard_map/ppermute | solution.py:370
  397.8 4.3 collective-permute-start.29
  (99 other events, 683.3 us)

commit v2 on v1

v2 whole, which is shorter than its diff:
```python
import functools

import jax
import jax.numpy as jnp
import ml_dtypes
import numpy as np
from jax import lax
from jax.experimental import pallas as pl
from jax.experimental.pallas import tpu as pltpu
from jax.sharding import PartitionSpec as P

ITERS = 4
HI = 48
LO = 128
ELEMS = 16
POINTS = 512
LISTS = 6
WIDE = ELEMS * POINTS
ENTRIES = 256
ROWS = 64
CHUNK = 1024
F32 = jnp.float32
BF16 = jnp.bfloat16
VMEM_LIMIT = 16 << 20


def element_tables():
    poly_order = 7
    node_count = poly_order + 1
    nodes = -np.cos(np.pi * np.arange(node_count) / poly_order)
    legendre = np.zeros((node_count, node_count))

    def fill():
        legendre[:, 0] = 1.0
        legendre[:, 1] = nodes
        for degree in range(2, node_count):
            legendre[:, degree] = (
                (2 * degree - 1) * nodes * legendre[:, degree - 1] - (degree - 1) * legendre[:, degree - 2]
            ) / degree

    for _ in range(60):
        fill()
        nodes = nodes - (nodes * legendre[:, poly_order] - legendre[:, poly_order - 1]) / (
            node_count * legendre[:, poly_order]
        )
    fill()
    top = legendre[:, poly_order]
    weights = 2.0 / (poly_order * node_count * top * top)
    deriv = np.zeros((node_count, node_count))
    for i in range(node_count):
        for j in range(node_count):
            if i != j:
                deriv[i, j] = top[i] / (top[j] * (nodes[i] - nodes[j]))
    deriv[0, 0] = -poly_order * node_count / 4.0
    deriv[poly_order, poly_order] = poly_order * node_count / 4.0
    mass = (weights[:, None, None] * weights[None, :, None] * weights[None, None, :]).reshape(-1)
    line = deriv.T @ (weights[:, None] * deriv)
    scaled = line / weights[None, :]
    eye = np.eye(node_count)
    first = np.kron(scaled, np.eye(64))
    second = np.kron(np.eye(4), np.kron(scaled, eye))
    third = np.kron(np.eye(4), np.kron(eye, scaled))
    diag = np.diag(scaled)
    ones = np.ones(node_count)
    diags = np.stack(
        [
            mass * np.kron(diag, np.kron(ones, ones)),
            mass * np.kron(ones, np.kron(diag, ones)),
            mass * np.kron(ones, np.kron(ones, diag)),
        ]
    )
    hats = np.stack([(1.0 - nodes) / 2.0, (1.0 + nodes) / 2.0])
    coarse = (
        hats[:, None, None, :, None, None]
        * hats[None, :, None, None, :, None]
        * hats[None, None, :, None, None, :]
    ).reshape(8, -1)
    return mass, first, np.concatenate([second, third], axis=1), diags, coarse


def table_pieces(table):
    rest = np.asarray(table, np.float32)
    pieces = []
    for _ in range(3):
        piece = rest.astype(ml_dtypes.bfloat16)
        pieces.append(piece)
        rest = rest - piece.astype(np.float32)
    return np.stack(pieces)


def pieces(value):
    upper = value.astype(BF16)
    rest = value - upper.astype(F32)
    middle = rest.astype(BF16)
    return [upper, middle, (rest - middle.astype(F32)).astype(BF16)]


def row_mask(slots, height):
    high = lax.shift_right_logical(slots, 7)
    width = slots.shape[1]
    return jnp.broadcast_to(high, (height, width)) == lax.broadcasted_iota(jnp.int32, (height, width), 0)


def lane_hot(slots):
    low = lax.bitwise_and(slots, LO - 1)
    width = slots.shape[1]
    hot = jnp.broadcast_to(low, (LO, width)) == lax.broadcasted_iota(jnp.int32, (LO, width), 0)
    return jnp.where(hot, 1.0, 0.0).astype(BF16)


def spread(values, mask):
    wide = [jnp.where(mask, jnp.broadcast_to(value, mask.shape), 0.0) for value in values]
    return jnp.concatenate([piece for value in wide for piece in pieces(value)], axis=0)


def put(left, hot):
    return lax.dot_general(left, hot, (((1,), (1,)), ((), ())), preferred_element_type=F32)


def table_parts(table):
    return jnp.concatenate(pieces(table), axis=1)


def take(parts, hot, mask):
    found = jnp.dot(parts, jnp.concatenate([hot] * 3, axis=0), preferred_element_type=F32)
    return jnp.sum(jnp.where(mask, found, 0.0), axis=0, keepdims=True)


def fold(stacked, height):
    return stacked[:height] + stacked[height : 2 * height] + stacked[2 * height : 3 * height]


def total(value):
    return jnp.sum(jnp.sum(value, axis=1, keepdims=True), axis=0, keepdims=True)


def place(scalars):
    lane = lax.broadcasted_iota(jnp.int32, (1, LO), 1)
    row = jnp.zeros((1, LO), F32)
    for index, scalar in enumerate(scalars):
        row = jnp.where(lane == index, scalar, row)
    return row


def column(row):
    size = row.shape[1]
    square = lax.broadcasted_iota(jnp.int32, (size, size), 0) == lax.broadcasted_iota(jnp.int32, (size, size), 1)
    return jnp.sum(jnp.where(square, jnp.broadcast_to(row, (size, size)), 0.0), axis=1, keepdims=True)


def flatten(square):
    lane = lax.broadcasted_iota(jnp.int32, (16, ENTRIES), 1)
    sub = lax.broadcasted_iota(jnp.int32, (16, ENTRIES), 0)
    spreader = jnp.where(lax.bitwise_and(lane, 15) == sub, 1.0, 0.0)
    wide = jnp.dot(square, spreader, precision=lax.Precision.HIGHEST, preferred_element_type=F32)
    return jnp.sum(jnp.where(lax.shift_right_logical(lane, 4) == sub, wide, 0.0), axis=0, keepdims=True)


def list_row(split_ref, curve_ref, t):
    return split_ref[0, 0, t : t + 1, :] if t < 2 else curve_ref[0, 0, t - 2 : t - 1, :]


def list_hot(hot_ref, t):
    return hot_ref[:, WIDE + t * LO : WIDE + (t + 1) * LO]


def point_hot(hot_ref, e):
    return hot_ref[:, e * POINTS : (e + 1) * POINTS]


def owner_mask():
    lane = lax.broadcasted_iota(jnp.int32, (ELEMS, ENTRIES), 1)
    return lax.bitwise_and(lane, 15) == lax.broadcasted_iota(jnp.int32, (ELEMS, ENTRIES), 0)


def coarse_line(scaled, phi_ref, pick_ref):
    acc = jnp.zeros((ELEMS, ENTRIES), F32)
    for v in range(8):
        restricted = jnp.sum(scaled * phi_ref[v : v + 1, :], axis=1, keepdims=True)
        acc = acc + restricted * pick_ref[v]
    return jnp.sum(acc, axis=0, keepdims=True)


def coarse_correction(image, phi_ref, pick_ref, xcols, xhot):
    line = take(table_parts(image), xhot, row_mask(xcols, ROWS))
    result = jnp.zeros((ELEMS, POINTS), F32)
    for v in range(8):
        vertex = jnp.sum(pick_ref[v] * line, axis=1, keepdims=True)
        result = result + vertex * phi_ref[v : v + 1, :]
    return result


def image_of(line, cols, hot):
    return fold(put(spread([line], row_mask(cols, ROWS)), hot), ROWS)


def write_payload(pay_ref, image, rows):
    here = lax.axis_index("split")
    for g in range(8):
        for r in range(8):
            pay_ref[g, 0:1, r * LO : (r + 1) * LO] = image[8 * g + r : 8 * g + r + 1, :]
        row = jnp.where(here == g + 1, rows[0], jnp.where(here == g - 1, rows[1], jnp.zeros((1, LO), F32)))
        pay_ref[g, 0:1, CHUNK:] = row


def setup_scatter(
    rhs_ref, slot_ref, split_ref, curve_ref, stretch_ref, helm_ref, corner_ref, xvals_ref, xcols_ref, xcount_ref,
    mass_ref, diag_ref, phi_ref,
    hot_ref, sums_ref, scale_ref, line_ref, entry_ref, pick_ref, xhot_ref, *out_refs
):
    columns = [column(stretch_ref[d : d + 1, :]) for d in range(3)] + [column(helm_ref[...])]
    scale_ref[...] = jnp.concatenate(columns + columns, axis=1)
    diag = columns[3] * mass_ref[...]
    for d in range(3):
        diag = diag + columns[d] * diag_ref[d : d + 1, :]
    live = lax.broadcasted_iota(jnp.int32, (16, 16), 0) < jnp.broadcast_to(xcount_ref[...], (16, 16))
    factor = flatten(jnp.where(live, xvals_ref[...], 0.0))
    cols = flatten(xcols_ref[...].astype(F32))
    line_ref[...] = factor
    entries = (cols + 0.5).astype(jnp.int32)
    entry_ref[...] = entries
    xhot_ref[...] = lane_hot(entries)
    owner = lax.bitwise_and(lax.broadcasted_iota(jnp.int32, (ELEMS, ENTRIES), 1), 15)
    corners = [column(corner_ref[v : v + 1, :].astype(F32)) for v in range(8)]
    for v in range(8):
        pick_ref[v] = jnp.where((corners[v] + 0.5).astype(jnp.int32) == owner, factor, 0.0)
    corner = jnp.concatenate(corners, axis=1)
    lists = jnp.concatenate(
        [column(list_row(split_ref, curve_ref, t).astype(F32)) for t in range(LISTS)], axis=0
    )
    lists = (lists + 0.5).astype(jnp.int32)
    acc = jnp.zeros((9 * HI, LO), F32)
    weights = jnp.zeros((3 * ELEMS, LISTS * LO), F32)
    for e in range(ELEMS):
        slots = slot_ref[e : e + 1, :]
        hot = lane_hot(slots)
        hot_ref[:, e * POINTS : (e + 1) * POINTS] = hot
        mask = row_mask(slots, HI)
        left = spread([jnp.ones((1, POINTS), F32), diag[e : e + 1, :], rhs_ref[e : e + 1, :]], mask)
        acc = acc + put(left, hot)
        unknown = lax.broadcasted_iota(jnp.int32, (ELEMS, 8), 0).astype(F32)
        vertex = jnp.where(jnp.abs(corner[e : e + 1, :] - unknown) < 0.5, 1.0, 0.0)
        basis = jnp.dot(vertex, phi_ref[...], precision=lax.Precision.HIGHEST, preferred_element_type=F32)
        shape = (LISTS * LO, POINTS)
        same = jnp.where(jnp.broadcast_to(slots, shape) == jnp.broadcast_to(lists, shape), 1.0, 0.0)
        weights = weights + put(jnp.concatenate(pieces(basis), axis=0), same.astype(BF16))
    weights = fold(weights, ELEMS)
    tables = []
    for field in range(3):
        table = fold(acc[3 * HI * field : 3 * HI * (field + 1)], HI)
        sums_ref[field] = table
        tables.append(table_parts(table))
    for t in range(LISTS):
        slots = list_row(split_ref, curve_ref, t)
        hot = lane_hot(slots)
        hot_ref[:, WIDE + t * LO : WIDE + (t + 1) * LO] = hot
        mask = row_mask(slots, HI)
        rows = [take(tables[field], hot, mask) for field in range(3)]
        rows += [cols[:, :LO], cols[:, LO:], factor[:, :LO], factor[:, LO:], jnp.zeros((1, LO), F32)]
        for r in range(8):
            out_refs[t][r : r + 1, :] = rows[r]
        out_refs[t][8:24, :] = weights[:, t * LO : (t + 1) * LO]


def incoming_table(split_ref, curve_ref, hot_ref, rows):
    acc = jnp.zeros((3 * HI, LO), F32)
    for t in range(LISTS):
        mask = row_mask(list_row(split_ref, curve_ref, t), HI)
        acc = acc + put(spread([rows[t]], mask), list_hot(hot_ref, t))
    return fold(acc, HI)


def setup_gather(slot_ref, split_ref, curve_ref, hot_ref, sums_ref, phi_ref, pick_ref, entry_ref, xhot_ref, *refs):
    in_refs = refs[:LISTS]
    minv_ref, dinv_ref, right_ref, nline_ref, nentry_ref, nhot_ref, pay_ref, rows_ref = refs[LISTS:]
    tables = [
        table_parts(
            sums_ref[field] + incoming_table(split_ref, curve_ref, hot_ref, [ref[field : field + 1, :] for ref in in_refs])
        )
        for field in range(3)
    ]
    for e in range(ELEMS):
        mask = row_mask(slot_ref[e : e + 1, :], HI)
        hot = point_hot(hot_ref, e)
        minv_ref[e : e + 1, :] = 1.0 / take(tables[0], hot, mask)
        dinv_ref[e : e + 1, :] = 1.0 / take(tables[1], hot, mask)
        right_ref[e : e + 1, :] = take(tables[2], hot, mask)
    rows = []
    for t in range(LISTS):
        mult = take(tables[0], list_hot(hot_ref, t), row_mask(list_row(split_ref, curve_ref, t), HI))
        rows.append(jnp.where(mult > 0.5, 1.0 / jnp.where(mult > 0.5, mult, 1.0), 0.0))
        there = jnp.concatenate([in_refs[t][3:4, :], in_refs[t][4:5, :]], axis=1)
        entries = (there + 0.5).astype(jnp.int32)
        nentry_ref[t : t + 1, :] = entries
        nhot_ref[:, t * ENTRIES : (t + 1) * ENTRIES] = lane_hot(entries)
        nline_ref[t : t + 1, :] = jnp.concatenate([in_refs[t][5:6, :], in_refs[t][6:7, :]], axis=1)
    for t in range(2, LISTS):
        rows_ref[t - 2 : t - 1, :] = rows[t]
    line = coarse_line(right_ref[...] * minv_ref[...], phi_ref, pick_ref)
    write_payload(pay_ref, image_of(line, entry_ref[...], xhot_ref[...]), rows)


def operator(u, scale_ref, mass_ref, first_ref, second_ref):
    def product(parts, ref):
        rows = parts[0].shape[0]
        one = jnp.dot(jnp.concatenate(parts, axis=0), ref[0], preferred_element_type=F32)
        two = jnp.dot(jnp.concatenate(parts[:2], axis=0), ref[1], preferred_element_type=F32)
        three = jnp.dot(parts[0], ref[2], preferred_element_type=F32)
        return one[:rows] + (one[rows : 2 * rows] + two[:rows] + (one[2 * rows :] + two[rows:] + three))

    half = POINTS // 2
    parts = pieces(u)
    along = product(parts, first_ref)
    inside = product([jnp.concatenate([p[:, :half], p[:, half:]], axis=0) for p in parts], second_ref)
    second = jnp.concatenate([inside[:ELEMS, :half], inside[ELEMS:, :half]], axis=1)
    third = jnp.concatenate([inside[:ELEMS, half:], inside[ELEMS:, half:]], axis=1)
    result = scale_ref[:, 0:1] * along + scale_ref[:, 1:2] * second + scale_ref[:, 2:3] * third
    return mass_ref[...] * (result + scale_ref[:, 3:4] * u)


def scatter_points(field_ref, slot_ref, hot_ref):
    acc = jnp.zeros((3 * HI, LO), F32)
    for e in range(ELEMS):
        left = spread([field_ref[e : e + 1, :]], row_mask(slot_ref[e : e + 1, :], HI))
        acc = acc + put(left, point_hot(hot_ref, e))
    return fold(acc, HI)


def gather_points(table, slot_ref, hot_ref, out_ref):
    parts = table_parts(table)
    for e in range(ELEMS):
        out_ref[e : e + 1, :] = take(parts, point_hot(hot_ref, e), row_mask(slot_ref[e : e + 1, :], HI))


def send_lists(table, split_ref, curve_ref, hot_ref):
    parts = table_parts(table)
    return [
        take(parts, list_hot(hot_ref, t), row_mask(list_row(split_ref, curve_ref, t), HI)) for t in range(LISTS)
    ]


def halo_rows(shalo_ref, chalo_ref):
    return [shalo_ref[t : t + 1, :] for t in range(2)] + [chalo_ref[t : t + 1, :] for t in range(4)]


def krylov_step(index, last, *refs):
    (slot_ref, split_ref, curve_ref, hot_ref, scale_ref, mass_ref, first_ref, second_ref, phi_ref, pick_ref,
     entry_ref, xhot_ref, nline_ref, nentry_ref, nhot_ref, minv_ref, dinv_ref, norm_ref, gathered_ref,
     shalo_ref, chalo_ref) = refs[:21]
    refs = refs[21:]
    image_ref, field_ref = refs[-2:]
    refs = refs[:-2]
    rows = halo_rows(shalo_ref, chalo_ref)
    if index == 0:
        right_ref, *sent_refs = refs[:7]
        refs = refs[7:]
        force = right_ref[...]
    else:
        weight_ref, sums_ref = refs[:2]
        refs = refs[2:]
    base_ref, newnorm_ref, newsums_ref = refs[:3]
    refs = refs[3:]
    if index == 0:
        newweight_ref = refs[0]
        refs = refs[1:]
        for t in range(LISTS):
            newweight_ref[t] = sent_refs[t][8:24, :] * rows[t]
        weight_ref = newweight_ref
    else:
        force_ref = refs[0]
        refs = refs[1:]
        gather_points(
            sums_ref[...] + incoming_table(split_ref, curve_ref, hot_ref, rows), slot_ref, hot_ref, force_ref
        )
        force = force_ref[...]
    for g in range(8):
        for r in range(8):
            image_ref[8 * g + r : 8 * g + r + 1, :] = gathered_ref[g, 0:1, r * LO : (r + 1) * LO]
    image = image_ref[...]
    size = 1.0 + jnp.sqrt(total(image * image))
    lane = lax.broadcasted_iota(jnp.int32, (1, LO), 1)
    newnorm_ref[...] = jnp.where(lane == index, size, norm_ref[...]) if index else jnp.broadcast_to(size, (1, LO))
    correction = coarse_correction(image, phi_ref, pick_ref, entry_ref[...], xhot_ref[...])
    base = (force * dinv_ref[...] + correction) * (1.0 / size)
    base_ref[...] = base
    field_ref[...] = operator(base, scale_ref, mass_ref, first_ref, second_ref)
    table = scatter_points(field_ref, slot_ref, hot_ref)
    newsums_ref[...] = table
    rows = send_lists(table, split_ref, curve_ref, hot_ref)
    if last:
        for t in range(LISTS):
            refs[t][...] = rows[t]
        return
    pay_ref, rows_ref = refs
    for t in range(2, LISTS):
        rows_ref[t - 2 : t - 1, :] = rows[t]
    gather_points(table, slot_ref, hot_ref, field_ref)
    line = coarse_line(field_ref[...] * minv_ref[...], phi_ref, pick_ref)
    image = image_of(line, entry_ref[...], xhot_ref[...])
    owner = owner_mask()
    for t in range(LISTS):
        loads = jnp.sum(weight_ref[t] * rows[t], axis=1, keepdims=True)
        line = jnp.sum(jnp.where(owner, loads, 0.0), axis=0, keepdims=True) * nline_ref[t : t + 1, :]
        image = image + image_of(line, nentry_ref[t : t + 1, :], nhot_ref[:, t * ENTRIES : (t + 1) * ENTRIES])
    write_payload(pay_ref, image, rows)


def after_split(got_ref, rows_ref, pay_ref, shalo_ref):
    here, size = lax.axis_index("split"), got_ref.shape[0]
    for t, offset in enumerate((-1, 1)):
        there = here + offset
        row = got_ref[jnp.clip(there, 0, size - 1), 0:1, CHUNK:]
        shalo_ref[t : t + 1, :] = jnp.where(jnp.logical_and(there >= 0, there < size), row, jnp.zeros((1, LO), F32))
    chunk = got_ref[0, 0:1, :CHUNK]
    for g in range(1, size):
        chunk = chunk + got_ref[g, 0:1, :CHUNK]
    wide = jnp.concatenate([chunk, jnp.zeros((1, LO), F32)], axis=1)
    here, size = lax.axis_index("curve"), pay_ref.shape[0]
    for g in range(size):
        pay_ref[g] = wide
    for t, offset in enumerate((-2, -1, 1, 2)):
        there = here + offset

        @pl.when(jnp.logical_and(there >= 0, there < size))
        def _():
            pay_ref[jnp.clip(there, 0, size - 1), 0:1, CHUNK:] = rows_ref[t : t + 1, :]


def after_curve(got_ref, pay_ref, chalo_ref):
    here, size = lax.axis_index("curve"), got_ref.shape[0]
    for t, offset in enumerate((-2, -1, 1, 2)):
        there = here + offset
        row = got_ref[jnp.clip(there, 0, size - 1), 0:1, CHUNK:]
        chalo_ref[t : t + 1, :] = jnp.where(jnp.logical_and(there >= 0, there < size), row, jnp.zeros((1, LO), F32))
    sums = [got_ref[g, 0:1, :CHUNK] for g in range(4)]
    for g in range(4, size):
        sums[g % 4] = sums[g % 4] + got_ref[g, 0:1, :CHUNK]
    chunk = (sums[0] + sums[1]) + (sums[2] + sums[3])
    for g in range(pay_ref.shape[0]):
        pay_ref[g] = chunk


def gram(*refs):
    slot_ref, split_ref, curve_ref, hot_ref, sums_ref, minv_ref, right_ref = refs[:7]
    base_refs, force_refs, in_refs = refs[7:11], refs[11:14], refs[14:20]
    last_ref, pay_ref = refs[20:]
    rows = [ref[...] for ref in in_refs]
    gather_points(
        sums_ref[...] + incoming_table(split_ref, curve_ref, hot_ref, rows), slot_ref, hot_ref, last_ref
    )
    weighted = [ref[...] * minv_ref[...] for ref in base_refs]
    scalars = []
    for ref in (right_ref, *force_refs, last_ref):
        scalars += [total(ref[...] * base) for base in weighted]
    row = place(scalars)
    for g in range(pay_ref.shape[0]):
        pay_ref[g] = row


def finish(*refs):
    got_ref, norm_ref, right_ref = refs[:3]
    base_refs, force_refs = refs[3:7], refs[7:11]
    solution_ref, residual_ref = refs[11:]
    sums = [got_ref[g] for g in range(8)]
    for g in range(8, got_ref.shape[0]):
        sums[g % 8] = sums[g % 8] + got_ref[g]
    row = ((sums[0] + sums[1]) + (sums[2] + sums[3])) + ((sums[4] + sums[5]) + (sums[6] + sums[7]))
    table = [[row[:, 4 * i + j : 4 * i + j + 1] for j in range(4)] for i in range(5)]
    norms = [norm_ref[0:1, j : j + 1] for j in range(4)]

    def pair(left, right):
        acc = None
        for i, a in enumerate(left):
            inner = None
            for j, b in enumerate(right):
                if b is not None:
                    inner = b * table[i][j] if inner is None else inner + b * table[i][j]
            if a is not None and inner is not None:
                acc = a * inner if acc is None else acc + a * inner
        return acc

    def less(value, factor, other):
        if other is None:
            return value
        return -factor * other if value is None else value - factor * other

    residual = [jnp.ones((1, 1), F32)] + [None] * 4
    precond = [norms[0]] + [None] * 3
    direction = list(precond)
    solution = [None] * 4
    rz = pair(residual, precond)
    for k in range(ITERS):
        moved = [None] + direction
        alpha = rz / pair(moved, direction)
        solution = [less(value, -alpha, other) for value, other in zip(solution, direction)]
        residual = [less(value, alpha, other) for value, other in zip(residual, moved)]
        if k < ITERS - 1:
            shifted = [None] + [None if d is None else d * norms[j + 1] for j, d in enumerate(direction[:3])]
            precond = [less(value, alpha, other) for value, other in zip(precond, shifted)]
            rz_next = pair(residual, precond)
            beta = rz_next / rz
            direction = [less(value, -beta, other) for value, other in zip(precond, direction)]
            rz = rz_next
    result = solution[0] * base_refs[0][...]
    for j in range(1, 4):
        result = result + solution[j] * base_refs[j][...]
    solution_ref[...] = result
    result = right_ref[...]
    for j in range(4):
        result = result + residual[j + 1] * force_refs[j][...]
    residual_ref[...] = result


def run(body, name, args, outs, scratch=()):
    return pl.pallas_call(
        body,
        name=name,
        out_shape=[jax.ShapeDtypeStruct(shape, dtype) for shape, dtype in outs],
        in_specs=[pl.BlockSpec(memory_space=pltpu.VMEM) for _ in args],
        out_specs=[pl.BlockSpec(memory_space=pltpu.VMEM) for _ in outs],
        scratch_shapes=list(scratch),
        compiler_params=pltpu.CompilerParams(vmem_limit_bytes=VMEM_LIMIT),
    )(*args)


def shift(block, axis, offset):
    size = lax.axis_size(axis)
    route = [(i, i + offset) for i in range(size) if 0 <= i + offset < size]
    return lax.ppermute(block, axis, route)


WAYS = (("split", -1), ("split", 1), ("curve", -2), ("curve", -1), ("curve", 1), ("curve", 2))


def exchange(outgoing):
    arrived = [None] * LISTS
    for t, (axis, offset) in enumerate(WAYS):
        back = WAYS.index((axis, -offset))
        arrived[back] = shift(outgoing[t], axis, offset)
    return arrived


def reduce_image(pay, rows):
    splits, curves = lax.axis_size("split"), lax.axis_size("curve")
    got = lax.all_to_all(pay, "split", 0, 0)
    pay, shalo = run(
        after_split, "after_split", (got, rows), [((curves, 1, CHUNK + LO), F32), ((2, LO), F32)]
    )
    got = lax.all_to_all(pay, "curve", 0, 0)
    pay, chalo = run(after_curve, "after_curve", (got,), [((splits, 1, CHUNK), F32), ((4, LO), F32)])
    return lax.all_to_all(pay, "split", 0, 0), shalo, chalo


def local(rhs_load, stretch, helm_shift, local_slot, share_curve, share_split, coarse_slot, x_vals, x_cols, x_count):
    mass, first, second, diags, coarse = element_tables()
    mass = jnp.asarray(mass.reshape(1, -1), F32)
    diags = jnp.asarray(diags, F32)
    phi = jnp.asarray(coarse, F32)
    first = jnp.asarray(table_pieces(first))
    second = jnp.asarray(table_pieces(second))
    field = ((ELEMS, POINTS), F32)
    table = ((HI, LO), F32)
    line = ((1, LO), F32)
    payload = [((8, 1, CHUNK + LO), F32), ((4, LO), F32)]
    entry = jnp.int32

    hot, sums3, scale, _, entries, pick, xhot, *sent = run(
        setup_scatter,
        "setup_scatter",
        (rhs_load, local_slot, share_split, share_curve, stretch, helm_shift.reshape(1, -1), coarse_slot, x_vals,
         x_cols, x_count.reshape(1, -1), mass, diags, phi),
        [((LO, WIDE + LISTS * LO), BF16), ((3, HI, LO), F32), ((ELEMS, 8), F32), ((1, ENTRIES), F32),
         ((1, ENTRIES), entry), ((8, ELEMS, ENTRIES), F32), ((LO, ENTRIES), BF16)] + [((24, LO), F32)] * LISTS,
    )
    arrived = exchange(sent)
    shape = (local_slot, share_split, share_curve, hot)
    minv, dinv, right, nline, nentry, nhot, pay, rows = run(
        setup_gather,
        "setup_gather",
        (*shape, sums3, phi, pick, entries, xhot, *arrived),
        [field, field, field, ((LISTS, ENTRIES), F32), ((LISTS, ENTRIES), entry), ((LO, LISTS * ENTRIES), BF16)]
        + payload,
    )
    common = (*shape, scale, mass, first, second, phi, pick, entries, xhot, nline, nentry, nhot, minv, dinv)
    scratch = [pltpu.VMEM((ROWS, LO), F32), pltpu.VMEM((ELEMS, POINTS), F32)]
    norm = jnp.ones((1, LO), F32)
    bases, forces = [], []
    for index in range(ITERS):
        last = index == ITERS - 1
        gathered, shalo, chalo = reduce_image(pay, rows)
        own = (right, *arrived) if index == 0 else (weight, sums)
        outs = [field, line, table] + [((LISTS, ELEMS, LO), F32) if index == 0 else field]
        base, norm, sums, extra, *rest = run(
            functools.partial(krylov_step, index, last),
            f"krylov_step{index}",
            (*common, norm, gathered, shalo, chalo, *own),
            outs + ([line] * LISTS if last else payload),
            scratch,
        )
        bases.append(base)
        if index == 0:
            weight = extra
        else:
            forces.append(extra)
        if not last:
            pay, rows = rest
    devices = lax.axis_size("curve") * lax.axis_size("split")
    force, pay = run(
        gram,
        "gram",
        (*shape, sums, minv, right, *bases, *forces, *exchange(rest)),
        [field, ((devices, 1, LO), F32)],
    )
    got = lax.all_to_all(pay, ("curve", "split"), 0, 0)
    solution, residual = run(
        finish, "finish", (got, norm, right, *bases, *forces, force), [field, field]
    )
    return solution, residual


def solution(mesh):
    in_specs = (
        P(("curve", "split"), None),
        P(None, ("curve", "split")),
        P(("curve", "split")),
        P(("curve", "split"), None),
        P("curve", "split", None, None),
        P("curve", "split", None, None),
        P(None, ("curve", "split")),
        P(None, ("curve", "split")),
        P(None, ("curve", "split")),
        P(("curve", "split")),
    )
    out_specs = (P(("curve", "split"), None), P(("curve", "split"), None))
    return jax.shard_map(local, mesh=mesh, in_specs=in_specs, out_specs=out_specs, check_vma=False)
```

time: 443 us -> 291 us (0.66)
  local copies, waits for them, and re-layouts: 64.8 us -> 10.7 us
  starting transfers between devices: 75.8 us -> 29.8 us
  blocking collectives: 250 us -> 208 us
  other arithmetic: 14 us -> 0 us
  Pallas kernels: 20.3 us -> 34 us
  waiting for transfers between devices: 11.9 us -> 6.08 us
    ppermute x30 -> x12, starting transfers between devices: 75.8 us -> 29.8 us  [shift(): return lax.ppermute(block, axis, route)]
    unnamed x204 -> x42, local copies, waits for them, and re-layouts: 56.1 us -> 10.7 us
    all_to_all x13, blocking collectives: 250 us -> 208 us  [the longest x4 94.1 us: reduce_image(): got = lax.all_to_all(pay, 'curve', 0, 0)]
    pallas_call x11 -> x16, Pallas kernels: 20.3 us -> 34 us  [run(): pl.pallas_call(body, name=name, out_shape=[jax.ShapeDtypeStruct(shape, dt...]
    reduce_sum x8 -> x0, other arithmetic: 12.6 us -> none  [the longest x4 6.83 us: reduce_all(): jnp.sum(swap(jnp.broadcast_to(part[None], (size,) + part.shape), 'curve')...]
    broadcast_in_dim x10 -> x1, local copies, waits for them, and re-layouts: 5.9 us -> 0.01 us  [local(): norm = jnp.ones((1, LO), F32)]
    ppermute x30 -> x12, waiting for transfers between devices: 11.9 us -> 6.08 us  [shift(): return lax.ppermute(block, axis, route)]
  transfers between devices with their start and end apart: 30 -> 12, of which waited for: 8 -> 4; matrix products, arithmetic and copies ran while one was open for 1% -> 0% of each run, Pallas kernels for 0% -> 0%
where the time goes in v2:
time: 291 us; the launch traced here: 290 us
  blocking collectives  208 us (71%)
  Pallas kernels  34 us (12%)
  starting transfers between devices  29.8 us (10%)
  local copies, waits for them, and re-layouts  10.7 us (4%)
  waiting for transfers between devices  6.08 us (2%)
    all_to_all x4, blocking collectives, reduce_image(): got = lax.all_to_all(pay, 'curve', 0, 0)  94.1 us
    all_to_all x4, blocking collectives, reduce_image(): got = lax.all_to_all(pay, 'split', 0, 0)  43.8 us
    all_to_all x4, blocking collectives, reduce_image(): return (lax.all_to_all(pay, 'split', 0, 0), shalo, chalo)  36.9 us
    pallas_call x16, Pallas kernels, run(): pl.pallas_call(body, name=name, out_shape=[jax.ShapeDtypeStruct(shape, dt...  34 us
    all_to_all x1, blocking collectives, local(): got = lax.all_to_all(pay, ('curve', 'split'), 0, 0)  33.7 us
    ppermute x12, starting transfers between devices, shift(): return lax.ppermute(block, axis, route)  29.8 us
    unnamed x42, local copies, waits for them, and re-layouts  10.7 us
    ppermute x12, waiting for transfers between devices, shift(): return lax.ppermute(block, axis, route)  6.08 us
  transfers between devices with their start and end apart: 12, of which 4 were waited for; matrix products, arithmetic and copies ran while one was open for 0% of the time, Pallas kernels for 0%

profile of v2, /device:TPU:1, one launch (start us, length us, event | category | flops | bytes accessed | tf_op | source)
XLA Modules:
  0.0 290.0 jit_solution(2393208592145838151)
XLA Ops:
  9.9 8.3 %setup_scatter.1 = (bf16[128,8960]{1,0:T(8,128)(2,1)S(1)}, f32[3,48,128]{2,1,0:T(8,128)S(1)}, f32[16,8]{1,0:T(8,128)S(1)}, f32[1,256]{1,0:T(1,128)}, s32[1,256]{...) custom-call(f32[16,512]{1,0:T(8,128)S(1)} %copy-done.13, ...), custom_call_target="tpu_custom_call" | custom-call | tf_op jit(solution)/shard_map/setup_scatter/pallas_call | solution.py:515
  18.2 4.0 %collective-permute-start = (f32[24,128]{1,0:T(8,128)S(1)}, f32[24,128]{1,0:T(8,128)S(1)}, u32[]{:S(2)}, u32[]{:S(2)}) collective-permute-start(f32[24,128]{1,0:T(8,128)S(1)} %get-tuple-element.74), channel_id=1, source_target_pairs={{0,1},{1,2},{2,3},{3,4},{4,5},{5,6},{6,7},{8,9},{9,10},{10,11},{11... | collective-permute-start | bytes 36872 | tf_op jit(solution)/shard_map/ppermute | solution.py:529
  23.5 3.1 %collective-permute-start.2 = (f32[24,128]{1,0:T(8,128)S(1)}, f32[24,128]{1,0:T(8,128)S(1)}, u32[]{:S(2)}, u32[]{:S(2)}) collective-permute-start(f32[24,128]{1,0:T(8,128)S(1)} %get-tuple-element.76), channel_id=1, source_target_pairs={{0,16},{8,24},{16,32},{24,40},{32,48},{40,56},{48,64},{56,72},{64,... | collective-permute-start | bytes 36872 | tf_op jit(solution)/shard_map/ppermute | solution.py:529
  26.6 4.2 %collective-permute-start.3 = (f32[24,128]{1,0:T(8,128)S(1)}, f32[24,128]{1,0:T(8,128)S(1)}, u32[]{:S(2)}, u32[]{:S(2)}) collective-permute-start(f32[24,128]{1,0:T(8,128)S(1)} %get-tuple-element.77), channel_id=1, source_target_pairs={{0,8},{8,16},{16,24},{24,32},{32,40},{40,48},{48,56},{56,64},{64,7... | collective-permute-start | bytes 36872 | tf_op jit(solution)/shard_map/ppermute | solution.py:529
  30.9 1.9 collective-permute-start.4
  34.1 1.7 collective-permute-done.4.refs_4_.refs_26_
  35.9 1.4 collective-permute-done.5.refs_5_.refs_27_
  38.7 4.2 %setup_gather.1 = (f32[16,512]{1,0:T(8,128)S(1)}, f32[16,512]{1,0:T(8,128)S(1)}, f32[16,512]{1,0:T(8,128)S(1)}, f32[6,256]{1,0:T(8,128)S(1)}, s32[6,256]{1,0:T(8...) custom-call(s32[16,512]{1,0:T(8,128)S(1)} %copy-done.3, ...), custom_call_target="tpu_custom_call" | custom-call | tf_op jit(solution)/shard_map/setup_gather/pallas_call | solution.py:515
  42.9 15.9 %all_to_all.65.got_ref = f32[8,1,1152]{2,1,0:T(1,128)S(1)} all-to-all(f32[8,1,1152]{2,1,0:T(1,128)S(1)} %get-tuple-element.85), channel_id=1, replica_groups=mesh['curve'=64,'split'=8] {'split'}, dimensions={0} | all-to-all | bytes 73728 | tf_op jit(solution)/shard_map/all_to_all | solution.py:545
  58.9 32.0 %all_to_all.66.got_ref = f32[64,1,1152]{2,1,0:T(1,128)S(1)} all-to-all(f32[64,1,1152]{2,1,0:T(1,128)S(1)} %get-tuple-element.87), channel_id=1, replica_groups=mesh['curve'=64,'split'=8] {'curve'}, dimensions={0} | all-to-all | bytes 589824 | tf_op jit(solution)/shard_map/all_to_all | solution.py:549
  90.9 9.2 %all_to_all.67.refs_18_ = f32[8,1,1024]{2,1,0:T(1,128)S(1)} all-to-all(f32[8,1,1024]{2,1,0:T(1,128)S(1)} %get-tuple-element.88), channel_id=1, replica_groups=mesh['curve'=64,'split'=8] {'split'}, dimensions={0} | all-to-all | bytes 65536 | tf_op jit(solution)/shard_map/all_to_all | solution.py:551
  100.1 4.2 %krylov_step0.1 = (f32[16,512]{1,0:T(8,128)S(1)}, f32[1,128]{1,0:T(1,128)S(1)}, f32[48,128]{1,0:T(8,128)S(1)}, f32[6,16,128]{2,1,0:T(8,128)S(1)}, f32[8,1,1152]{2,1,0:T(1,128)S(1)}, /*index=5*/f32[4,128]{1,0:T(4,128)S(1)}) custom-call(s32[16,512]{1,0:T(8,128)S(1)} %copy-done.4, s32[1,1,2,128]{3,2,1,0:T(2,128)S(1)} %copy-done.12, ...), custom_call_target="tpu_custom_call" | custom-call | tf_op jit(solution)/shard_map/krylov_step0/pallas_call | solution.py:515
  104.3 9.3 %all_to_all.68.got_ref = f32[8,1,1152]{2,1,0:T(1,128)S(1)} all-to-all(f32[8,1,1152]{2,1,0:T(1,128)S(1)} %get-tuple-element.93), channel_id=1, replica_groups=mesh['curve'=64,'split'=8] {'split'}, dimensions={0} | all-to-all | bytes 73728 | tf_op jit(solution)/shard_map/all_to_all | solution.py:545
  113.7 20.7 %all_to_all.69.got_ref = f32[64,1,1152]{2,1,0:T(1,128)S(1)} all-to-all(f32[64,1,1152]{2,1,0:T(1,128)S(1)} %get-tuple-element.95), channel_id=1, replica_groups=mesh['curve'=64,'split'=8] {'curve'}, dimensions={0} | all-to-all | bytes 589824 | tf_op jit(solution)/shard_map/all_to_all | solution.py:549
  134.4 9.2 %all_to_all.70.refs_18_ = f32[8,1,1024]{2,1,0:T(1,128)S(1)} all-to-all(f32[8,1,1024]{2,1,0:T(1,128)S(1)} %get-tuple-element.96), channel_id=1, replica_groups=mesh['curve'=64,'split'=8] {'split'}, dimensions={0} | all-to-all | bytes 65536 | tf_op jit(solution)/shard_map/all_to_all | solution.py:551
  143.7 5.5 %krylov_step1.1 = (f32[16,512]{1,0:T(8,128)S(1)}, f32[1,128]{1,0:T(1,128)S(1)}, f32[48,128]{1,0:T(8,128)S(1)}, f32[16,512]{1,0:T(8,128)S(1)}, f32[8,1,1152]{2,1,0:T(1,128)S(1)}, /*index=5*/f32[4,128]{1,0:T(4,128)S(1)}) custom-call(s32[16,512]{1,0:T(8,128)S(1)} %copy-done.4, s32[1,1,2,128]{3,2,1,0:T(2,128)S(1)} %copy-done.12, s32[1,1,4,128]{3,2,1,0:T(4,128)S(1)} %copy-done.8, ...), custom_call_target="tpu_custom_call" | custom-call | tf_op jit(solution)/shard_map/krylov_step1/pallas_call | solution.py:515
  149.2 9.3 %all_to_all.71.got_ref = f32[8,1,1152]{2,1,0:T(1,128)S(1)} all-to-all(f32[8,1,1152]{2,1,0:T(1,128)S(1)} %get-tuple-element.102), channel_id=1, replica_groups=mesh['curve'=64,'split'=8] {'split'}, dimensions={0} | all-to-all | bytes 73728 | tf_op jit(solution)/shard_map/all_to_all | solution.py:545
  158.6 20.7 %all_to_all.72.got_ref = f32[64,1,1152]{2,1,0:T(1,128)S(1)} all-to-all(f32[64,1,1152]{2,1,0:T(1,128)S(1)} %get-tuple-element.104), channel_id=1, replica_groups=mesh['curve'=64,'split'=8] {'curve'}, dimensions={0} | all-to-all | bytes 589824 | tf_op jit(solution)/shard_map/all_to_all | solution.py:549
  179.3 9.2 %all_to_all.73.refs_18_ = f32[8,1,1024]{2,1,0:T(1,128)S(1)} all-to-all(f32[8,1,1024]{2,1,0:T(1,128)S(1)} %get-tuple-element.105), channel_id=1, replica_groups=mesh['curve'=64,'split'=8] {'split'}, dimensions={0} | all-to-all | bytes 65536 | tf_op jit(solution)/shard_map/all_to_all | solution.py:551
  188.5 5.5 %krylov_step2.1 = (f32[16,512]{1,0:T(8,128)S(1)}, f32[1,128]{1,0:T(1,128)S(1)}, f32[48,128]{1,0:T(8,128)S(1)}, f32[16,512]{1,0:T(8,128)S(1)}, f32[8,1,1152]{2,1,0:T(1,128)S(1)}, /*index=5*/f32[4,128]{1,0:T(4,128)S(1)}) custom-call(s32[16,512]{1,0:T(8,128)S(1)} %copy-done.4, s32[1,1,2,128]{3,2,1,0:T(2,128)S(1)} %copy-done.12, s32[1,1,4,128]{3,2,1,0:T(4,128)S(1)} %copy-done.8, ...), custom_call_target="tpu_custom_call" | custom-call | tf_op jit(solution)/shard_map/krylov_step2/pallas_call | solution.py:515
  194.0 9.3 %all_to_all.74.got_ref = f32[8,1,1152]{2,1,0:T(1,128)S(1)} all-to-all(f32[8,1,1152]{2,1,0:T(1,128)S(1)} %get-tuple-element.110), channel_id=1, replica_groups=mesh['curve'=64,'split'=8] {'split'}, dimensions={0} | all-to-all | bytes 73728 | tf_op jit(solution)/shard_map/all_to_all | solution.py:545
  203.3 20.7 %all_to_all.75.got_ref = f32[64,1,1152]{2,1,0:T(1,128)S(1)} all-to-all(f32[64,1,1152]{2,1,0:T(1,128)S(1)} %get-tuple-element.112), channel_id=1, replica_groups=mesh['curve'=64,'split'=8] {'curve'}, dimensions={0} | all-to-all | bytes 589824 | tf_op jit(solution)/shard_map/all_to_all | solution.py:549
  224.1 9.2 %all_to_all.76.refs_18_ = f32[8,1,1024]{2,1,0:T(1,128)S(1)} all-to-all(f32[8,1,1024]{2,1,0:T(1,128)S(1)} %get-tuple-element.113), channel_id=1, replica_groups=mesh['curve'=64,'split'=8] {'split'}, dimensions={0} | all-to-all | bytes 65536 | tf_op jit(solution)/shard_map/all_to_all | solution.py:551
  233.3 3.4 %krylov_step3.1 = (f32[16,512]{1,0:T(8,128)S(1)}, f32[1,128]{1,0:T(1,128)S(1)}, f32[48,128]{1,0:T(8,128)S(1)}, f32[16,512]{1,0:T(8,128)S(1)}, f32[1,128]{1,0:T(1...) custom-call(s32[16,512]{1,0:T(8,128)S(1)} %copy-done.4, ...), custom_call_target="tpu_custom_call" | custom-call | tf_op jit(solution)/shard_map/krylov_step3/pallas_call | solution.py:515
  236.7 2.2 collective-permute-start.6
  240.2 2.4 collective-permute-start.8
  242.6 4.8 %collective-permute-start.9 = (f32[1,128]{1,0:T(1,128)S(1)}, f32[1,128]{1,0:T(1,128)S(1)}, u32[]{:S(2)}, u32[]{:S(2)}) collective-permute-start(f32[1,128]{1,0:T(1,128)S(1)} %get-tuple-element.128), channel_id=1, source_target_pairs={{0,8},{8,16},{16,24},{24,32},{32,40},{40,48},{48,56},{56,64},{64,7... | collective-permute-start | bytes 1544 | tf_op jit(solution)/shard_map/ppermute | solution.py:529
  247.4 1.9 collective-permute-start.10
  250.7 1.6 collective-permute-done.10.refs_18_
  252.3 1.4 collective-permute-done.11.refs_19_
  253.6 1.7 gram.1
  255.4 33.7 %all_to_all.77.refs_0_ = f32[512,1,128]{2,1,0:T(1,128)S(1)} all-to-all(f32[512,1,128]{2,1,0:T(1,128)S(1)} %get-tuple-element.131), channel_id=1, replica_groups=mesh['curve'=64,'split'=8] {'curve','split'}, dimensions={0} | all-to-all | bytes 524288 | tf_op jit(solution)/shard_map/all_to_all | solution.py:614
  (64 shorter events, 17.2 us)
Async XLA Ops:
  0.6 99.5 %copy-start.10 = (f32[1,512]{1,0:T(1,128)S(1)}, f32[1,512]{1,0:T(1,128)}, u32[]{:S(2)}) copy-start(f32[1,512]{1,0:T(1,128)} %constant.12.clone.mass_ref.refs_5_) | copy-start | bytes 6148
  0.6 99.5 %copy-start.1 = (bf16[3,256,512]{2,1,0:T(8,128)(2,1)S(1)}, bf16[3,256,512]{2,1,0:T(8,128)(2,1)}, u32[]{:S(2)}) copy-start(bf16[3,256,512]{2,1,0:T(8,128)(2,1)} %constant.16.clone.refs_7_) | copy-start | bytes 2359300
  0.7 99.5 %copy-start = (bf16[3,512,512]{2,1,0:T(8,128)(2,1)S(1)}, bf16[3,512,512]{2,1,0:T(8,128)(2,1)}, u32[]{:S(2)}) copy-start(bf16[3,512,512]{2,1,0:T(8,128)(2,1)} %constant.15.clone.refs_6_) | copy-start | bytes 4718596
  0.7 0.9 copy-start.2
  1.6 0.7 copy-start.5
  2.3 0.7 copy-start.7
  3.0 0.7 copy-start.9
  3.7 0.7 copy-start.11
  4.3 0.8 copy-start.13
  5.1 0.7 copy-start.14
  5.8 0.7 copy-start.15
  6.5 0.7 copy-start.16
  7.2 0.7 copy-start.17
  7.9 0.7 copy-start.18
  8.6 0.7 copy-start.19
  18.2 14.6 %collective-permute-start = (f32[24,128]{1,0:T(8,128)S(1)}, f32[24,128]{1,0:T(8,128)S(1)}, u32[]{:S(2)}, u32[]{:S(2)}) collective-permute-start(f32[24,128]{1,0:T(8,128)S(1)} %get-tuple-element.74), channel_id=1, source_target_pairs={{0,1},{1,2},{2,3},{3,4},{4,5},{5,6},{6,7},{8,9},{9,10},{10,11},{11... | collective-permute-start | bytes 36872 | tf_op jit(solution)/shard_map/ppermute | solution.py:529
  22.2 11.9 %collective-permute-start.1 = (f32[24,128]{1,0:T(8,128)S(1)}, f32[24,128]{1,0:T(8,128)S(1)}, u32[]{:S(2)}, u32[]{:S(2)}) collective-permute-start(f32[24,128]{1,0:T(8,128)S(1)} %get-tuple-element.75), channel_id=1, source_target_pairs={{1,0},{2,1},{3,2},{4,3},{5,4},{6,5},{7,6},{9,8},{10,9},{11,10},{12... | collective-permute-start | bytes 36872 | tf_op jit(solution)/shard_map/ppermute | solution.py:529
  23.5 10.6 %collective-permute-start.2 = (f32[24,128]{1,0:T(8,128)S(1)}, f32[24,128]{1,0:T(8,128)S(1)}, u32[]{:S(2)}, u32[]{:S(2)}) collective-permute-start(f32[24,128]{1,0:T(8,128)S(1)} %get-tuple-element.76), channel_id=1, source_target_pairs={{0,16},{8,24},{16,32},{24,40},{32,48},{40,56},{48,64},{56,72},{64,... | collective-permute-start | bytes 36872 | tf_op jit(solution)/shard_map/ppermute | solution.py:529
  26.6 7.5 %collective-permute-start.3 = (f32[24,128]{1,0:T(8,128)S(1)}, f32[24,128]{1,0:T(8,128)S(1)}, u32[]{:S(2)}, u32[]{:S(2)}) collective-permute-start(f32[24,128]{1,0:T(8,128)S(1)} %get-tuple-element.77), channel_id=1, source_target_pairs={{0,8},{8,16},{16,24},{24,32},{32,40},{40,48},{48,56},{56,64},{64,7... | collective-permute-start | bytes 36872 | tf_op jit(solution)/shard_map/ppermute | solution.py:529
  30.9 5.0 %collective-permute-start.4 = (f32[24,128]{1,0:T(8,128)S(1)}, f32[24,128]{1,0:T(8,128)S(1)}, u32[]{:S(2)}, u32[]{:S(2)}) collective-permute-start(f32[24,128]{1,0:T(8,128)S(1)} %get-tuple-element.78), channel_id=1, source_target_pairs={{8,0},{16,8},{24,16},{32,24},{40,32},{48,40},{56,48},{64,56},{72,6... | collective-permute-start | bytes 36872 | tf_op jit(solution)/shard_map/ppermute | solution.py:529
  32.8 4.4 %collective-permute-start.5 = (f32[24,128]{1,0:T(8,128)S(1)}, f32[24,128]{1,0:T(8,128)S(1)}, u32[]{:S(2)}, u32[]{:S(2)}) collective-permute-start(f32[24,128]{1,0:T(8,128)S(1)} %get-tuple-element.79), channel_id=1, source_target_pairs={{16,0},{24,8},{32,16},{40,24},{48,32},{56,40},{64,48},{72,56},{80,... | collective-permute-start | bytes 36872 | tf_op jit(solution)/shard_map/ppermute | solution.py:529
  37.2 0.8 copy-start.3
  38.0 0.7 copy-start.6
  38.7 61.4 %copy-start.4 = (s32[16,512]{1,0:T(8,128)S(1)}, s32[16,512]{1,0:T(8,128)}, u32[]{:S(2)}) copy-start(s32[16,512]{1,0:T(8,128)} %refs_0_.9) | copy-start | bytes 98308
  38.7 61.4 %copy-start.8 = (s32[1,1,4,128]{3,2,1,0:T(4,128)S(1)}, s32[1,1,4,128]{3,2,1,0:T(4,128)}, u32[]{:S(2)}) copy-start(s32[1,1,4,128]{3,2,1,0:T(4,128)} %refs_2_.9) | copy-start | bytes 6148
  38.7 61.4 %copy-start.12 = (s32[1,1,2,128]{3,2,1,0:T(2,128)S(1)}, s32[1,1,2,128]{3,2,1,0:T(2,128)}, u32[]{:S(2)}) copy-start(s32[1,1,2,128]{3,2,1,0:T(2,128)} %refs_1_.9) | copy-start | bytes 3076
  236.7 12.7 %collective-permute-start.6 = (f32[1,128]{1,0:T(1,128)S(1)}, f32[1,128]{1,0:T(1,128)S(1)}, u32[]{:S(2)}, u32[]{:S(2)}) collective-permute-start(f32[1,128]{1,0:T(1,128)S(1)} %get-tuple-element.125), channel_id=1, source_target_pairs={{0,1},{1,2},{2,3},{3,4},{4,5},{5,6},{6,7},{8,9},{9,10},{10,11},{11... | collective-permute-start | bytes 1544 | tf_op jit(solution)/shard_map/ppermute | solution.py:529
  238.9 11.8 %collective-permute-start.7 = (f32[1,128]{1,0:T(1,128)S(1)}, f32[1,128]{1,0:T(1,128)S(1)}, u32[]{:S(2)}, u32[]{:S(2)}) collective-permute-start(f32[1,128]{1,0:T(1,128)S(1)} %get-tuple-element.126), channel_id=1, source_target_pairs={{1,0},{2,1},{3,2},{4,3},{5,4},{6,5},{7,6},{9,8},{10,9},{11,10},{12... | collective-permute-start | bytes 1544 | tf_op jit(solution)/shard_map/ppermute | solution.py:529
  240.2 10.5 %collective-permute-start.8 = (f32[1,128]{1,0:T(1,128)S(1)}, f32[1,128]{1,0:T(1,128)S(1)}, u32[]{:S(2)}, u32[]{:S(2)}) collective-permute-start(f32[1,128]{1,0:T(1,128)S(1)} %get-tuple-element.127), channel_id=1, source_target_pairs={{0,16},{8,24},{16,32},{24,40},{32,48},{40,56},{48,64},{56,72},{64,... | collective-permute-start | bytes 1544 | tf_op jit(solution)/shard_map/ppermute | solution.py:529
  242.6 8.1 %collective-permute-start.9 = (f32[1,128]{1,0:T(1,128)S(1)}, f32[1,128]{1,0:T(1,128)S(1)}, u32[]{:S(2)}, u32[]{:S(2)}) collective-permute-start(f32[1,128]{1,0:T(1,128)S(1)} %get-tuple-element.128), channel_id=1, source_target_pairs={{0,8},{8,16},{16,24},{24,32},{32,40},{40,48},{48,56},{56,64},{64,7... | collective-permute-start | bytes 1544 | tf_op jit(solution)/shard_map/ppermute | solution.py:529
  247.4 4.9 %collective-permute-start.10 = (f32[1,128]{1,0:T(1,128)S(1)}, f32[1,128]{1,0:T(1,128)S(1)}, u32[]{:S(2)}, u32[]{:S(2)}) collective-permute-start(f32[1,128]{1,0:T(1,128)S(1)} %get-tuple-element.129), channel_id=1, source_target_pairs={{8,0},{16,8},{24,16},{32,24},{40,32},{48,40},{56,48},{64,56},{72,6... | collective-permute-start | bytes 1544 | tf_op jit(solution)/shard_map/ppermute | solution.py:529
  249.3 4.3 %collective-permute-start.11 = (f32[1,128]{1,0:T(1,128)S(1)}, f32[1,128]{1,0:T(1,128)S(1)}, u32[]{:S(2)}, u32[]{:S(2)}) collective-permute-start(f32[1,128]{1,0:T(1,128)S(1)} %get-tuple-element.130), channel_id=1, source_target_pairs={{16,0},{24,8},{32,16},{40,24},{48,32},{56,40},{64,48},{72,56},{80,... | collective-permute-start | bytes 1544 | tf_op jit(solution)/shard_map/ppermute | solution.py:529
  (1 other events, 0.7 us)

commit v3 on v2

--- a/solution.py
+++ b/solution.py
@@ -19,6 +19,7 @@
 ENTRIES = 256
 ROWS = 64
 CHUNK = 1024
+PIECES = 2
 F32 = jnp.float32
 BF16 = jnp.bfloat16
 VMEM_LIMIT = 16 << 20
@@ -81,7 +82,7 @@
 def table_pieces(table):
     rest = np.asarray(table, np.float32)
     pieces = []
-    for _ in range(3):
+    for _ in range(PIECES):
         piece = rest.astype(ml_dtypes.bfloat16)
         pieces.append(piece)
         rest = rest - piece.astype(np.float32)
@@ -89,10 +90,12 @@
 
 
 def pieces(value):
-    upper = value.astype(BF16)
-    rest = value - upper.astype(F32)
-    middle = rest.astype(BF16)
-    return [upper, middle, (rest - middle.astype(F32)).astype(BF16)]
+    found = []
+    for left in reversed(range(PIECES)):
+        found.append(value.astype(BF16))
+        if left:
+            value = value - found[-1].astype(F32)
+    return found
 
 
 def row_mask(slots, height):
@@ -122,12 +125,15 @@
 
 
 def take(parts, hot, mask):
-    found = jnp.dot(parts, jnp.concatenate([hot] * 3, axis=0), preferred_element_type=F32)
+    found = jnp.dot(parts, jnp.concatenate([hot] * PIECES, axis=0), preferred_element_type=F32)
     return jnp.sum(jnp.where(mask, found, 0.0), axis=0, keepdims=True)
 
 
 def fold(stacked, height):
-    return stacked[:height] + stacked[height : 2 * height] + stacked[2 * height : 3 * height]
+    result = stacked[:height]
+    for piece in range(1, PIECES):
+        result = result + stacked[piece * height : (piece + 1) * height]
+    return result
 
 
 def total(value):
@@ -203,11 +209,18 @@
         pay_ref[g, 0:1, CHUNK:] = row
 
 
-def setup_scatter(
-    rhs_ref, slot_ref, split_ref, curve_ref, stretch_ref, helm_ref, corner_ref, xvals_ref, xcols_ref, xcount_ref,
-    mass_ref, diag_ref, phi_ref,
-    hot_ref, sums_ref, scale_ref, line_ref, entry_ref, pick_ref, xhot_ref, *out_refs
-):
+def setup_scatter(*refs):
+    sources, refs = refs[:15], refs[15:]
+    slot_ref, split_ref, curve_ref, mass_ref, phi_ref, first_ref, second_ref = refs[:7]
+    hot_ref, sums_ref, scale_ref, entry_ref, pick_ref, xhot_ref = refs[7:13]
+    out_refs = refs[13:19]
+    rhs_ref, stretch_ref, helm_ref, corner_ref, xvals_ref, xcols_ref, xcount_ref, diag_ref, sems = refs[19:]
+    targets = (rhs_ref, stretch_ref, helm_ref, corner_ref, xvals_ref, xcols_ref, xcount_ref, diag_ref) + refs[:7]
+    copies = [pltpu.make_async_copy(a, b, sems.at[i]) for i, (a, b) in enumerate(zip(sources, targets))]
+    for copy in copies:
+        copy.start()
+    for copy in copies:
+        copy.wait()
     columns = [column(stretch_ref[d : d + 1, :]) for d in range(3)] + [column(helm_ref[...])]
     scale_ref[...] = jnp.concatenate(columns + columns, axis=1)
     diag = columns[3] * mass_ref[...]
@@ -216,7 +229,6 @@
     live = lax.broadcasted_iota(jnp.int32, (16, 16), 0) < jnp.broadcast_to(xcount_ref[...], (16, 16))
     factor = flatten(jnp.where(live, xvals_ref[...], 0.0))
     cols = flatten(xcols_ref[...].astype(F32))
-    line_ref[...] = factor
     entries = (cols + 0.5).astype(jnp.int32)
     entry_ref[...] = entries
     xhot_ref[...] = lane_hot(entries)
@@ -229,14 +241,15 @@
         [column(list_row(split_ref, curve_ref, t).astype(F32)) for t in range(LISTS)], axis=0
     )
     lists = (lists + 0.5).astype(jnp.int32)
-    acc = jnp.zeros((9 * HI, LO), F32)
-    weights = jnp.zeros((3 * ELEMS, LISTS * LO), F32)
+    acc = jnp.zeros(((1 + 2 * PIECES) * HI, LO), F32)
+    weights = jnp.zeros((PIECES * ELEMS, LISTS * LO), F32)
     for e in range(ELEMS):
         slots = slot_ref[e : e + 1, :]
         hot = lane_hot(slots)
         hot_ref[:, e * POINTS : (e + 1) * POINTS] = hot
         mask = row_mask(slots, HI)
-        left = spread([jnp.ones((1, POINTS), F32), diag[e : e + 1, :], rhs_ref[e : e + 1, :]], mask)
+        left = spread([diag[e : e + 1, :], rhs_ref[e : e + 1, :]], mask)
+        left = jnp.concatenate([jnp.where(mask, 1.0, 0.0).astype(BF16), left], axis=0)
         acc = acc + put(left, hot)
         unknown = lax.broadcasted_iota(jnp.int32, (ELEMS, 8), 0).astype(F32)
         vertex = jnp.where(jnp.abs(corner[e : e + 1, :] - unknown) < 0.5, 1.0, 0.0)
@@ -247,7 +260,8 @@
     weights = fold(weights, ELEMS)
     tables = []
     for field in range(3):
-        table = fold(acc[3 * HI * field : 3 * HI * (field + 1)], HI)
+        first = HI + PIECES * HI * (field - 1)
+        table = fold(acc[first : first + PIECES * HI], HI) if field else acc[:HI]
         sums_ref[field] = table
         tables.append(table_parts(table))
     for t in range(LISTS):
@@ -263,7 +277,7 @@
 
 
 def incoming_table(split_ref, curve_ref, hot_ref, rows):
-    acc = jnp.zeros((3 * HI, LO), F32)
+    acc = jnp.zeros((PIECES * HI, LO), F32)
     for t in range(LISTS):
         mask = row_mask(list_row(split_ref, curve_ref, t), HI)
         acc = acc + put(spread([rows[t]], mask), list_hot(hot_ref, t))
@@ -304,9 +318,7 @@
     def product(parts, ref):
         rows = parts[0].shape[0]
         one = jnp.dot(jnp.concatenate(parts, axis=0), ref[0], preferred_element_type=F32)
-        two = jnp.dot(jnp.concatenate(parts[:2], axis=0), ref[1], preferred_element_type=F32)
-        three = jnp.dot(parts[0], ref[2], preferred_element_type=F32)
-        return one[:rows] + (one[rows : 2 * rows] + two[:rows] + (one[2 * rows :] + two[rows:] + three))
+        return one[:rows] + (one[rows:] + jnp.dot(parts[0], ref[1], preferred_element_type=F32))
 
     half = POINTS // 2
     parts = pieces(u)
@@ -319,7 +331,7 @@
 
 
 def scatter_points(field_ref, slot_ref, hot_ref):
-    acc = jnp.zeros((3 * HI, LO), F32)
+    acc = jnp.zeros((PIECES * HI, LO), F32)
     for e in range(ELEMS):
         left = spread([field_ref[e : e + 1, :]], row_mask(slot_ref[e : e + 1, :], HI))
         acc = acc + put(left, point_hot(hot_ref, e))
@@ -341,6 +353,17 @@
 
 def halo_rows(shalo_ref, chalo_ref):
     return [shalo_ref[t : t + 1, :] for t in range(2)] + [chalo_ref[t : t + 1, :] for t in range(4)]
+
+
+def coarse_shift(image, earlier):
+    factors = []
+    for other in earlier:
+        size = total(other * other)
+        fits = size > 1e-30
+        factors.append(jnp.where(fits, total(image * other) / jnp.where(fits, size, 1.0), 0.0))
+    for factor, other in zip(factors, earlier):
+        image = image - factor * other
+    return factors, image
 
 
 def krylov_step(index, last, *refs):
@@ -358,6 +381,8 @@
     else:
         weight_ref, sums_ref = refs[:2]
         refs = refs[2:]
+        olds, refs = refs[: 2 * index], refs[2 * index :]
+        base_refs, coarse_refs = olds[:index], olds[index:]
     base_ref, newnorm_ref, newsums_ref = refs[:3]
     refs = refs[3:]
     if index == 0:
@@ -377,12 +402,22 @@
         for r in range(8):
             image_ref[8 * g + r : 8 * g + r + 1, :] = gathered_ref[g, 0:1, r * LO : (r + 1) * LO]
     image = image_ref[...]
+    correction = coarse_correction(image, phi_ref, pick_ref, entry_ref[...], xhot_ref[...])
+    base = force * dinv_ref[...] + correction
+    if index:
+        factors, image = coarse_shift(image, [ref[...] for ref in coarse_refs])
+        for factor, ref in zip(factors, base_refs):
+            base = base - factor * ref[...]
+    else:
+        factors = []
     size = 1.0 + jnp.sqrt(total(image * image))
-    lane = lax.broadcasted_iota(jnp.int32, (1, LO), 1)
-    newnorm_ref[...] = jnp.where(lane == index, size, norm_ref[...]) if index else jnp.broadcast_to(size, (1, LO))
-    correction = coarse_correction(image, phi_ref, pick_ref, entry_ref[...], xhot_ref[...])
-    base = (force * dinv_ref[...] + correction) * (1.0 / size)
+    base = base * (1.0 / size)
     base_ref[...] = base
+    if not last:
+        coarse_ref, *refs = refs
+        coarse_ref[...] = image * (1.0 / size)
+    newnorm_ref[...] = norm_ref[...]
+    newnorm_ref[index : index + 1, :] = place(factors + [size])
     field_ref[...] = operator(base, scale_ref, mass_ref, first_ref, second_ref)
     table = scatter_points(field_ref, slot_ref, hot_ref)
     newsums_ref[...] = table
@@ -466,7 +501,7 @@
         sums[g % 8] = sums[g % 8] + got_ref[g]
     row = ((sums[0] + sums[1]) + (sums[2] + sums[3])) + ((sums[4] + sums[5]) + (sums[6] + sums[7]))
     table = [[row[:, 4 * i + j : 4 * i + j + 1] for j in range(4)] for i in range(5)]
-    norms = [norm_ref[0:1, j : j + 1] for j in range(4)]
+    relation = [[norm_ref[i : i + 1, j : j + 1] for j in range(i + 1)] for i in range(4)]
 
     def pair(left, right):
         acc = None
@@ -485,7 +520,7 @@
         return -factor * other if value is None else value - factor * other
 
     residual = [jnp.ones((1, 1), F32)] + [None] * 4
-    precond = [norms[0]] + [None] * 3
+    precond = [relation[0][0]] + [None] * 3
     direction = list(precond)
     solution = [None] * 4
     rz = pair(residual, precond)
@@ -495,7 +530,11 @@
         solution = [less(value, -alpha, other) for value, other in zip(solution, direction)]
         residual = [less(value, alpha, other) for value, other in zip(residual, moved)]
         if k < ITERS - 1:
-            shifted = [None] + [None if d is None else d * norms[j + 1] for j, d in enumerate(direction[:3])]
+            shifted = [None] * 4
+            for j, d in enumerate(direction[:3]):
+                if d is not None:
+                    for i, factor in enumerate(relation[j + 1]):
+                        shifted[i] = less(shifted[i], -d, factor)
             precond = [less(value, alpha, other) for value, other in zip(precond, shifted)]
             rz_next = pair(residual, precond)
             beta = rz_next / rz
@@ -511,12 +550,12 @@
     residual_ref[...] = result
 
 
-def run(body, name, args, outs, scratch=()):
+def run(body, name, args, outs, scratch=(), where=pltpu.VMEM):
     return pl.pallas_call(
         body,
         name=name,
         out_shape=[jax.ShapeDtypeStruct(shape, dtype) for shape, dtype in outs],
-        in_specs=[pl.BlockSpec(memory_space=pltpu.VMEM) for _ in args],
+        in_specs=[pl.BlockSpec(memory_space=where) for _ in args],
         out_specs=[pl.BlockSpec(memory_space=pltpu.VMEM) for _ in outs],
         scratch_shapes=list(scratch),
         compiler_params=pltpu.CompilerParams(vmem_limit_bytes=VMEM_LIMIT),
@@ -564,14 +603,17 @@
     payload = [((8, 1, CHUNK + LO), F32), ((4, LO), F32)]
     entry = jnp.int32
 
-    hot, sums3, scale, _, entries, pick, xhot, *sent = run(
-        setup_scatter,
-        "setup_scatter",
-        (rhs_load, local_slot, share_split, share_curve, stretch, helm_shift.reshape(1, -1), coarse_slot, x_vals,
-         x_cols, x_count.reshape(1, -1), mass, diags, phi),
-        [((LO, WIDE + LISTS * LO), BF16), ((3, HI, LO), F32), ((ELEMS, 8), F32), ((1, ENTRIES), F32),
-         ((1, ENTRIES), entry), ((8, ELEMS, ENTRIES), F32), ((LO, ENTRIES), BF16)] + [((24, LO), F32)] * LISTS,
-    )
+    sources = (rhs_load, stretch, helm_shift.reshape(1, -1), coarse_slot, x_vals, x_cols, x_count.reshape(1, -1), diags,
+               local_slot, share_split, share_curve, mass, phi, first, second)
+    kept = [(array.shape, array.dtype) for array in sources[8:]]
+    outs = kept + [
+        ((LO, WIDE + LISTS * LO), BF16), ((3, HI, LO), F32), ((ELEMS, 8), F32), ((1, ENTRIES), entry),
+        ((8, ELEMS, ENTRIES), F32), ((LO, ENTRIES), BF16),
+    ] + [((24, LO), F32)] * LISTS
+    scratch = [pltpu.VMEM(array.shape, array.dtype) for array in sources[:8]]
+    scratch.append(pltpu.SemaphoreType.DMA((len(sources),)))
+    (local_slot, share_split, share_curve, mass, phi, first, second, hot, sums3, scale, entries, pick, xhot,
+     *sent) = run(setup_scatter, "setup_scatter", tuple(pltpu.with_memory_space_constraint(a, pltpu.HBM) for a in sources), outs, scratch, pltpu.HBM)
     arrived = exchange(sent)
     shape = (local_slot, share_split, share_curve, hot)
     minv, dinv, right, nline, nentry, nhot, pay, rows = run(
@@ -583,13 +625,14 @@
     )
     common = (*shape, scale, mass, first, second, phi, pick, entries, xhot, nline, nentry, nhot, minv, dinv)
     scratch = [pltpu.VMEM((ROWS, LO), F32), pltpu.VMEM((ELEMS, POINTS), F32)]
-    norm = jnp.ones((1, LO), F32)
-    bases, forces = [], []
+    norm = jnp.ones((8, LO), F32)
+    bases, forces, coarses = [], [], []
     for index in range(ITERS):
         last = index == ITERS - 1
         gathered, shalo, chalo = reduce_image(pay, rows)
-        own = (right, *arrived) if index == 0 else (weight, sums)
-        outs = [field, line, table] + [((LISTS, ELEMS, LO), F32) if index == 0 else field]
+        own = (right, *arrived) if index == 0 else (weight, sums, *bases, *coarses)
+        outs = [field, ((8, LO), F32), table] + [((LISTS, ELEMS, LO), F32) if index == 0 else field]
+        outs += [] if last else [((ROWS, LO), F32)]
         base, norm, sums, extra, *rest = run(
             functools.partial(krylov_step, index, last),
             f"krylov_step{index}",
@@ -603,7 +646,8 @@
         else:
             forces.append(extra)
         if not last:
-            pay, rows = rest
+            coarse, pay, rows = rest
+            coarses.append(coarse)
     devices = lax.axis_size("curve") * lax.axis_size("split")
     force, pay = run(
         gram,

time: 291 us -> 276 us (0.948)
  local copies, waits for them, and re-layouts: 10.7 us -> 0.01 us
  Pallas kernels: 34 us -> 30.2 us
    unnamed x42 -> x0, local copies, waits for them, and re-layouts: 10.7 us -> none
    pallas_call x16, Pallas kernels: 34 us -> 30.2 us  [run(): pl.pallas_call(body, name=name, out_shape=[jax.ShapeDtypeStruct(shape, dt...]
where the time goes in v3:
time: 276 us
  blocking collectives  209 us (76%)
  Pallas kernels  30.2 us (11%)
  starting transfers between devices  29.9 us (11%)
  waiting for transfers between devices  6.08 us (2%)
    all_to_all x4, blocking collectives, reduce_image(): got = lax.all_to_all(pay, 'curve', 0, 0)  94.2 us
    all_to_all x4, blocking collectives, reduce_image(): got = lax.all_to_all(pay, 'split', 0, 0)  43.8 us
    all_to_all x4, blocking collectives, reduce_image(): return (lax.all_to_all(pay, 'split', 0, 0), shalo, chalo)  36.9 us
    all_to_all x1, blocking collectives, local(): got = lax.all_to_all(pay, ('curve', 'split'), 0, 0)  33.6 us
    pallas_call x16, Pallas kernels, run(): pl.pallas_call(body, name=name, out_shape=[jax.ShapeDtypeStruct(shape, dt...  30.2 us
    ppermute x12, starting transfers between devices, shift(): return lax.ppermute(block, axis, route)  29.9 us
    ppermute x12, waiting for transfers between devices, shift(): return lax.ppermute(block, axis, route)  6.08 us
  transfers between devices with their start and end apart: 12, of which 4 were waited for; matrix products, arithmetic and copies ran while one was open for 0% of the time, Pallas kernels for 0%

profile of v3, /device:TPU:1, one launch (start us, length us, event | category | flops | bytes accessed | tf_op | source)
XLA Modules:
  0.0 275.6 jit_solution(11247527191910394103)
XLA Ops:
  0.6 8.5 %setup_scatter.1 = (s32[16,512]{1,0:T(8,128)S(1)}, s32[1,1,2,128]{3,2,1,0:T(2,128)S(1)}, s32[1,1,4,128]{3,2,1,0:T(4,128)S(1)}, f32[1,512]{1,0:T(1,128)S(1)}, f32...) custom-call(f32[16,512]{1,0:T(8,128)} %refs_0_.1, ...), custom_call_target="tpu_custom_call" | custom-call | tf_op jit(solution)/shard_map/setup_scatter/pallas_call | solution.py:554
  9.1 4.0 %collective-permute-start = (f32[24,128]{1,0:T(8,128)S(1)}, f32[24,128]{1,0:T(8,128)S(1)}, u32[]{:S(2)}, u32[]{:S(2)}) collective-permute-start(f32[24,128]{1,0:T(8,128)S(1)} %get-tuple-element.91), channel_id=1, source_target_pairs={{0,1},{1,2},{2,3},{3,4},{4,5},{5,6},{6,7},{8,9},{9,10},{10,11},{11... | collective-permute-start | bytes 36872 | tf_op jit(solution)/shard_map/ppermute | solution.py:568
  14.5 3.1 %collective-permute-start.2 = (f32[24,128]{1,0:T(8,128)S(1)}, f32[24,128]{1,0:T(8,128)S(1)}, u32[]{:S(2)}, u32[]{:S(2)}) collective-permute-start(f32[24,128]{1,0:T(8,128)S(1)} %get-tuple-element.93), channel_id=1, source_target_pairs={{0,16},{8,24},{16,32},{24,40},{32,48},{40,56},{48,64},{56,72},{64,... | collective-permute-start | bytes 36872 | tf_op jit(solution)/shard_map/ppermute | solution.py:568
  17.6 4.2 %collective-permute-start.3 = (f32[24,128]{1,0:T(8,128)S(1)}, f32[24,128]{1,0:T(8,128)S(1)}, u32[]{:S(2)}, u32[]{:S(2)}) collective-permute-start(f32[24,128]{1,0:T(8,128)S(1)} %get-tuple-element.94), channel_id=1, source_target_pairs={{0,8},{8,16},{16,24},{24,32},{32,40},{40,48},{48,56},{56,64},{64,7... | collective-permute-start | bytes 36872 | tf_op jit(solution)/shard_map/ppermute | solution.py:568
  21.9 1.9 collective-permute-start.4
  25.1 1.7 collective-permute-done.4.refs_4_.refs_26_
  26.9 1.4 collective-permute-done.5.refs_5_.refs_27_
  28.2 3.1 %setup_gather.1 = (f32[16,512]{1,0:T(8,128)S(1)}, f32[16,512]{1,0:T(8,128)S(1)}, f32[16,512]{1,0:T(8,128)S(1)}, f32[6,256]{1,0:T(8,128)S(1)}, s32[6,256]{1,0:T(8...) custom-call(s32[16,512]{1,0:T(8,128)S(1)} %get-tuple-element.78.slot_ref.refs_0_, ...), custom_call_target="tpu_custom_call" | custom-call | tf_op jit(solution)/shard_map/setup_gather/pallas_call | solution.py:554
  31.4 15.9 %all_to_all.65.got_ref = f32[8,1,1152]{2,1,0:T(1,128)S(1)} all-to-all(f32[8,1,1152]{2,1,0:T(1,128)S(1)} %get-tuple-element.102), channel_id=1, replica_groups=mesh['curve'=64,'split'=8] {'split'}, dimensions={0} | all-to-all | bytes 73728 | tf_op jit(solution)/shard_map/all_to_all | solution.py:584
  47.3 32.0 %all_to_all.66.got_ref = f32[64,1,1152]{2,1,0:T(1,128)S(1)} all-to-all(f32[64,1,1152]{2,1,0:T(1,128)S(1)} %get-tuple-element.104), channel_id=1, replica_groups=mesh['curve'=64,'split'=8] {'curve'}, dimensions={0} | all-to-all | bytes 589824 | tf_op jit(solution)/shard_map/all_to_all | solution.py:588
  79.3 9.2 %all_to_all.67.refs_18_ = f32[8,1,1024]{2,1,0:T(1,128)S(1)} all-to-all(f32[8,1,1024]{2,1,0:T(1,128)S(1)} %get-tuple-element.105), channel_id=1, replica_groups=mesh['curve'=64,'split'=8] {'split'}, dimensions={0} | all-to-all | bytes 65536 | tf_op jit(solution)/shard_map/all_to_all | solution.py:590
  88.6 3.6 %krylov_step0.1 = (f32[16,512]{1,0:T(8,128)S(1)}, f32[8,128]{1,0:T(8,128)S(1)}, f32[48,128]{1,0:T(8,128)S(1)}, f32[6,16,128]{2,1,0:T(8,128)S(1)}, f32[64,128]{1,...) custom-call(s32[16,512]{1,0:T(8,128)S(1)} %get-tuple-element.78.slot_ref.refs_0_, ...), custom_call_target="tpu_custom_call" | custom-call | tf_op jit(solution)/shard_map/krylov_step0/pallas_call | solution.py:554
  92.3 9.3 %all_to_all.68.got_ref = f32[8,1,1152]{2,1,0:T(1,128)S(1)} all-to-all(f32[8,1,1152]{2,1,0:T(1,128)S(1)} %get-tuple-element.110), channel_id=1, replica_groups=mesh['curve'=64,'split'=8] {'split'}, dimensions={0} | all-to-all | bytes 73728 | tf_op jit(solution)/shard_map/all_to_all | solution.py:584
  101.6 20.8 %all_to_all.69.got_ref = f32[64,1,1152]{2,1,0:T(1,128)S(1)} all-to-all(f32[64,1,1152]{2,1,0:T(1,128)S(1)} %get-tuple-element.112), channel_id=1, replica_groups=mesh['curve'=64,'split'=8] {'curve'}, dimensions={0} | all-to-all | bytes 589824 | tf_op jit(solution)/shard_map/all_to_all | solution.py:588
  122.5 9.2 %all_to_all.70.refs_18_ = f32[8,1,1024]{2,1,0:T(1,128)S(1)} all-to-all(f32[8,1,1024]{2,1,0:T(1,128)S(1)} %get-tuple-element.113), channel_id=1, replica_groups=mesh['curve'=64,'split'=8] {'split'}, dimensions={0} | all-to-all | bytes 65536 | tf_op jit(solution)/shard_map/all_to_all | solution.py:590
  131.7 4.5 %krylov_step1.1 = (f32[16,512]{1,0:T(8,128)S(1)}, f32[8,128]{1,0:T(8,128)S(1)}, f32[48,128]{1,0:T(8,128)S(1)}, f32[16,512]{1,0:T(8,128)S(1)}, f32[64,128]{1,0:T(...) custom-call(s32[16,512]{1,0:T(8,128)S(1)} %get-tuple-element.78.slot_ref.refs_0_, ...), custom_call_target="tpu_custom_call" | custom-call | tf_op jit(solution)/shard_map/krylov_step1/pallas_call | solution.py:554
  136.2 9.3 %all_to_all.71.got_ref = f32[8,1,1152]{2,1,0:T(1,128)S(1)} all-to-all(f32[8,1,1152]{2,1,0:T(1,128)S(1)} %get-tuple-element.121), channel_id=1, replica_groups=mesh['curve'=64,'split'=8] {'split'}, dimensions={0} | all-to-all | bytes 73728 | tf_op jit(solution)/shard_map/all_to_all | solution.py:584
  145.6 20.7 %all_to_all.72.got_ref = f32[64,1,1152]{2,1,0:T(1,128)S(1)} all-to-all(f32[64,1,1152]{2,1,0:T(1,128)S(1)} %get-tuple-element.123), channel_id=1, replica_groups=mesh['curve'=64,'split'=8] {'curve'}, dimensions={0} | all-to-all | bytes 589824 | tf_op jit(solution)/shard_map/all_to_all | solution.py:588
  166.3 9.2 %all_to_all.73.refs_18_ = f32[8,1,1024]{2,1,0:T(1,128)S(1)} all-to-all(f32[8,1,1024]{2,1,0:T(1,128)S(1)} %get-tuple-element.124), channel_id=1, replica_groups=mesh['curve'=64,'split'=8] {'split'}, dimensions={0} | all-to-all | bytes 65536 | tf_op jit(solution)/shard_map/all_to_all | solution.py:590
  175.5 4.5 %krylov_step2.1 = (f32[16,512]{1,0:T(8,128)S(1)}, f32[8,128]{1,0:T(8,128)S(1)}, f32[48,128]{1,0:T(8,128)S(1)}, f32[16,512]{1,0:T(8,128)S(1)}, f32[64,128]{1,0:T(...) custom-call(s32[16,512]{1,0:T(8,128)S(1)} %get-tuple-element.78.slot_ref.refs_0_, ...), custom_call_target="tpu_custom_call" | custom-call | tf_op jit(solution)/shard_map/krylov_step2/pallas_call | solution.py:554
  180.0 9.3 %all_to_all.74.got_ref = f32[8,1,1152]{2,1,0:T(1,128)S(1)} all-to-all(f32[8,1,1152]{2,1,0:T(1,128)S(1)} %get-tuple-element.131), channel_id=1, replica_groups=mesh['curve'=64,'split'=8] {'split'}, dimensions={0} | all-to-all | bytes 73728 | tf_op jit(solution)/shard_map/all_to_all | solution.py:584
  189.3 20.7 %all_to_all.75.got_ref = f32[64,1,1152]{2,1,0:T(1,128)S(1)} all-to-all(f32[64,1,1152]{2,1,0:T(1,128)S(1)} %get-tuple-element.133), channel_id=1, replica_groups=mesh['curve'=64,'split'=8] {'curve'}, dimensions={0} | all-to-all | bytes 589824 | tf_op jit(solution)/shard_map/all_to_all | solution.py:588
  210.0 9.2 %all_to_all.76.refs_18_ = f32[8,1,1024]{2,1,0:T(1,128)S(1)} all-to-all(f32[8,1,1024]{2,1,0:T(1,128)S(1)} %get-tuple-element.134), channel_id=1, replica_groups=mesh['curve'=64,'split'=8] {'split'}, dimensions={0} | all-to-all | bytes 65536 | tf_op jit(solution)/shard_map/all_to_all | solution.py:590
  219.2 3.3 %krylov_step3.1 = (f32[16,512]{1,0:T(8,128)S(1)}, f32[8,128]{1,0:T(8,128)S(1)}, f32[48,128]{1,0:T(8,128)S(1)}, f32[16,512]{1,0:T(8,128)S(1)}, f32[1,128]{1,0:T(1...) custom-call(s32[16,512]{1,0:T(8,128)S(1)} %get-tuple-element.78.slot, ...), custom_call_target="tpu_custom_call" | custom-call | tf_op jit(solution)/shard_map/krylov_step3/pallas_call | solution.py:554
  222.5 2.2 collective-permute-start.6
  226.0 2.4 collective-permute-start.8
  228.5 4.8 %collective-permute-start.9 = (f32[1,128]{1,0:T(1,128)S(1)}, f32[1,128]{1,0:T(1,128)S(1)}, u32[]{:S(2)}, u32[]{:S(2)}) collective-permute-start(f32[1,128]{1,0:T(1,128)S(1)} %get-tuple-element.148), channel_id=1, source_target_pairs={{0,8},{8,16},{16,24},{24,32},{32,40},{40,48},{48,56},{56,64},{64,7... | collective-permute-start | bytes 1544 | tf_op jit(solution)/shard_map/ppermute | solution.py:568
  233.3 1.9 collective-permute-start.10
  236.6 1.6 collective-permute-done.10.refs_18_
  238.2 1.4 collective-permute-done.11.refs_19_
  239.5 1.5 gram.1
  241.0 33.6 %all_to_all.77.refs_0_ = f32[512,1,128]{2,1,0:T(1,128)S(1)} all-to-all(f32[512,1,128]{2,1,0:T(1,128)S(1)} %get-tuple-element.151), channel_id=1, replica_groups=mesh['curve'=64,'split'=8] {'curve','split'}, dimensions={0} | all-to-all | bytes 524288 | tf_op jit(solution)/shard_map/all_to_all | solution.py:658
  (22 shorter events, 6.4 us)
Async XLA Ops:
  9.1 14.6 %collective-permute-start = (f32[24,128]{1,0:T(8,128)S(1)}, f32[24,128]{1,0:T(8,128)S(1)}, u32[]{:S(2)}, u32[]{:S(2)}) collective-permute-start(f32[24,128]{1,0:T(8,128)S(1)} %get-tuple-element.91), channel_id=1, source_target_pairs={{0,1},{1,2},{2,3},{3,4},{4,5},{5,6},{6,7},{8,9},{9,10},{10,11},{11... | collective-permute-start | bytes 36872 | tf_op jit(solution)/shard_map/ppermute | solution.py:568
  13.2 11.9 %collective-permute-start.1 = (f32[24,128]{1,0:T(8,128)S(1)}, f32[24,128]{1,0:T(8,128)S(1)}, u32[]{:S(2)}, u32[]{:S(2)}) collective-permute-start(f32[24,128]{1,0:T(8,128)S(1)} %get-tuple-element.92), channel_id=1, source_target_pairs={{1,0},{2,1},{3,2},{4,3},{5,4},{6,5},{7,6},{9,8},{10,9},{11,10},{12... | collective-permute-start | bytes 36872 | tf_op jit(solution)/shard_map/ppermute | solution.py:568
  14.5 10.6 %collective-permute-start.2 = (f32[24,128]{1,0:T(8,128)S(1)}, f32[24,128]{1,0:T(8,128)S(1)}, u32[]{:S(2)}, u32[]{:S(2)}) collective-permute-start(f32[24,128]{1,0:T(8,128)S(1)} %get-tuple-element.93), channel_id=1, source_target_pairs={{0,16},{8,24},{16,32},{24,40},{32,48},{40,56},{48,64},{56,72},{64,... | collective-permute-start | bytes 36872 | tf_op jit(solution)/shard_map/ppermute | solution.py:568
  17.6 7.5 %collective-permute-start.3 = (f32[24,128]{1,0:T(8,128)S(1)}, f32[24,128]{1,0:T(8,128)S(1)}, u32[]{:S(2)}, u32[]{:S(2)}) collective-permute-start(f32[24,128]{1,0:T(8,128)S(1)} %get-tuple-element.94), channel_id=1, source_target_pairs={{0,8},{8,16},{16,24},{24,32},{32,40},{40,48},{48,56},{56,64},{64,7... | collective-permute-start | bytes 36872 | tf_op jit(solution)/shard_map/ppermute | solution.py:568
  21.9 5.0 %collective-permute-start.4 = (f32[24,128]{1,0:T(8,128)S(1)}, f32[24,128]{1,0:T(8,128)S(1)}, u32[]{:S(2)}, u32[]{:S(2)}) collective-permute-start(f32[24,128]{1,0:T(8,128)S(1)} %get-tuple-element.95), channel_id=1, source_target_pairs={{8,0},{16,8},{24,16},{32,24},{40,32},{48,40},{56,48},{64,56},{72,6... | collective-permute-start | bytes 36872 | tf_op jit(solution)/shard_map/ppermute | solution.py:568
  23.8 4.4 %collective-permute-start.5 = (f32[24,128]{1,0:T(8,128)S(1)}, f32[24,128]{1,0:T(8,128)S(1)}, u32[]{:S(2)}, u32[]{:S(2)}) collective-permute-start(f32[24,128]{1,0:T(8,128)S(1)} %get-tuple-element.96), channel_id=1, source_target_pairs={{16,0},{24,8},{32,16},{40,24},{48,32},{56,40},{64,48},{72,56},{80,... | collective-permute-start | bytes 36872 | tf_op jit(solution)/shard_map/ppermute | solution.py:568
  222.5 12.8 %collective-permute-start.6 = (f32[1,128]{1,0:T(1,128)S(1)}, f32[1,128]{1,0:T(1,128)S(1)}, u32[]{:S(2)}, u32[]{:S(2)}) collective-permute-start(f32[1,128]{1,0:T(1,128)S(1)} %get-tuple-element.145), channel_id=1, source_target_pairs={{0,1},{1,2},{2,3},{3,4},{4,5},{5,6},{6,7},{8,9},{9,10},{10,11},{11... | collective-permute-start | bytes 1544 | tf_op jit(solution)/shard_map/ppermute | solution.py:568
  224.7 11.8 %collective-permute-start.7 = (f32[1,128]{1,0:T(1,128)S(1)}, f32[1,128]{1,0:T(1,128)S(1)}, u32[]{:S(2)}, u32[]{:S(2)}) collective-permute-start(f32[1,128]{1,0:T(1,128)S(1)} %get-tuple-element.146), channel_id=1, source_target_pairs={{1,0},{2,1},{3,2},{4,3},{5,4},{6,5},{7,6},{9,8},{10,9},{11,10},{12... | collective-permute-start | bytes 1544 | tf_op jit(solution)/shard_map/ppermute | solution.py:568
  226.0 10.5 %collective-permute-start.8 = (f32[1,128]{1,0:T(1,128)S(1)}, f32[1,128]{1,0:T(1,128)S(1)}, u32[]{:S(2)}, u32[]{:S(2)}) collective-permute-start(f32[1,128]{1,0:T(1,128)S(1)} %get-tuple-element.147), channel_id=1, source_target_pairs={{0,16},{8,24},{16,32},{24,40},{32,48},{40,56},{48,64},{56,72},{64,... | collective-permute-start | bytes 1544 | tf_op jit(solution)/shard_map/ppermute | solution.py:568
  228.5 8.1 %collective-permute-start.9 = (f32[1,128]{1,0:T(1,128)S(1)}, f32[1,128]{1,0:T(1,128)S(1)}, u32[]{:S(2)}, u32[]{:S(2)}) collective-permute-start(f32[1,128]{1,0:T(1,128)S(1)} %get-tuple-element.148), channel_id=1, source_target_pairs={{0,8},{8,16},{16,24},{24,32},{32,40},{40,48},{48,56},{56,64},{64,7... | collective-permute-start | bytes 1544 | tf_op jit(solution)/shard_map/ppermute | solution.py:568
  233.3 4.9 %collective-permute-start.10 = (f32[1,128]{1,0:T(1,128)S(1)}, f32[1,128]{1,0:T(1,128)S(1)}, u32[]{:S(2)}, u32[]{:S(2)}) collective-permute-start(f32[1,128]{1,0:T(1,128)S(1)} %get-tuple-element.149), channel_id=1, source_target_pairs={{8,0},{16,8},{24,16},{32,24},{40,32},{48,40},{56,48},{64,56},{72,6... | collective-permute-start | bytes 1544 | tf_op jit(solution)/shard_map/ppermute | solution.py:568
  235.3 4.3 %collective-permute-start.11 = (f32[1,128]{1,0:T(1,128)S(1)}, f32[1,128]{1,0:T(1,128)S(1)}, u32[]{:S(2)}, u32[]{:S(2)}) collective-permute-start(f32[1,128]{1,0:T(1,128)S(1)} %get-tuple-element.150), channel_id=1, source_target_pairs={{16,0},{24,8},{32,16},{40,24},{48,32},{56,40},{64,48},{72,56},{80,... | collective-permute-start | bytes 1544 | tf_op jit(solution)/shard_map/ppermute | solution.py:568

commit v4 on v3

--- a/solution.py
+++ b/solution.py
@@ -18,7 +18,8 @@
 WIDE = ELEMS * POINTS
 ENTRIES = 256
 ROWS = 64
-CHUNK = 1024
+GROUP = 8
+CHUNK = ROWS * LO // GROUP
 PIECES = 2
 F32 = jnp.float32
 BF16 = jnp.bfloat16
@@ -200,13 +201,25 @@
     return fold(put(spread([line], row_mask(cols, ROWS)), hot), ROWS)
 
 
-def write_payload(pay_ref, image, rows):
-    here = lax.axis_index("split")
-    for g in range(8):
+def place_in_curve():
+    here = lax.axis_index("curve")
+    return lax.div(here, GROUP), lax.rem(here, GROUP)
+
+
+def kept_row(fits, row):
+    return jnp.where(fits, row, jnp.zeros_like(row))
+
+
+def write_payload(pay_ref, rows_ref, image, rows):
+    inner = place_in_curve()[1]
+    for g in range(GROUP):
         for r in range(8):
             pay_ref[g, 0:1, r * LO : (r + 1) * LO] = image[8 * g + r : 8 * g + r + 1, :]
-        row = jnp.where(here == g + 1, rows[0], jnp.where(here == g - 1, rows[1], jnp.zeros((1, LO), F32)))
+        row = jnp.zeros((1, LO), F32)
+        for t in range(2, LISTS):
+            row = jnp.where(lax.rem(inner + WAYS[t][1] + GROUP, GROUP) == g, rows[t], row)
         pay_ref[g, 0:1, CHUNK:] = row
+    rows_ref[...] = jnp.concatenate(rows[:2], axis=0)
 
 
 def setup_scatter(*refs):
@@ -271,9 +284,7 @@
         mask = row_mask(slots, HI)
         rows = [take(tables[field], hot, mask) for field in range(3)]
         rows += [cols[:, :LO], cols[:, LO:], factor[:, :LO], factor[:, LO:], jnp.zeros((1, LO), F32)]
-        for r in range(8):
-            out_refs[t][r : r + 1, :] = rows[r]
-        out_refs[t][8:24, :] = weights[:, t * LO : (t + 1) * LO]
+        out_refs[t][...] = jnp.concatenate(rows + [weights[:, t * LO : (t + 1) * LO]], axis=0)
 
 
 def incoming_table(split_ref, curve_ref, hot_ref, rows):
@@ -285,11 +296,11 @@
 
 
 def setup_gather(slot_ref, split_ref, curve_ref, hot_ref, sums_ref, phi_ref, pick_ref, entry_ref, xhot_ref, *refs):
-    in_refs = refs[:LISTS]
-    minv_ref, dinv_ref, right_ref, nline_ref, nentry_ref, nhot_ref, pay_ref, rows_ref = refs[LISTS:]
+    blocks = refs[:LISTS]
+    minv_ref, dinv_ref, right_ref, nline_ref, nentry_ref, nhot_ref, weight_ref, pay_ref, rows_ref = refs[LISTS:]
     tables = [
         table_parts(
-            sums_ref[field] + incoming_table(split_ref, curve_ref, hot_ref, [ref[field : field + 1, :] for ref in in_refs])
+            sums_ref[field] + incoming_table(split_ref, curve_ref, hot_ref, [block[field : field + 1, :] for block in blocks])
         )
         for field in range(3)
     ]
@@ -303,15 +314,14 @@
     for t in range(LISTS):
         mult = take(tables[0], list_hot(hot_ref, t), row_mask(list_row(split_ref, curve_ref, t), HI))
         rows.append(jnp.where(mult > 0.5, 1.0 / jnp.where(mult > 0.5, mult, 1.0), 0.0))
-        there = jnp.concatenate([in_refs[t][3:4, :], in_refs[t][4:5, :]], axis=1)
+        there = jnp.concatenate([blocks[t][3:4, :], blocks[t][4:5, :]], axis=1)
+        weight_ref[t] = blocks[t][8:24, :]
         entries = (there + 0.5).astype(jnp.int32)
         nentry_ref[t : t + 1, :] = entries
         nhot_ref[:, t * ENTRIES : (t + 1) * ENTRIES] = lane_hot(entries)
-        nline_ref[t : t + 1, :] = jnp.concatenate([in_refs[t][5:6, :], in_refs[t][6:7, :]], axis=1)
-    for t in range(2, LISTS):
-        rows_ref[t - 2 : t - 1, :] = rows[t]
+        nline_ref[t : t + 1, :] = jnp.concatenate([blocks[t][5:6, :], blocks[t][6:7, :]], axis=1)
     line = coarse_line(right_ref[...] * minv_ref[...], phi_ref, pick_ref)
-    write_payload(pay_ref, image_of(line, entry_ref[...], xhot_ref[...]), rows)
+    write_payload(pay_ref, rows_ref, image_of(line, entry_ref[...], xhot_ref[...]), rows)
 
 
 def operator(u, scale_ref, mass_ref, first_ref, second_ref):
@@ -349,10 +359,6 @@
     return [
         take(parts, list_hot(hot_ref, t), row_mask(list_row(split_ref, curve_ref, t), HI)) for t in range(LISTS)
     ]
-
-
-def halo_rows(shalo_ref, chalo_ref):
-    return [shalo_ref[t : t + 1, :] for t in range(2)] + [chalo_ref[t : t + 1, :] for t in range(4)]
 
 
 def coarse_shift(image, earlier):
@@ -369,14 +375,14 @@
 def krylov_step(index, last, *refs):
     (slot_ref, split_ref, curve_ref, hot_ref, scale_ref, mass_ref, first_ref, second_ref, phi_ref, pick_ref,
      entry_ref, xhot_ref, nline_ref, nentry_ref, nhot_ref, minv_ref, dinv_ref, norm_ref, gathered_ref,
-     shalo_ref, chalo_ref) = refs[:21]
-    refs = refs[21:]
+     halo_ref) = refs[:20]
+    refs = refs[20:]
     image_ref, field_ref = refs[-2:]
     refs = refs[:-2]
-    rows = halo_rows(shalo_ref, chalo_ref)
+    rows = [halo_ref[t : t + 1, :] for t in range(LISTS)]
     if index == 0:
-        right_ref, *sent_refs = refs[:7]
-        refs = refs[7:]
+        right_ref, plain_ref = refs[:2]
+        refs = refs[2:]
         force = right_ref[...]
     else:
         weight_ref, sums_ref = refs[:2]
@@ -389,7 +395,7 @@
         newweight_ref = refs[0]
         refs = refs[1:]
         for t in range(LISTS):
-            newweight_ref[t] = sent_refs[t][8:24, :] * rows[t]
+            newweight_ref[t] = plain_ref[t] * rows[t]
         weight_ref = newweight_ref
     else:
         force_ref = refs[0]
@@ -398,7 +404,7 @@
             sums_ref[...] + incoming_table(split_ref, curve_ref, hot_ref, rows), slot_ref, hot_ref, force_ref
         )
         force = force_ref[...]
-    for g in range(8):
+    for g in range(GROUP):
         for r in range(8):
             image_ref[8 * g + r : 8 * g + r + 1, :] = gathered_ref[g, 0:1, r * LO : (r + 1) * LO]
     image = image_ref[...]
@@ -427,8 +433,6 @@
             refs[t][...] = rows[t]
         return
     pay_ref, rows_ref = refs
-    for t in range(2, LISTS):
-        rows_ref[t - 2 : t - 1, :] = rows[t]
     gather_points(table, slot_ref, hot_ref, field_ref)
     line = coarse_line(field_ref[...] * minv_ref[...], phi_ref, pick_ref)
     image = image_of(line, entry_ref[...], xhot_ref[...])
@@ -437,49 +441,66 @@
         loads = jnp.sum(weight_ref[t] * rows[t], axis=1, keepdims=True)
         line = jnp.sum(jnp.where(owner, loads, 0.0), axis=0, keepdims=True) * nline_ref[t : t + 1, :]
         image = image + image_of(line, nentry_ref[t : t + 1, :], nhot_ref[:, t * ENTRIES : (t + 1) * ENTRIES])
-    write_payload(pay_ref, image, rows)
-
-
-def after_split(got_ref, rows_ref, pay_ref, shalo_ref):
-    here, size = lax.axis_index("split"), got_ref.shape[0]
-    for t, offset in enumerate((-1, 1)):
-        there = here + offset
-        row = got_ref[jnp.clip(there, 0, size - 1), 0:1, CHUNK:]
-        shalo_ref[t : t + 1, :] = jnp.where(jnp.logical_and(there >= 0, there < size), row, jnp.zeros((1, LO), F32))
+    write_payload(pay_ref, rows_ref, image, rows)
+
+
+def sum_chunk(got_ref):
     chunk = got_ref[0, 0:1, :CHUNK]
-    for g in range(1, size):
+    for g in range(1, GROUP):
         chunk = chunk + got_ref[g, 0:1, :CHUNK]
-    wide = jnp.concatenate([chunk, jnp.zeros((1, LO), F32)], axis=1)
-    here, size = lax.axis_index("curve"), pay_ref.shape[0]
-    for g in range(size):
-        pay_ref[g] = wide
-    for t, offset in enumerate((-2, -1, 1, 2)):
-        there = here + offset
-
-        @pl.when(jnp.logical_and(there >= 0, there < size))
-        def _():
-            pay_ref[jnp.clip(there, 0, size - 1), 0:1, CHUNK:] = rows_ref[t : t + 1, :]
-
-
-def after_curve(got_ref, pay_ref, chalo_ref):
-    here, size = lax.axis_index("curve"), got_ref.shape[0]
-    for t, offset in enumerate((-2, -1, 1, 2)):
-        there = here + offset
-        row = got_ref[jnp.clip(there, 0, size - 1), 0:1, CHUNK:]
-        chalo_ref[t : t + 1, :] = jnp.where(jnp.logical_and(there >= 0, there < size), row, jnp.zeros((1, LO), F32))
-    sums = [got_ref[g, 0:1, :CHUNK] for g in range(4)]
-    for g in range(4, size):
-        sums[g % 4] = sums[g % 4] + got_ref[g, 0:1, :CHUNK]
-    chunk = (sums[0] + sums[1]) + (sums[2] + sums[3])
-    for g in range(pay_ref.shape[0]):
+    return chunk
+
+
+def after_inner(got_ref, rows_ref, pay_ref, chalo_ref):
+    inner = place_in_curve()[1]
+    for t in range(2, LISTS):
+        there = lax.rem(inner + WAYS[t][1] + GROUP, GROUP)
+        chalo_ref[t - 2 : t - 1, :] = got_ref[there, 0:1, CHUNK:]
+    chunk = sum_chunk(got_ref)
+    here = lax.axis_index("split")
+    for g in range(GROUP):
+        pay_ref[g, 0:1, :CHUNK] = chunk
+        row = jnp.where(here - 1 == g, rows_ref[0:1, :], kept_row(here + 1 == g, rows_ref[1:2, :]))
+        pay_ref[g, 0:1, CHUNK:] = row
+
+
+def after_split(got_ref, chalo_ref, pay_ref, shalo_ref):
+    here = lax.axis_index("split")
+    for t in range(2):
+        there = here + WAYS[t][1]
+        row = got_ref[jnp.clip(there, 0, GROUP - 1), 0:1, CHUNK:]
+        shalo_ref[t : t + 1, :] = kept_row(jnp.logical_and(there >= 0, there < GROUP), row)
+    chunk = sum_chunk(got_ref)
+    outer = place_in_curve()[0]
+    up = jnp.concatenate([chalo_ref[1:2, :], chalo_ref[0:1, :]], axis=1)
+    down = jnp.concatenate([chalo_ref[2:3, :], chalo_ref[3:4, :]], axis=1)
+    for g in range(GROUP):
+        pay_ref[g, 0:1, :CHUNK] = chunk
+        pay_ref[g, 0:1, CHUNK:] = jnp.where(outer + 1 == g, up, kept_row(outer - 1 == g, down))
+
+
+def after_outer(got_ref, shalo_ref, chalo_ref, pay_ref, halo_ref):
+    chunk = sum_chunk(got_ref)
+    for g in range(GROUP):
         pay_ref[g] = chunk
+    outer, inner = place_in_curve()
+    rows = [shalo_ref[t : t + 1, :] for t in range(2)]
+    for t in range(2, LISTS):
+        offset = WAYS[t][1]
+        beyond = inner + offset >= GROUP if offset > 0 else inner + offset < 0
+        there = outer + (1 if offset > 0 else -1)
+        lane = CHUNK + (abs(offset) - 1) * LO
+        far = got_ref[jnp.clip(there, 0, GROUP - 1), 0:1, lane : lane + LO]
+        far = kept_row(jnp.logical_and(there >= 0, there < GROUP), far)
+        rows.append(jnp.where(beyond, far, chalo_ref[t - 2 : t - 1, :]))
+    halo_ref[...] = jnp.concatenate(rows, axis=0)
 
 
 def gram(*refs):
     slot_ref, split_ref, curve_ref, hot_ref, sums_ref, minv_ref, right_ref = refs[:7]
-    base_refs, force_refs, in_refs = refs[7:11], refs[11:14], refs[14:20]
+    base_refs, force_refs = refs[7:11], refs[11:14]
     last_ref, pay_ref = refs[20:]
-    rows = [ref[...] for ref in in_refs]
+    rows = [ref[...] for ref in refs[14:20]]
     gather_points(
         sums_ref[...] + incoming_table(split_ref, curve_ref, hot_ref, rows), slot_ref, hot_ref, last_ref
     )
@@ -580,14 +601,20 @@
 
 
 def reduce_image(pay, rows):
-    splits, curves = lax.axis_size("split"), lax.axis_size("curve")
+    size = lax.axis_size("curve")
+    near = [list(range(first, first + GROUP)) for first in range(0, size, GROUP)]
+    far = [list(range(first, size, GROUP)) for first in range(GROUP)]
+
+    def frame(count):
+        return ((GROUP, 1, CHUNK + count * LO), F32)
+
+    got = lax.all_to_all(pay, "curve", 0, 0, axis_index_groups=near)
+    pay, chalo = run(after_inner, "after_inner", (got, rows), [frame(1), ((4, LO), F32)])
     got = lax.all_to_all(pay, "split", 0, 0)
-    pay, shalo = run(
-        after_split, "after_split", (got, rows), [((curves, 1, CHUNK + LO), F32), ((2, LO), F32)]
-    )
-    got = lax.all_to_all(pay, "curve", 0, 0)
-    pay, chalo = run(after_curve, "after_curve", (got,), [((splits, 1, CHUNK), F32), ((4, LO), F32)])
-    return lax.all_to_all(pay, "split", 0, 0), shalo, chalo
+    pay, shalo = run(after_split, "after_split", (got, chalo), [frame(2), ((2, LO), F32)])
+    got = lax.all_to_all(pay, "curve", 0, 0, axis_index_groups=far)
+    pay, halo = run(after_outer, "after_outer", (got, shalo, chalo), [frame(0), ((LISTS, LO), F32)])
+    return lax.all_to_all(pay, "curve", 0, 0, axis_index_groups=near), halo
 
 
 def local(rhs_load, stretch, helm_shift, local_slot, share_curve, share_split, coarse_slot, x_vals, x_cols, x_count):
@@ -600,7 +627,9 @@
     field = ((ELEMS, POINTS), F32)
     table = ((HI, LO), F32)
     line = ((1, LO), F32)
-    payload = [((8, 1, CHUNK + LO), F32), ((4, LO), F32)]
+    payload = [((GROUP, 1, CHUNK + LO), F32), ((2, LO), F32)]
+    sent = [((24, LO), F32)] * LISTS
+    sent_last = [line] * LISTS
     entry = jnp.int32
 
     sources = (rhs_load, stretch, helm_shift.reshape(1, -1), coarse_slot, x_vals, x_cols, x_count.reshape(1, -1), diags,
@@ -609,18 +638,19 @@
     outs = kept + [
         ((LO, WIDE + LISTS * LO), BF16), ((3, HI, LO), F32), ((ELEMS, 8), F32), ((1, ENTRIES), entry),
         ((8, ELEMS, ENTRIES), F32), ((LO, ENTRIES), BF16),
-    ] + [((24, LO), F32)] * LISTS
+    ] + sent
     scratch = [pltpu.VMEM(array.shape, array.dtype) for array in sources[:8]]
     scratch.append(pltpu.SemaphoreType.DMA((len(sources),)))
     (local_slot, share_split, share_curve, mass, phi, first, second, hot, sums3, scale, entries, pick, xhot,
-     *sent) = run(setup_scatter, "setup_scatter", tuple(pltpu.with_memory_space_constraint(a, pltpu.HBM) for a in sources), outs, scratch, pltpu.HBM)
-    arrived = exchange(sent)
+     *outgoing) = run(setup_scatter, "setup_scatter", tuple(pltpu.with_memory_space_constraint(a, pltpu.HBM) for a in sources), outs, scratch, pltpu.HBM)
+    arrived = exchange(outgoing)
     shape = (local_slot, share_split, share_curve, hot)
-    minv, dinv, right, nline, nentry, nhot, pay, rows = run(
+    minv, dinv, right, nline, nentry, nhot, plain, pay, rows = run(
         setup_gather,
         "setup_gather",
         (*shape, sums3, phi, pick, entries, xhot, *arrived),
-        [field, field, field, ((LISTS, ENTRIES), F32), ((LISTS, ENTRIES), entry), ((LO, LISTS * ENTRIES), BF16)]
+        [field, field, field, ((LISTS, ENTRIES), F32), ((LISTS, ENTRIES), entry), ((LO, LISTS * ENTRIES), BF16),
+         ((LISTS, ELEMS, LO), F32)]
         + payload,
     )
     common = (*shape, scale, mass, first, second, phi, pick, entries, xhot, nline, nentry, nhot, minv, dinv)
@@ -629,15 +659,15 @@
     bases, forces, coarses = [], [], []
     for index in range(ITERS):
         last = index == ITERS - 1
-        gathered, shalo, chalo = reduce_image(pay, rows)
-        own = (right, *arrived) if index == 0 else (weight, sums, *bases, *coarses)
+        gathered, halo = reduce_image(pay, rows)
+        own = (right, plain) if index == 0 else (weight, sums, *bases, *coarses)
         outs = [field, ((8, LO), F32), table] + [((LISTS, ELEMS, LO), F32) if index == 0 else field]
         outs += [] if last else [((ROWS, LO), F32)]
         base, norm, sums, extra, *rest = run(
             functools.partial(krylov_step, index, last),
             f"krylov_step{index}",
-            (*common, norm, gathered, shalo, chalo, *own),
-            outs + ([line] * LISTS if last else payload),
+            (*common, norm, gathered, halo, *own),
+            outs + (sent_last if last else payload),
             scratch,
         )
         bases.append(base)

time: 276 us -> 265 us (0.960)
  blocking collectives: 209 us -> 199 us
    all_to_all x8 -> x12, blocking collectives: 131 us -> 122 us  [the longest x4 44.2 us: reduce_image(): got = lax.all_to_all(pay, 'curve', 0, 0, axis_index_groups=far)]
    pallas_call x16 -> x20, Pallas kernels: 30.2 us -> 30.2 us  [run(): pl.pallas_call(body, name=name, out_shape=[jax.ShapeDtypeStruct(shape, dt...]
where the time goes in v4:
time: 265 us; the launch traced here: 264 us
  blocking collectives  199 us (75%)
  Pallas kernels  30.2 us (11%)
  starting transfers between devices  28.1 us (11%)
  waiting for transfers between devices  6.08 us (2%)
    all_to_all x4, blocking collectives, reduce_image(): got = lax.all_to_all(pay, 'curve', 0, 0, axis_index_groups=far)  44.2 us
    all_to_all x4, blocking collectives, reduce_image(): got = lax.all_to_all(pay, 'split', 0, 0)  43.7 us
    all_to_all x4, blocking collectives, reduce_image(): return (lax.all_to_all(pay, 'curve', 0, 0, axis_index_groups=near), halo)  41 us
    all_to_all x4, blocking collectives, reduce_image(): got = lax.all_to_all(pay, 'curve', 0, 0, axis_index_groups=near)  36.8 us
    all_to_all x1, blocking collectives, local(): got = lax.all_to_all(pay, ('curve', 'split'), 0, 0)  33.2 us
    pallas_call x20, Pallas kernels, run(): pl.pallas_call(body, name=name, out_shape=[jax.ShapeDtypeStruct(shape, dt...  30.2 us
    ppermute x12, starting transfers between devices, shift(): return lax.ppermute(block, axis, route)  28.1 us
    ppermute x12, waiting for transfers between devices, shift(): return lax.ppermute(block, axis, route)  6.08 us
  transfers between devices with their start and end apart: 12, of which 4 were waited for; matrix products, arithmetic and copies ran while one was open for 0% of the time, Pallas kernels for 0%

profile of v4, /device:TPU:1, one launch (start us, length us, event | category | flops | bytes accessed | tf_op | source)
XLA Modules:
  0.0 264.1 jit_solution(6864469248604188090)
XLA Ops:
  0.6 8.5 %setup_scatter.1 = (s32[16,512]{1,0:T(8,128)S(1)}, s32[1,1,2,128]{3,2,1,0:T(2,128)S(1)}, s32[1,1,4,128]{3,2,1,0:T(4,128)S(1)}, f32[1,512]{1,0:T(1,128)S(1)}, f32...) custom-call(f32[16,512]{1,0:T(8,128)} %refs_0_.1, ...), custom_call_target="tpu_custom_call" | custom-call | tf_op jit(solution)/shard_map/setup_scatter/pallas_call | solution.py:575
  9.1 4.0 %collective-permute-start = (f32[24,128]{1,0:T(8,128)S(1)}, f32[24,128]{1,0:T(8,128)S(1)}, u32[]{:S(2)}, u32[]{:S(2)}) collective-permute-start(f32[24,128]{1,0:T(8,128)S(1)} %get-tuple-element.100), channel_id=1, source_target_pairs={{0,1},{1,2},{2,3},{3,4},{4,5},{5,6},{6,7},{8,9},{9,10},{10,11},{11... | collective-permute-start | bytes 36872 | tf_op jit(solution)/shard_map/ppermute | solution.py:589
  14.5 3.1 %collective-permute-start.2 = (f32[24,128]{1,0:T(8,128)S(1)}, f32[24,128]{1,0:T(8,128)S(1)}, u32[]{:S(2)}, u32[]{:S(2)}) collective-permute-start(f32[24,128]{1,0:T(8,128)S(1)} %get-tuple-element.102), channel_id=1, source_target_pairs={{0,16},{8,24},{16,32},{24,40},{32,48},{40,56},{48,64},{56,72},{64,... | collective-permute-start | bytes 36872 | tf_op jit(solution)/shard_map/ppermute | solution.py:589
  17.6 4.2 %collective-permute-start.3 = (f32[24,128]{1,0:T(8,128)S(1)}, f32[24,128]{1,0:T(8,128)S(1)}, u32[]{:S(2)}, u32[]{:S(2)}) collective-permute-start(f32[24,128]{1,0:T(8,128)S(1)} %get-tuple-element.103), channel_id=1, source_target_pairs={{0,8},{8,16},{16,24},{24,32},{32,40},{40,48},{48,56},{56,64},{64,7... | collective-permute-start | bytes 36872 | tf_op jit(solution)/shard_map/ppermute | solution.py:589
  21.8 1.9 collective-permute-start.4
  25.1 1.7 collective-permute-done.4.refs_4_
  28.2 3.1 %setup_gather.1 = (f32[16,512]{1,0:T(8,128)S(1)}, f32[16,512]{1,0:T(8,128)S(1)}, f32[16,512]{1,0:T(8,128)S(1)}, f32[6,256]{1,0:T(8,128)S(1)}, s32[6,256]{1,0:T(8...) custom-call(s32[16,512]{1,0:T(8,128)S(1)} %get-tuple-element.87.slot, ...), custom_call_target="tpu_custom_call" | custom-call | tf_op jit(solution)/shard_map/setup_gather/pallas_call | solution.py:575
  31.4 13.3 %all_to_all.85.got_ref = f32[8,1,1152]{2,1,0:T(1,128)S(1)} all-to-all(f32[8,1,1152]{2,1,0:T(1,128)S(1)} %get-tuple-element.111), channel_id=1, replica_groups={{0,8,16,24,32,40,48,56},{64,72,80,88,96,104,112,120},{128,136,144,152,1..., dimensions={0} | all-to-all | bytes 73728 | tf_op jit(solution)/shard_map/all_to_all | solution.py:611
  44.7 15.8 %all_to_all.86.got_ref = f32[8,1,1152]{2,1,0:T(1,128)S(1)} all-to-all(f32[8,1,1152]{2,1,0:T(1,128)S(1)} %get-tuple-element.113), channel_id=1, replica_groups=mesh['curve'=64,'split'=8] {'split'}, dimensions={0} | all-to-all | bytes 73728 | tf_op jit(solution)/shard_map/all_to_all | solution.py:613
  60.5 16.2 %all_to_all.87.got_ref = f32[8,1,1280]{2,1,0:T(1,128)S(1)} all-to-all(f32[8,1,1280]{2,1,0:T(1,128)S(1)} %get-tuple-element.115), channel_id=1, replica_groups={{0,64,128,192,256,320,384,448},{8,72,136,200,264,328,392,456},{16,80,14..., dimensions={0} | all-to-all | bytes 81920 | tf_op jit(solution)/shard_map/all_to_all | solution.py:615
  76.7 10.7 %all_to_all.88.refs_18_ = f32[8,1,1024]{2,1,0:T(1,128)S(1)} all-to-all(f32[8,1,1024]{2,1,0:T(1,128)S(1)} %get-tuple-element.117), channel_id=1, replica_groups={{0,8,16,24,32,40,48,56},{64,72,80,88,96,104,112,120},{128,136,144,152,1..., dimensions={0} | all-to-all | bytes 65536 | tf_op jit(solution)/shard_map/all_to_all | solution.py:617
  87.4 3.6 %krylov_step0.1 = (f32[16,512]{1,0:T(8,128)S(1)}, f32[8,128]{1,0:T(8,128)S(1)}, f32[48,128]{1,0:T(8,128)S(1)}, f32[6,16,128]{2,1,0:T(8,128)S(1)}, f32[64,128]{1,...) custom-call(s32[16,512]{1,0:T(8,128)S(1)} %get-tuple-element.87.slot_ref.refs_0_, ...), custom_call_target="tpu_custom_call" | custom-call | tf_op jit(solution)/shard_map/krylov_step0/pallas_call | solution.py:575
  91.0 7.8 %all_to_all.89.got_ref = f32[8,1,1152]{2,1,0:T(1,128)S(1)} all-to-all(f32[8,1,1152]{2,1,0:T(1,128)S(1)} %get-tuple-element.122), channel_id=1, replica_groups={{0,8,16,24,32,40,48,56},{64,72,80,88,96,104,112,120},{128,136,144,152,1..., dimensions={0} | all-to-all | bytes 73728 | tf_op jit(solution)/shard_map/all_to_all | solution.py:611
  98.9 9.3 %all_to_all.90.got_ref = f32[8,1,1152]{2,1,0:T(1,128)S(1)} all-to-all(f32[8,1,1152]{2,1,0:T(1,128)S(1)} %get-tuple-element.124), channel_id=1, replica_groups=mesh['curve'=64,'split'=8] {'split'}, dimensions={0} | all-to-all | bytes 73728 | tf_op jit(solution)/shard_map/all_to_all | solution.py:613
  108.2 9.3 %all_to_all.91.got_ref = f32[8,1,1280]{2,1,0:T(1,128)S(1)} all-to-all(f32[8,1,1280]{2,1,0:T(1,128)S(1)} %get-tuple-element.126), channel_id=1, replica_groups={{0,64,128,192,256,320,384,448},{8,72,136,200,264,328,392,456},{16,80,14..., dimensions={0} | all-to-all | bytes 81920 | tf_op jit(solution)/shard_map/all_to_all | solution.py:615
  117.6 10.1 %all_to_all.92.refs_18_ = f32[8,1,1024]{2,1,0:T(1,128)S(1)} all-to-all(f32[8,1,1024]{2,1,0:T(1,128)S(1)} %get-tuple-element.128), channel_id=1, replica_groups={{0,8,16,24,32,40,48,56},{64,72,80,88,96,104,112,120},{128,136,144,152,1..., dimensions={0} | all-to-all | bytes 65536 | tf_op jit(solution)/shard_map/all_to_all | solution.py:617
  127.7 4.5 %krylov_step1.1 = (f32[16,512]{1,0:T(8,128)S(1)}, f32[8,128]{1,0:T(8,128)S(1)}, f32[48,128]{1,0:T(8,128)S(1)}, f32[16,512]{1,0:T(8,128)S(1)}, f32[64,128]{1,0:T(...) custom-call(s32[16,512]{1,0:T(8,128)S(1)} %get-tuple-element.87.slot_ref.refs_0_, ...), custom_call_target="tpu_custom_call" | custom-call | tf_op jit(solution)/shard_map/krylov_step1/pallas_call | solution.py:575
  132.2 7.8 %all_to_all.93.got_ref = f32[8,1,1152]{2,1,0:T(1,128)S(1)} all-to-all(f32[8,1,1152]{2,1,0:T(1,128)S(1)} %get-tuple-element.135), channel_id=1, replica_groups={{0,8,16,24,32,40,48,56},{64,72,80,88,96,104,112,120},{128,136,144,152,1..., dimensions={0} | all-to-all | bytes 73728 | tf_op jit(solution)/shard_map/all_to_all | solution.py:611
  140.0 9.3 %all_to_all.94.got_ref = f32[8,1,1152]{2,1,0:T(1,128)S(1)} all-to-all(f32[8,1,1152]{2,1,0:T(1,128)S(1)} %get-tuple-element.137), channel_id=1, replica_groups=mesh['curve'=64,'split'=8] {'split'}, dimensions={0} | all-to-all | bytes 73728 | tf_op jit(solution)/shard_map/all_to_all | solution.py:613
  149.4 9.3 %all_to_all.95.got_ref = f32[8,1,1280]{2,1,0:T(1,128)S(1)} all-to-all(f32[8,1,1280]{2,1,0:T(1,128)S(1)} %get-tuple-element.139), channel_id=1, replica_groups={{0,64,128,192,256,320,384,448},{8,72,136,200,264,328,392,456},{16,80,14..., dimensions={0} | all-to-all | bytes 81920 | tf_op jit(solution)/shard_map/all_to_all | solution.py:615
  158.7 10.1 %all_to_all.96.refs_18_ = f32[8,1,1024]{2,1,0:T(1,128)S(1)} all-to-all(f32[8,1,1024]{2,1,0:T(1,128)S(1)} %get-tuple-element.141), channel_id=1, replica_groups={{0,8,16,24,32,40,48,56},{64,72,80,88,96,104,112,120},{128,136,144,152,1..., dimensions={0} | all-to-all | bytes 65536 | tf_op jit(solution)/shard_map/all_to_all | solution.py:617
  168.8 4.5 %krylov_step2.1 = (f32[16,512]{1,0:T(8,128)S(1)}, f32[8,128]{1,0:T(8,128)S(1)}, f32[48,128]{1,0:T(8,128)S(1)}, f32[16,512]{1,0:T(8,128)S(1)}, f32[64,128]{1,0:T(...) custom-call(s32[16,512]{1,0:T(8,128)S(1)} %get-tuple-element.87.slot_ref.refs_0_, ...), custom_call_target="tpu_custom_call" | custom-call | tf_op jit(solution)/shard_map/krylov_step2/pallas_call | solution.py:575
  173.3 7.8 %all_to_all.97.got_ref = f32[8,1,1152]{2,1,0:T(1,128)S(1)} all-to-all(f32[8,1,1152]{2,1,0:T(1,128)S(1)} %get-tuple-element.147), channel_id=1, replica_groups={{0,8,16,24,32,40,48,56},{64,72,80,88,96,104,112,120},{128,136,144,152,1..., dimensions={0} | all-to-all | bytes 73728 | tf_op jit(solution)/shard_map/all_to_all | solution.py:611
  181.2 9.3 %all_to_all.98.got_ref = f32[8,1,1152]{2,1,0:T(1,128)S(1)} all-to-all(f32[8,1,1152]{2,1,0:T(1,128)S(1)} %get-tuple-element.149), channel_id=1, replica_groups=mesh['curve'=64,'split'=8] {'split'}, dimensions={0} | all-to-all | bytes 73728 | tf_op jit(solution)/shard_map/all_to_all | solution.py:613
  190.5 9.3 %all_to_all.99.got_ref = f32[8,1,1280]{2,1,0:T(1,128)S(1)} all-to-all(f32[8,1,1280]{2,1,0:T(1,128)S(1)} %get-tuple-element.151), channel_id=1, replica_groups={{0,64,128,192,256,320,384,448},{8,72,136,200,264,328,392,456},{16,80,14..., dimensions={0} | all-to-all | bytes 81920 | tf_op jit(solution)/shard_map/all_to_all | solution.py:615
  199.9 10.1 %all_to_all.100.refs_18_ = f32[8,1,1024]{2,1,0:T(1,128)S(1)} all-to-all(f32[8,1,1024]{2,1,0:T(1,128)S(1)} %get-tuple-element.153), channel_id=1, replica_groups={{0,8,16,24,32,40,48,56},{64,72,80,88,96,104,112,120},{128,136,144,152,1..., dimensions={0} | all-to-all | bytes 65536 | tf_op jit(solution)/shard_map/all_to_all | solution.py:617
  210.0 3.3 %krylov_step3.1 = (f32[16,512]{1,0:T(8,128)S(1)}, f32[8,128]{1,0:T(8,128)S(1)}, f32[48,128]{1,0:T(8,128)S(1)}, f32[16,512]{1,0:T(8,128)S(1)}, f32[1,128]{1,0:T(1...) custom-call(s32[16,512]{1,0:T(8,128)S(1)} %get-tuple-element.87.slot, ...), custom_call_target="tpu_custom_call" | custom-call | tf_op jit(solution)/shard_map/krylov_step3/pallas_call | solution.py:575
  213.3 2.2 collective-permute-start.6
  216.8 2.2 collective-permute-start.8
  219.0 3.3 %collective-permute-start.9 = (f32[1,128]{1,0:T(1,128)S(1)}, f32[1,128]{1,0:T(1,128)S(1)}, u32[]{:S(2)}, u32[]{:S(2)}) collective-permute-start(f32[1,128]{1,0:T(1,128)S(1)} %get-tuple-element.166), channel_id=1, source_target_pairs={{0,8},{8,16},{16,24},{24,32},{32,40},{40,48},{48,56},{56,64},{64,7... | collective-permute-start | bytes 1544 | tf_op jit(solution)/shard_map/ppermute | solution.py:589
  222.3 1.9 collective-permute-start.10
  230.0 33.2 %all_to_all.101.refs_0_ = f32[512,1,128]{2,1,0:T(1,128)S(1)} all-to-all(f32[512,1,128]{2,1,0:T(1,128)S(1)} %get-tuple-element.169), channel_id=1, replica_groups=mesh['curve'=64,'split'=8] {'curve','split'}, dimensions={0} | all-to-all | bytes 524288 | tf_op jit(solution)/shard_map/all_to_all | solution.py:688
  (30 shorter events, 12.2 us)
Async XLA Ops:
  9.1 14.6 %collective-permute-start = (f32[24,128]{1,0:T(8,128)S(1)}, f32[24,128]{1,0:T(8,128)S(1)}, u32[]{:S(2)}, u32[]{:S(2)}) collective-permute-start(f32[24,128]{1,0:T(8,128)S(1)} %get-tuple-element.100), channel_id=1, source_target_pairs={{0,1},{1,2},{2,3},{3,4},{4,5},{5,6},{6,7},{8,9},{9,10},{10,11},{11... | collective-permute-start | bytes 36872 | tf_op jit(solution)/shard_map/ppermute | solution.py:589
  13.2 11.9 %collective-permute-start.1 = (f32[24,128]{1,0:T(8,128)S(1)}, f32[24,128]{1,0:T(8,128)S(1)}, u32[]{:S(2)}, u32[]{:S(2)}) collective-permute-start(f32[24,128]{1,0:T(8,128)S(1)} %get-tuple-element.101), channel_id=1, source_target_pairs={{1,0},{2,1},{3,2},{4,3},{5,4},{6,5},{7,6},{9,8},{10,9},{11,10},{12... | collective-permute-start | bytes 36872 | tf_op jit(solution)/shard_map/ppermute | solution.py:589
  14.5 10.6 %collective-permute-start.2 = (f32[24,128]{1,0:T(8,128)S(1)}, f32[24,128]{1,0:T(8,128)S(1)}, u32[]{:S(2)}, u32[]{:S(2)}) collective-permute-start(f32[24,128]{1,0:T(8,128)S(1)} %get-tuple-element.102), channel_id=1, source_target_pairs={{0,16},{8,24},{16,32},{24,40},{32,48},{40,56},{48,64},{56,72},{64,... | collective-permute-start | bytes 36872 | tf_op jit(solution)/shard_map/ppermute | solution.py:589
  17.6 7.5 %collective-permute-start.3 = (f32[24,128]{1,0:T(8,128)S(1)}, f32[24,128]{1,0:T(8,128)S(1)}, u32[]{:S(2)}, u32[]{:S(2)}) collective-permute-start(f32[24,128]{1,0:T(8,128)S(1)} %get-tuple-element.103), channel_id=1, source_target_pairs={{0,8},{8,16},{16,24},{24,32},{32,40},{40,48},{48,56},{56,64},{64,7... | collective-permute-start | bytes 36872 | tf_op jit(solution)/shard_map/ppermute | solution.py:589
  21.8 5.0 %collective-permute-start.4 = (f32[24,128]{1,0:T(8,128)S(1)}, f32[24,128]{1,0:T(8,128)S(1)}, u32[]{:S(2)}, u32[]{:S(2)}) collective-permute-start(f32[24,128]{1,0:T(8,128)S(1)} %get-tuple-element.104), channel_id=1, source_target_pairs={{8,0},{16,8},{24,16},{32,24},{40,32},{48,40},{56,48},{64,56},{72,6... | collective-permute-start | bytes 36872 | tf_op jit(solution)/shard_map/ppermute | solution.py:589
  23.8 4.4 %collective-permute-start.5 = (f32[24,128]{1,0:T(8,128)S(1)}, f32[24,128]{1,0:T(8,128)S(1)}, u32[]{:S(2)}, u32[]{:S(2)}) collective-permute-start(f32[24,128]{1,0:T(8,128)S(1)} %get-tuple-element.105), channel_id=1, source_target_pairs={{16,0},{24,8},{32,16},{40,24},{48,32},{56,40},{64,48},{72,56},{80,... | collective-permute-start | bytes 36872 | tf_op jit(solution)/shard_map/ppermute | solution.py:589
  213.3 10.9 %collective-permute-start.6 = (f32[1,128]{1,0:T(1,128)S(1)}, f32[1,128]{1,0:T(1,128)S(1)}, u32[]{:S(2)}, u32[]{:S(2)}) collective-permute-start(f32[1,128]{1,0:T(1,128)S(1)} %get-tuple-element.163), channel_id=1, source_target_pairs={{0,1},{1,2},{2,3},{3,4},{4,5},{5,6},{6,7},{8,9},{9,10},{10,11},{11... | collective-permute-start | bytes 1544 | tf_op jit(solution)/shard_map/ppermute | solution.py:589
  215.5 10.0 %collective-permute-start.7 = (f32[1,128]{1,0:T(1,128)S(1)}, f32[1,128]{1,0:T(1,128)S(1)}, u32[]{:S(2)}, u32[]{:S(2)}) collective-permute-start(f32[1,128]{1,0:T(1,128)S(1)} %get-tuple-element.164), channel_id=1, source_target_pairs={{1,0},{2,1},{3,2},{4,3},{5,4},{6,5},{7,6},{9,8},{10,9},{11,10},{12... | collective-permute-start | bytes 1544 | tf_op jit(solution)/shard_map/ppermute | solution.py:589
  216.8 8.7 %collective-permute-start.8 = (f32[1,128]{1,0:T(1,128)S(1)}, f32[1,128]{1,0:T(1,128)S(1)}, u32[]{:S(2)}, u32[]{:S(2)}) collective-permute-start(f32[1,128]{1,0:T(1,128)S(1)} %get-tuple-element.165), channel_id=1, source_target_pairs={{0,16},{8,24},{16,32},{24,40},{32,48},{40,56},{48,64},{56,72},{64,... | collective-permute-start | bytes 1544 | tf_op jit(solution)/shard_map/ppermute | solution.py:589
  219.0 6.6 %collective-permute-start.9 = (f32[1,128]{1,0:T(1,128)S(1)}, f32[1,128]{1,0:T(1,128)S(1)}, u32[]{:S(2)}, u32[]{:S(2)}) collective-permute-start(f32[1,128]{1,0:T(1,128)S(1)} %get-tuple-element.166), channel_id=1, source_target_pairs={{0,8},{8,16},{16,24},{24,32},{32,40},{40,48},{48,56},{56,64},{64,7... | collective-permute-start | bytes 1544 | tf_op jit(solution)/shard_map/ppermute | solution.py:589
  222.3 4.9 %collective-permute-start.10 = (f32[1,128]{1,0:T(1,128)S(1)}, f32[1,128]{1,0:T(1,128)S(1)}, u32[]{:S(2)}, u32[]{:S(2)}) collective-permute-start(f32[1,128]{1,0:T(1,128)S(1)} %get-tuple-element.167), channel_id=1, source_target_pairs={{8,0},{16,8},{24,16},{32,24},{40,32},{48,40},{56,48},{64,56},{72,6... | collective-permute-start | bytes 1544 | tf_op jit(solution)/shard_map/ppermute | solution.py:589
  224.2 4.3 %collective-permute-start.11 = (f32[1,128]{1,0:T(1,128)S(1)}, f32[1,128]{1,0:T(1,128)S(1)}, u32[]{:S(2)}, u32[]{:S(2)}) collective-permute-start(f32[1,128]{1,0:T(1,128)S(1)} %get-tuple-element.168), channel_id=1, source_target_pairs={{16,0},{24,8},{32,16},{40,24},{48,32},{56,40},{64,48},{72,56},{80,... | collective-permute-start | bytes 1544 | tf_op jit(solution)/shard_map/ppermute | solution.py:589

commit v5 on v4

--- a/solution.py
+++ b/solution.py
@@ -21,6 +21,7 @@
 GROUP = 8
 CHUNK = ROWS * LO // GROUP
 PIECES = 2
+LATE = 13
 F32 = jnp.float32
 BF16 = jnp.bfloat16
 VMEM_LIMIT = 16 << 20
@@ -167,8 +168,13 @@
     return split_ref[0, 0, t : t + 1, :] if t < 2 else curve_ref[0, 0, t - 2 : t - 1, :]
 
 
-def list_hot(hot_ref, t):
-    return hot_ref[:, WIDE + t * LO : WIDE + (t + 1) * LO]
+def list_mask(split_ref, curve_ref):
+    rows = [list_row(split_ref, curve_ref, t) for t in range(LISTS)]
+    return row_mask(jnp.concatenate(rows, axis=1), HI)
+
+
+def by_list(wide):
+    return [wide[:, t * LO : (t + 1) * LO] for t in range(LISTS)]
 
 
 def point_hot(hot_ref, e):
@@ -232,7 +238,7 @@
     copies = [pltpu.make_async_copy(a, b, sems.at[i]) for i, (a, b) in enumerate(zip(sources, targets))]
     for copy in copies:
         copy.start()
-    for copy in copies:
+    for copy in copies[:LATE]:
         copy.wait()
     columns = [column(stretch_ref[d : d + 1, :]) for d in range(3)] + [column(helm_ref[...])]
     scale_ref[...] = jnp.concatenate(columns + columns, axis=1)
@@ -277,22 +283,22 @@
         table = fold(acc[first : first + PIECES * HI], HI) if field else acc[:HI]
         sums_ref[field] = table
         tables.append(table_parts(table))
+    slots = jnp.concatenate([list_row(split_ref, curve_ref, t) for t in range(LISTS)], axis=1)
+    hot = lane_hot(slots)
+    hot_ref[:, WIDE:] = hot
+    mask = row_mask(slots, HI)
+    rows = [take(tables[field], hot, mask) for field in range(3)]
+    plain = [cols[:, :LO], cols[:, LO:], factor[:, :LO], factor[:, LO:], jnp.zeros((1, LO), F32)]
     for t in range(LISTS):
-        slots = list_row(split_ref, curve_ref, t)
-        hot = lane_hot(slots)
-        hot_ref[:, WIDE + t * LO : WIDE + (t + 1) * LO] = hot
-        mask = row_mask(slots, HI)
-        rows = [take(tables[field], hot, mask) for field in range(3)]
-        rows += [cols[:, :LO], cols[:, LO:], factor[:, :LO], factor[:, LO:], jnp.zeros((1, LO), F32)]
-        out_refs[t][...] = jnp.concatenate(rows + [weights[:, t * LO : (t + 1) * LO]], axis=0)
+        lanes = slice(t * LO, (t + 1) * LO)
+        out_refs[t][...] = jnp.concatenate([row[:, lanes] for row in rows] + plain + [weights[:, lanes]], axis=0)
+    for copy in copies[LATE:]:
+        copy.wait()
 
 
 def incoming_table(split_ref, curve_ref, hot_ref, rows):
-    acc = jnp.zeros((PIECES * HI, LO), F32)
-    for t in range(LISTS):
-        mask = row_mask(list_row(split_ref, curve_ref, t), HI)
-        acc = acc + put(spread([rows[t]], mask), list_hot(hot_ref, t))
-    return fold(acc, HI)
+    left = spread([jnp.concatenate(rows, axis=1)], list_mask(split_ref, curve_ref))
+    return fold(put(left, hot_ref[:, WIDE:]), HI)
 
 
 def setup_gather(slot_ref, split_ref, curve_ref, hot_ref, sums_ref, phi_ref, pick_ref, entry_ref, xhot_ref, *refs):
@@ -310,15 +316,18 @@
         minv_ref[e : e + 1, :] = 1.0 / take(tables[0], hot, mask)
         dinv_ref[e : e + 1, :] = 1.0 / take(tables[1], hot, mask)
         right_ref[e : e + 1, :] = take(tables[2], hot, mask)
-    rows = []
+    mult = take(tables[0], hot_ref[:, WIDE:], list_mask(split_ref, curve_ref))
+    rows = by_list(jnp.where(mult > 0.5, 1.0 / jnp.where(mult > 0.5, mult, 1.0), 0.0))
+    own = entry_ref[...]
+    nentry_ref[:, :ENTRIES] = own
+    nhot_ref[:, :ENTRIES] = xhot_ref[...]
     for t in range(LISTS):
-        mult = take(tables[0], list_hot(hot_ref, t), row_mask(list_row(split_ref, curve_ref, t), HI))
-        rows.append(jnp.where(mult > 0.5, 1.0 / jnp.where(mult > 0.5, mult, 1.0), 0.0))
         there = jnp.concatenate([blocks[t][3:4, :], blocks[t][4:5, :]], axis=1)
         weight_ref[t] = blocks[t][8:24, :]
         entries = (there + 0.5).astype(jnp.int32)
-        nentry_ref[t : t + 1, :] = entries
-        nhot_ref[:, t * ENTRIES : (t + 1) * ENTRIES] = lane_hot(entries)
+        lanes = slice((t + 1) * ENTRIES, (t + 2) * ENTRIES)
+        nentry_ref[:, lanes] = entries
+        nhot_ref[:, lanes] = lane_hot(entries)
         nline_ref[t : t + 1, :] = jnp.concatenate([blocks[t][5:6, :], blocks[t][6:7, :]], axis=1)
     line = coarse_line(right_ref[...] * minv_ref[...], phi_ref, pick_ref)
     write_payload(pay_ref, rows_ref, image_of(line, entry_ref[...], xhot_ref[...]), rows)
@@ -355,10 +364,7 @@
 
 
 def send_lists(table, split_ref, curve_ref, hot_ref):
-    parts = table_parts(table)
-    return [
-        take(parts, list_hot(hot_ref, t), row_mask(list_row(split_ref, curve_ref, t), HI)) for t in range(LISTS)
-    ]
+    return by_list(take(table_parts(table), hot_ref[:, WIDE:], list_mask(split_ref, curve_ref)))
 
 
 def coarse_shift(image, earlier):
@@ -435,12 +441,12 @@
     pay_ref, rows_ref = refs
     gather_points(table, slot_ref, hot_ref, field_ref)
     line = coarse_line(field_ref[...] * minv_ref[...], phi_ref, pick_ref)
-    image = image_of(line, entry_ref[...], xhot_ref[...])
+    lines = [line]
     owner = owner_mask()
     for t in range(LISTS):
         loads = jnp.sum(weight_ref[t] * rows[t], axis=1, keepdims=True)
-        line = jnp.sum(jnp.where(owner, loads, 0.0), axis=0, keepdims=True) * nline_ref[t : t + 1, :]
-        image = image + image_of(line, nentry_ref[t : t + 1, :], nhot_ref[:, t * ENTRIES : (t + 1) * ENTRIES])
+        lines.append(jnp.sum(jnp.where(owner, loads, 0.0), axis=0, keepdims=True) * nline_ref[t : t + 1, :])
+    image = image_of(jnp.concatenate(lines, axis=1), nentry_ref[...], nhot_ref[...])
     write_payload(pay_ref, rows_ref, image, rows)
 
 
@@ -649,7 +655,7 @@
         setup_gather,
         "setup_gather",
         (*shape, sums3, phi, pick, entries, xhot, *arrived),
-        [field, field, field, ((LISTS, ENTRIES), F32), ((LISTS, ENTRIES), entry), ((LO, LISTS * ENTRIES), BF16),
+        [field, field, field, ((LISTS, ENTRIES), F32), ((1, (LISTS + 1) * ENTRIES), entry), ((LO, (LISTS + 1) * ENTRIES), BF16),
          ((LISTS, ELEMS, LO), F32)]
         + payload,
     )

time: 265 us -> 264 us (level)
  no operation moved by 1% of the time
where the time goes in v5:
time: 264 us; the launch traced here: 263 us
  blocking collectives  199 us (75%)
  Pallas kernels  29 us (11%)
  starting transfers between devices  28.1 us (11%)
  waiting for transfers between devices  6.08 us (2%)
    all_to_all x4, blocking collectives, reduce_image(): got = lax.all_to_all(pay, 'curve', 0, 0, axis_index_groups=far)  44.2 us
    all_to_all x4, blocking collectives, reduce_image(): got = lax.all_to_all(pay, 'split', 0, 0)  43.7 us
    all_to_all x4, blocking collectives, reduce_image(): return (lax.all_to_all(pay, 'curve', 0, 0, axis_index_groups=near), halo)  41 us
    all_to_all x4, blocking collectives, reduce_image(): got = lax.all_to_all(pay, 'curve', 0, 0, axis_index_groups=near)  36.8 us
    all_to_all x1, blocking collectives, local(): got = lax.all_to_all(pay, ('curve', 'split'), 0, 0)  33.2 us
    pallas_call x20, Pallas kernels, run(): pl.pallas_call(body, name=name, out_shape=[jax.ShapeDtypeStruct(shape, dt...  29 us
    ppermute x12, starting transfers between devices, shift(): return lax.ppermute(block, axis, route)  28.1 us
    ppermute x12, waiting for transfers between devices, shift(): return lax.ppermute(block, axis, route)  6.08 us
  transfers between devices with their start and end apart: 12, of which 4 were waited for; matrix products, arithmetic and copies ran while one was open for 0% of the time, Pallas kernels for 0%

profile of v5, /device:TPU:1, one launch (start us, length us, event | category | flops | bytes accessed | tf_op | source)
XLA Modules:
  0.0 263.0 jit_solution(16366864613087345312)
XLA Ops:
  0.6 7.9 %setup_scatter.1 = (s32[16,512]{1,0:T(8,128)S(1)}, s32[1,1,2,128]{3,2,1,0:T(2,128)S(1)}, s32[1,1,4,128]{3,2,1,0:T(4,128)S(1)}, f32[1,512]{1,0:T(1,128)S(1)}, f32...) custom-call(f32[16,512]{1,0:T(8,128)} %refs_0_.1, ...), custom_call_target="tpu_custom_call" | custom-call | tf_op jit(solution)/shard_map/setup_scatter/pallas_call | solution.py:581
  8.5 4.0 %collective-permute-start = (f32[24,128]{1,0:T(8,128)S(1)}, f32[24,128]{1,0:T(8,128)S(1)}, u32[]{:S(2)}, u32[]{:S(2)}) collective-permute-start(f32[24,128]{1,0:T(8,128)S(1)} %get-tuple-element.100), channel_id=1, source_target_pairs={{0,1},{1,2},{2,3},{3,4},{4,5},{5,6},{6,7},{8,9},{9,10},{10,11},{11... | collective-permute-start | bytes 36872 | tf_op jit(solution)/shard_map/ppermute | solution.py:595
  13.9 3.1 %collective-permute-start.2 = (f32[24,128]{1,0:T(8,128)S(1)}, f32[24,128]{1,0:T(8,128)S(1)}, u32[]{:S(2)}, u32[]{:S(2)}) collective-permute-start(f32[24,128]{1,0:T(8,128)S(1)} %get-tuple-element.102), channel_id=1, source_target_pairs={{0,16},{8,24},{16,32},{24,40},{32,48},{40,56},{48,64},{56,72},{64,... | collective-permute-start | bytes 36872 | tf_op jit(solution)/shard_map/ppermute | solution.py:595
  17.0 4.2 %collective-permute-start.3 = (f32[24,128]{1,0:T(8,128)S(1)}, f32[24,128]{1,0:T(8,128)S(1)}, u32[]{:S(2)}, u32[]{:S(2)}) collective-permute-start(f32[24,128]{1,0:T(8,128)S(1)} %get-tuple-element.103), channel_id=1, source_target_pairs={{0,8},{8,16},{16,24},{24,32},{32,40},{40,48},{48,56},{56,64},{64,7... | collective-permute-start | bytes 36872 | tf_op jit(solution)/shard_map/ppermute | solution.py:595
  21.3 1.9 collective-permute-start.4
  24.5 1.7 collective-permute-done.4.refs_4_
  27.6 2.9 %setup_gather.1 = (f32[16,512]{1,0:T(8,128)S(1)}, f32[16,512]{1,0:T(8,128)S(1)}, f32[16,512]{1,0:T(8,128)S(1)}, f32[6,256]{1,0:T(8,128)S(1)}, s32[1,1792]{1,0:T(...) custom-call(s32[16,512]{1,0:T(8,128)S(1)} %get-tuple-element.87.slot, ...), custom_call_target="tpu_custom_call" | custom-call | tf_op jit(solution)/shard_map/setup_gather/pallas_call | solution.py:581
  30.6 13.3 %all_to_all.85.got_ref = f32[8,1,1152]{2,1,0:T(1,128)S(1)} all-to-all(f32[8,1,1152]{2,1,0:T(1,128)S(1)} %get-tuple-element.111), channel_id=1, replica_groups={{0,8,16,24,32,40,48,56},{64,72,80,88,96,104,112,120},{128,136,144,152,1..., dimensions={0} | all-to-all | bytes 73728 | tf_op jit(solution)/shard_map/all_to_all | solution.py:617
  43.9 15.8 %all_to_all.86.got_ref = f32[8,1,1152]{2,1,0:T(1,128)S(1)} all-to-all(f32[8,1,1152]{2,1,0:T(1,128)S(1)} %get-tuple-element.113), channel_id=1, replica_groups=mesh['curve'=64,'split'=8] {'split'}, dimensions={0} | all-to-all | bytes 73728 | tf_op jit(solution)/shard_map/all_to_all | solution.py:619
  59.7 16.2 %all_to_all.87.got_ref = f32[8,1,1280]{2,1,0:T(1,128)S(1)} all-to-all(f32[8,1,1280]{2,1,0:T(1,128)S(1)} %get-tuple-element.115), channel_id=1, replica_groups={{0,64,128,192,256,320,384,448},{8,72,136,200,264,328,392,456},{16,80,14..., dimensions={0} | all-to-all | bytes 81920 | tf_op jit(solution)/shard_map/all_to_all | solution.py:621
  75.9 10.7 %all_to_all.88.refs_18_ = f32[8,1,1024]{2,1,0:T(1,128)S(1)} all-to-all(f32[8,1,1024]{2,1,0:T(1,128)S(1)} %get-tuple-element.117), channel_id=1, replica_groups={{0,8,16,24,32,40,48,56},{64,72,80,88,96,104,112,120},{128,136,144,152,1..., dimensions={0} | all-to-all | bytes 65536 | tf_op jit(solution)/shard_map/all_to_all | solution.py:623
  86.6 3.6 %krylov_step0.1 = (f32[16,512]{1,0:T(8,128)S(1)}, f32[8,128]{1,0:T(8,128)S(1)}, f32[48,128]{1,0:T(8,128)S(1)}, f32[6,16,128]{2,1,0:T(8,128)S(1)}, f32[64,128]{1,...) custom-call(s32[16,512]{1,0:T(8,128)S(1)} %get-tuple-element.87.slot_ref.refs_0_, ...), custom_call_target="tpu_custom_call" | custom-call | tf_op jit(solution)/shard_map/krylov_step0/pallas_call | solution.py:581
  90.2 7.8 %all_to_all.89.got_ref = f32[8,1,1152]{2,1,0:T(1,128)S(1)} all-to-all(f32[8,1,1152]{2,1,0:T(1,128)S(1)} %get-tuple-element.122), channel_id=1, replica_groups={{0,8,16,24,32,40,48,56},{64,72,80,88,96,104,112,120},{128,136,144,152,1..., dimensions={0} | all-to-all | bytes 73728 | tf_op jit(solution)/shard_map/all_to_all | solution.py:617
  98.1 9.3 %all_to_all.90.got_ref = f32[8,1,1152]{2,1,0:T(1,128)S(1)} all-to-all(f32[8,1,1152]{2,1,0:T(1,128)S(1)} %get-tuple-element.124), channel_id=1, replica_groups=mesh['curve'=64,'split'=8] {'split'}, dimensions={0} | all-to-all | bytes 73728 | tf_op jit(solution)/shard_map/all_to_all | solution.py:619
  107.4 9.3 %all_to_all.91.got_ref = f32[8,1,1280]{2,1,0:T(1,128)S(1)} all-to-all(f32[8,1,1280]{2,1,0:T(1,128)S(1)} %get-tuple-element.126), channel_id=1, replica_groups={{0,64,128,192,256,320,384,448},{8,72,136,200,264,328,392,456},{16,80,14..., dimensions={0} | all-to-all | bytes 81920 | tf_op jit(solution)/shard_map/all_to_all | solution.py:621
  116.8 10.1 %all_to_all.92.refs_18_ = f32[8,1,1024]{2,1,0:T(1,128)S(1)} all-to-all(f32[8,1,1024]{2,1,0:T(1,128)S(1)} %get-tuple-element.128), channel_id=1, replica_groups={{0,8,16,24,32,40,48,56},{64,72,80,88,96,104,112,120},{128,136,144,152,1..., dimensions={0} | all-to-all | bytes 65536 | tf_op jit(solution)/shard_map/all_to_all | solution.py:623
  126.9 4.4 %krylov_step1.1 = (f32[16,512]{1,0:T(8,128)S(1)}, f32[8,128]{1,0:T(8,128)S(1)}, f32[48,128]{1,0:T(8,128)S(1)}, f32[16,512]{1,0:T(8,128)S(1)}, f32[64,128]{1,0:T(...) custom-call(s32[16,512]{1,0:T(8,128)S(1)} %get-tuple-element.87.slot_ref.refs_0_, ...), custom_call_target="tpu_custom_call" | custom-call | tf_op jit(solution)/shard_map/krylov_step1/pallas_call | solution.py:581
  131.3 7.8 %all_to_all.93.got_ref = f32[8,1,1152]{2,1,0:T(1,128)S(1)} all-to-all(f32[8,1,1152]{2,1,0:T(1,128)S(1)} %get-tuple-element.135), channel_id=1, replica_groups={{0,8,16,24,32,40,48,56},{64,72,80,88,96,104,112,120},{128,136,144,152,1..., dimensions={0} | all-to-all | bytes 73728 | tf_op jit(solution)/shard_map/all_to_all | solution.py:617
  139.2 9.3 %all_to_all.94.got_ref = f32[8,1,1152]{2,1,0:T(1,128)S(1)} all-to-all(f32[8,1,1152]{2,1,0:T(1,128)S(1)} %get-tuple-element.137), channel_id=1, replica_groups=mesh['curve'=64,'split'=8] {'split'}, dimensions={0} | all-to-all | bytes 73728 | tf_op jit(solution)/shard_map/all_to_all | solution.py:619
  148.5 9.3 %all_to_all.95.got_ref = f32[8,1,1280]{2,1,0:T(1,128)S(1)} all-to-all(f32[8,1,1280]{2,1,0:T(1,128)S(1)} %get-tuple-element.139), channel_id=1, replica_groups={{0,64,128,192,256,320,384,448},{8,72,136,200,264,328,392,456},{16,80,14..., dimensions={0} | all-to-all | bytes 81920 | tf_op jit(solution)/shard_map/all_to_all | solution.py:621
  157.9 10.1 %all_to_all.96.refs_18_ = f32[8,1,1024]{2,1,0:T(1,128)S(1)} all-to-all(f32[8,1,1024]{2,1,0:T(1,128)S(1)} %get-tuple-element.141), channel_id=1, replica_groups={{0,8,16,24,32,40,48,56},{64,72,80,88,96,104,112,120},{128,136,144,152,1..., dimensions={0} | all-to-all | bytes 65536 | tf_op jit(solution)/shard_map/all_to_all | solution.py:623
  168.0 4.4 %krylov_step2.1 = (f32[16,512]{1,0:T(8,128)S(1)}, f32[8,128]{1,0:T(8,128)S(1)}, f32[48,128]{1,0:T(8,128)S(1)}, f32[16,512]{1,0:T(8,128)S(1)}, f32[64,128]{1,0:T(...) custom-call(s32[16,512]{1,0:T(8,128)S(1)} %get-tuple-element.87.slot_ref.refs_0_, ...), custom_call_target="tpu_custom_call" | custom-call | tf_op jit(solution)/shard_map/krylov_step2/pallas_call | solution.py:581
  172.4 7.8 %all_to_all.97.got_ref = f32[8,1,1152]{2,1,0:T(1,128)S(1)} all-to-all(f32[8,1,1152]{2,1,0:T(1,128)S(1)} %get-tuple-element.147), channel_id=1, replica_groups={{0,8,16,24,32,40,48,56},{64,72,80,88,96,104,112,120},{128,136,144,152,1..., dimensions={0} | all-to-all | bytes 73728 | tf_op jit(solution)/shard_map/all_to_all | solution.py:617
  180.2 9.3 %all_to_all.98.got_ref = f32[8,1,1152]{2,1,0:T(1,128)S(1)} all-to-all(f32[8,1,1152]{2,1,0:T(1,128)S(1)} %get-tuple-element.149), channel_id=1, replica_groups=mesh['curve'=64,'split'=8] {'split'}, dimensions={0} | all-to-all | bytes 73728 | tf_op jit(solution)/shard_map/all_to_all | solution.py:619
  189.6 9.3 %all_to_all.99.got_ref = f32[8,1,1280]{2,1,0:T(1,128)S(1)} all-to-all(f32[8,1,1280]{2,1,0:T(1,128)S(1)} %get-tuple-element.151), channel_id=1, replica_groups={{0,64,128,192,256,320,384,448},{8,72,136,200,264,328,392,456},{16,80,14..., dimensions={0} | all-to-all | bytes 81920 | tf_op jit(solution)/shard_map/all_to_all | solution.py:621
  198.9 10.1 %all_to_all.100.refs_18_ = f32[8,1,1024]{2,1,0:T(1,128)S(1)} all-to-all(f32[8,1,1024]{2,1,0:T(1,128)S(1)} %get-tuple-element.153), channel_id=1, replica_groups={{0,8,16,24,32,40,48,56},{64,72,80,88,96,104,112,120},{128,136,144,152,1..., dimensions={0} | all-to-all | bytes 65536 | tf_op jit(solution)/shard_map/all_to_all | solution.py:623
  209.1 3.2 %krylov_step3.1 = (f32[16,512]{1,0:T(8,128)S(1)}, f32[8,128]{1,0:T(8,128)S(1)}, f32[48,128]{1,0:T(8,128)S(1)}, f32[16,512]{1,0:T(8,128)S(1)}, f32[1,128]{1,0:T(1...) custom-call(s32[16,512]{1,0:T(8,128)S(1)} %get-tuple-element.87.slot, ...), custom_call_target="tpu_custom_call" | custom-call | tf_op jit(solution)/shard_map/krylov_step3/pallas_call | solution.py:581
  212.3 2.2 collective-permute-start.6
  215.8 2.2 collective-permute-start.8
  218.0 3.3 %collective-permute-start.9 = (f32[1,128]{1,0:T(1,128)S(1)}, f32[1,128]{1,0:T(1,128)S(1)}, u32[]{:S(2)}, u32[]{:S(2)}) collective-permute-start(f32[1,128]{1,0:T(1,128)S(1)} %get-tuple-element.166), channel_id=1, source_target_pairs={{0,8},{8,16},{16,24},{24,32},{32,40},{40,48},{48,56},{56,64},{64,7... | collective-permute-start | bytes 1544 | tf_op jit(solution)/shard_map/ppermute | solution.py:595
  221.3 1.9 collective-permute-start.10
  228.8 33.2 %all_to_all.101.refs_0_ = f32[512,1,128]{2,1,0:T(1,128)S(1)} all-to-all(f32[512,1,128]{2,1,0:T(1,128)S(1)} %get-tuple-element.169), channel_id=1, replica_groups=mesh['curve'=64,'split'=8] {'curve','split'}, dimensions={0} | all-to-all | bytes 524288 | tf_op jit(solution)/shard_map/all_to_all | solution.py:694
  (30 shorter events, 12.1 us)
Async XLA Ops:
  8.5 14.6 %collective-permute-start = (f32[24,128]{1,0:T(8,128)S(1)}, f32[24,128]{1,0:T(8,128)S(1)}, u32[]{:S(2)}, u32[]{:S(2)}) collective-permute-start(f32[24,128]{1,0:T(8,128)S(1)} %get-tuple-element.100), channel_id=1, source_target_pairs={{0,1},{1,2},{2,3},{3,4},{4,5},{5,6},{6,7},{8,9},{9,10},{10,11},{11... | collective-permute-start | bytes 36872 | tf_op jit(solution)/shard_map/ppermute | solution.py:595
  12.6 11.9 %collective-permute-start.1 = (f32[24,128]{1,0:T(8,128)S(1)}, f32[24,128]{1,0:T(8,128)S(1)}, u32[]{:S(2)}, u32[]{:S(2)}) collective-permute-start(f32[24,128]{1,0:T(8,128)S(1)} %get-tuple-element.101), channel_id=1, source_target_pairs={{1,0},{2,1},{3,2},{4,3},{5,4},{6,5},{7,6},{9,8},{10,9},{11,10},{12... | collective-permute-start | bytes 36872 | tf_op jit(solution)/shard_map/ppermute | solution.py:595
  13.9 10.6 %collective-permute-start.2 = (f32[24,128]{1,0:T(8,128)S(1)}, f32[24,128]{1,0:T(8,128)S(1)}, u32[]{:S(2)}, u32[]{:S(2)}) collective-permute-start(f32[24,128]{1,0:T(8,128)S(1)} %get-tuple-element.102), channel_id=1, source_target_pairs={{0,16},{8,24},{16,32},{24,40},{32,48},{40,56},{48,64},{56,72},{64,... | collective-permute-start | bytes 36872 | tf_op jit(solution)/shard_map/ppermute | solution.py:595
  17.0 7.5 %collective-permute-start.3 = (f32[24,128]{1,0:T(8,128)S(1)}, f32[24,128]{1,0:T(8,128)S(1)}, u32[]{:S(2)}, u32[]{:S(2)}) collective-permute-start(f32[24,128]{1,0:T(8,128)S(1)} %get-tuple-element.103), channel_id=1, source_target_pairs={{0,8},{8,16},{16,24},{24,32},{32,40},{40,48},{48,56},{56,64},{64,7... | collective-permute-start | bytes 36872 | tf_op jit(solution)/shard_map/ppermute | solution.py:595
  21.3 5.0 %collective-permute-start.4 = (f32[24,128]{1,0:T(8,128)S(1)}, f32[24,128]{1,0:T(8,128)S(1)}, u32[]{:S(2)}, u32[]{:S(2)}) collective-permute-start(f32[24,128]{1,0:T(8,128)S(1)} %get-tuple-element.104), channel_id=1, source_target_pairs={{8,0},{16,8},{24,16},{32,24},{40,32},{48,40},{56,48},{64,56},{72,6... | collective-permute-start | bytes 36872 | tf_op jit(solution)/shard_map/ppermute | solution.py:595
  23.2 4.4 %collective-permute-start.5 = (f32[24,128]{1,0:T(8,128)S(1)}, f32[24,128]{1,0:T(8,128)S(1)}, u32[]{:S(2)}, u32[]{:S(2)}) collective-permute-start(f32[24,128]{1,0:T(8,128)S(1)} %get-tuple-element.105), channel_id=1, source_target_pairs={{16,0},{24,8},{32,16},{40,24},{48,32},{56,40},{64,48},{72,56},{80,... | collective-permute-start | bytes 36872 | tf_op jit(solution)/shard_map/ppermute | solution.py:595
  212.3 10.9 %collective-permute-start.6 = (f32[1,128]{1,0:T(1,128)S(1)}, f32[1,128]{1,0:T(1,128)S(1)}, u32[]{:S(2)}, u32[]{:S(2)}) collective-permute-start(f32[1,128]{1,0:T(1,128)S(1)} %get-tuple-element.163), channel_id=1, source_target_pairs={{0,1},{1,2},{2,3},{3,4},{4,5},{5,6},{6,7},{8,9},{9,10},{10,11},{11... | collective-permute-start | bytes 1544 | tf_op jit(solution)/shard_map/ppermute | solution.py:595
  214.5 10.0 %collective-permute-start.7 = (f32[1,128]{1,0:T(1,128)S(1)}, f32[1,128]{1,0:T(1,128)S(1)}, u32[]{:S(2)}, u32[]{:S(2)}) collective-permute-start(f32[1,128]{1,0:T(1,128)S(1)} %get-tuple-element.164), channel_id=1, source_target_pairs={{1,0},{2,1},{3,2},{4,3},{5,4},{6,5},{7,6},{9,8},{10,9},{11,10},{12... | collective-permute-start | bytes 1544 | tf_op jit(solution)/shard_map/ppermute | solution.py:595
  215.8 8.7 %collective-permute-start.8 = (f32[1,128]{1,0:T(1,128)S(1)}, f32[1,128]{1,0:T(1,128)S(1)}, u32[]{:S(2)}, u32[]{:S(2)}) collective-permute-start(f32[1,128]{1,0:T(1,128)S(1)} %get-tuple-element.165), channel_id=1, source_target_pairs={{0,16},{8,24},{16,32},{24,40},{32,48},{40,56},{48,64},{56,72},{64,... | collective-permute-start | bytes 1544 | tf_op jit(solution)/shard_map/ppermute | solution.py:595
  218.0 6.6 %collective-permute-start.9 = (f32[1,128]{1,0:T(1,128)S(1)}, f32[1,128]{1,0:T(1,128)S(1)}, u32[]{:S(2)}, u32[]{:S(2)}) collective-permute-start(f32[1,128]{1,0:T(1,128)S(1)} %get-tuple-element.166), channel_id=1, source_target_pairs={{0,8},{8,16},{16,24},{24,32},{32,40},{40,48},{48,56},{56,64},{64,7... | collective-permute-start | bytes 1544 | tf_op jit(solution)/shard_map/ppermute | solution.py:595
  221.3 4.9 %collective-permute-start.10 = (f32[1,128]{1,0:T(1,128)S(1)}, f32[1,128]{1,0:T(1,128)S(1)}, u32[]{:S(2)}, u32[]{:S(2)}) collective-permute-start(f32[1,128]{1,0:T(1,128)S(1)} %get-tuple-element.167), channel_id=1, source_target_pairs={{8,0},{16,8},{24,16},{32,24},{40,32},{48,40},{56,48},{64,56},{72,6... | collective-permute-start | bytes 1544 | tf_op jit(solution)/shard_map/ppermute | solution.py:595
  223.2 4.3 %collective-permute-start.11 = (f32[1,128]{1,0:T(1,128)S(1)}, f32[1,128]{1,0:T(1,128)S(1)}, u32[]{:S(2)}, u32[]{:S(2)}) collective-permute-start(f32[1,128]{1,0:T(1,128)S(1)} %get-tuple-element.168), channel_id=1, source_target_pairs={{16,0},{24,8},{32,16},{40,24},{48,32},{56,40},{64,48},{72,56},{80,... | collective-permute-start | bytes 1544 | tf_op jit(solution)/shard_map/ppermute | solution.py:595

commit v6 on v5

--- a/solution.py
+++ b/solution.py
@@ -20,7 +20,7 @@
 ROWS = 64
 GROUP = 8
 CHUNK = ROWS * LO // GROUP
-PIECES = 2
+PIECES = 3
 LATE = 13
 F32 = jnp.float32
 BF16 = jnp.bfloat16
@@ -337,7 +337,9 @@
     def product(parts, ref):
         rows = parts[0].shape[0]
         one = jnp.dot(jnp.concatenate(parts, axis=0), ref[0], preferred_element_type=F32)
-        return one[:rows] + (one[rows:] + jnp.dot(parts[0], ref[1], preferred_element_type=F32))
+        two = jnp.dot(jnp.concatenate(parts[:2], axis=0), ref[1], preferred_element_type=F32)
+        three = jnp.dot(parts[0], ref[2], preferred_element_type=F32)
+        return one[:rows] + (one[rows : 2 * rows] + two[:rows] + (one[2 * rows :] + two[rows:] + three))
 
     half = POINTS // 2
     parts = pieces(u)

time: 264 us -> 268 us (1.015)
  Pallas kernels: 29 us -> 32.6 us
    pallas_call x20, Pallas kernels: 29 us -> 32.6 us  [run(): pl.pallas_call(body, name=name, out_shape=[jax.ShapeDtypeStruct(shape, dt...]
where the time goes in v6:
time: 268 us; the launch traced here: 267 us
  blocking collectives  199 us (74%)
  Pallas kernels  32.6 us (12%)
  starting transfers between devices  28.1 us (10%)
  waiting for transfers between devices  6.08 us (2%)
    all_to_all x4, blocking collectives, reduce_image(): got = lax.all_to_all(pay, 'curve', 0, 0, axis_index_groups=far)  44.2 us
    all_to_all x4, blocking collectives, reduce_image(): got = lax.all_to_all(pay, 'split', 0, 0)  43.7 us
    all_to_all x4, blocking collectives, reduce_image(): return (lax.all_to_all(pay, 'curve', 0, 0, axis_index_groups=near), halo)  41 us
    all_to_all x4, blocking collectives, reduce_image(): got = lax.all_to_all(pay, 'curve', 0, 0, axis_index_groups=near)  36.8 us
    all_to_all x1, blocking collectives, local(): got = lax.all_to_all(pay, ('curve', 'split'), 0, 0)  33.2 us
    pallas_call x20, Pallas kernels, run(): pl.pallas_call(body, name=name, out_shape=[jax.ShapeDtypeStruct(shape, dt...  32.6 us
    ppermute x12, starting transfers between devices, shift(): return lax.ppermute(block, axis, route)  28.1 us
    ppermute x12, waiting for transfers between devices, shift(): return lax.ppermute(block, axis, route)  6.08 us
  transfers between devices with their start and end apart: 12, of which 4 were waited for; matrix products, arithmetic and copies ran while one was open for 0% of the time, Pallas kernels for 0%

profile of v6, /device:TPU:1, one launch (start us, length us, event | category | flops | bytes accessed | tf_op | source)
XLA Modules:
  0.0 266.5 jit_solution(13054150625296561550)
XLA Ops:
  0.6 8.1 %setup_scatter.1 = (s32[16,512]{1,0:T(8,128)S(1)}, s32[1,1,2,128]{3,2,1,0:T(2,128)S(1)}, s32[1,1,4,128]{3,2,1,0:T(4,128)S(1)}, f32[1,512]{1,0:T(1,128)S(1)}, f32...) custom-call(f32[16,512]{1,0:T(8,128)} %refs_0_.1, ...), custom_call_target="tpu_custom_call" | custom-call | tf_op jit(solution)/shard_map/setup_scatter/pallas_call | solution.py:583
  8.7 4.0 %collective-permute-start = (f32[24,128]{1,0:T(8,128)S(1)}, f32[24,128]{1,0:T(8,128)S(1)}, u32[]{:S(2)}, u32[]{:S(2)}) collective-permute-start(f32[24,128]{1,0:T(8,128)S(1)} %get-tuple-element.100), channel_id=1, source_target_pairs={{0,1},{1,2},{2,3},{3,4},{4,5},{5,6},{6,7},{8,9},{9,10},{10,11},{11... | collective-permute-start | bytes 36872 | tf_op jit(solution)/shard_map/ppermute | solution.py:597
  14.0 3.1 %collective-permute-start.2 = (f32[24,128]{1,0:T(8,128)S(1)}, f32[24,128]{1,0:T(8,128)S(1)}, u32[]{:S(2)}, u32[]{:S(2)}) collective-permute-start(f32[24,128]{1,0:T(8,128)S(1)} %get-tuple-element.102), channel_id=1, source_target_pairs={{0,16},{8,24},{16,32},{24,40},{32,48},{40,56},{48,64},{56,72},{64,... | collective-permute-start | bytes 36872 | tf_op jit(solution)/shard_map/ppermute | solution.py:597
  17.2 4.2 %collective-permute-start.3 = (f32[24,128]{1,0:T(8,128)S(1)}, f32[24,128]{1,0:T(8,128)S(1)}, u32[]{:S(2)}, u32[]{:S(2)}) collective-permute-start(f32[24,128]{1,0:T(8,128)S(1)} %get-tuple-element.103), channel_id=1, source_target_pairs={{0,8},{8,16},{16,24},{24,32},{32,40},{40,48},{48,56},{56,64},{64,7... | collective-permute-start | bytes 36872 | tf_op jit(solution)/shard_map/ppermute | solution.py:597
  21.4 1.9 collective-permute-start.4
  24.7 1.7 collective-permute-done.4.refs_4_
  27.8 3.3 %setup_gather.1 = (f32[16,512]{1,0:T(8,128)S(1)}, f32[16,512]{1,0:T(8,128)S(1)}, f32[16,512]{1,0:T(8,128)S(1)}, f32[6,256]{1,0:T(8,128)S(1)}, s32[1,1792]{1,0:T(...) custom-call(s32[16,512]{1,0:T(8,128)S(1)} %get-tuple-element.87.slot, ...), custom_call_target="tpu_custom_call" | custom-call | tf_op jit(solution)/shard_map/setup_gather/pallas_call | solution.py:583
  31.0 13.3 %all_to_all.85.got_ref = f32[8,1,1152]{2,1,0:T(1,128)S(1)} all-to-all(f32[8,1,1152]{2,1,0:T(1,128)S(1)} %get-tuple-element.111), channel_id=1, replica_groups={{0,8,16,24,32,40,48,56},{64,72,80,88,96,104,112,120},{128,136,144,152,1..., dimensions={0} | all-to-all | bytes 73728 | tf_op jit(solution)/shard_map/all_to_all | solution.py:619
  44.3 15.8 %all_to_all.86.got_ref = f32[8,1,1152]{2,1,0:T(1,128)S(1)} all-to-all(f32[8,1,1152]{2,1,0:T(1,128)S(1)} %get-tuple-element.113), channel_id=1, replica_groups=mesh['curve'=64,'split'=8] {'split'}, dimensions={0} | all-to-all | bytes 73728 | tf_op jit(solution)/shard_map/all_to_all | solution.py:621
  60.2 16.2 %all_to_all.87.got_ref = f32[8,1,1280]{2,1,0:T(1,128)S(1)} all-to-all(f32[8,1,1280]{2,1,0:T(1,128)S(1)} %get-tuple-element.115), channel_id=1, replica_groups={{0,64,128,192,256,320,384,448},{8,72,136,200,264,328,392,456},{16,80,14..., dimensions={0} | all-to-all | bytes 81920 | tf_op jit(solution)/shard_map/all_to_all | solution.py:623
  76.4 10.7 %all_to_all.88.refs_18_ = f32[8,1,1024]{2,1,0:T(1,128)S(1)} all-to-all(f32[8,1,1024]{2,1,0:T(1,128)S(1)} %get-tuple-element.117), channel_id=1, replica_groups={{0,8,16,24,32,40,48,56},{64,72,80,88,96,104,112,120},{128,136,144,152,1..., dimensions={0} | all-to-all | bytes 65536 | tf_op jit(solution)/shard_map/all_to_all | solution.py:625
  87.1 4.3 %krylov_step0.1 = (f32[16,512]{1,0:T(8,128)S(1)}, f32[8,128]{1,0:T(8,128)S(1)}, f32[48,128]{1,0:T(8,128)S(1)}, f32[6,16,128]{2,1,0:T(8,128)S(1)}, f32[64,128]{1,...) custom-call(s32[16,512]{1,0:T(8,128)S(1)} %get-tuple-element.87.slot_ref.refs_0_, ...), custom_call_target="tpu_custom_call" | custom-call | tf_op jit(solution)/shard_map/krylov_step0/pallas_call | solution.py:583
  91.4 7.8 %all_to_all.89.got_ref = f32[8,1,1152]{2,1,0:T(1,128)S(1)} all-to-all(f32[8,1,1152]{2,1,0:T(1,128)S(1)} %get-tuple-element.122), channel_id=1, replica_groups={{0,8,16,24,32,40,48,56},{64,72,80,88,96,104,112,120},{128,136,144,152,1..., dimensions={0} | all-to-all | bytes 73728 | tf_op jit(solution)/shard_map/all_to_all | solution.py:619
  99.2 9.3 %all_to_all.90.got_ref = f32[8,1,1152]{2,1,0:T(1,128)S(1)} all-to-all(f32[8,1,1152]{2,1,0:T(1,128)S(1)} %get-tuple-element.124), channel_id=1, replica_groups=mesh['curve'=64,'split'=8] {'split'}, dimensions={0} | all-to-all | bytes 73728 | tf_op jit(solution)/shard_map/all_to_all | solution.py:621
  108.6 9.3 %all_to_all.91.got_ref = f32[8,1,1280]{2,1,0:T(1,128)S(1)} all-to-all(f32[8,1,1280]{2,1,0:T(1,128)S(1)} %get-tuple-element.126), channel_id=1, replica_groups={{0,64,128,192,256,320,384,448},{8,72,136,200,264,328,392,456},{16,80,14..., dimensions={0} | all-to-all | bytes 81920 | tf_op jit(solution)/shard_map/all_to_all | solution.py:623
  117.9 10.1 %all_to_all.92.refs_18_ = f32[8,1,1024]{2,1,0:T(1,128)S(1)} all-to-all(f32[8,1,1024]{2,1,0:T(1,128)S(1)} %get-tuple-element.128), channel_id=1, replica_groups={{0,8,16,24,32,40,48,56},{64,72,80,88,96,104,112,120},{128,136,144,152,1..., dimensions={0} | all-to-all | bytes 65536 | tf_op jit(solution)/shard_map/all_to_all | solution.py:625
  128.1 5.5 %krylov_step1.1 = (f32[16,512]{1,0:T(8,128)S(1)}, f32[8,128]{1,0:T(8,128)S(1)}, f32[48,128]{1,0:T(8,128)S(1)}, f32[16,512]{1,0:T(8,128)S(1)}, f32[64,128]{1,0:T(...) custom-call(s32[16,512]{1,0:T(8,128)S(1)} %get-tuple-element.87.slot_ref.refs_0_, ...), custom_call_target="tpu_custom_call" | custom-call | tf_op jit(solution)/shard_map/krylov_step1/pallas_call | solution.py:583
  133.6 7.8 %all_to_all.93.got_ref = f32[8,1,1152]{2,1,0:T(1,128)S(1)} all-to-all(f32[8,1,1152]{2,1,0:T(1,128)S(1)} %get-tuple-element.135), channel_id=1, replica_groups={{0,8,16,24,32,40,48,56},{64,72,80,88,96,104,112,120},{128,136,144,152,1..., dimensions={0} | all-to-all | bytes 73728 | tf_op jit(solution)/shard_map/all_to_all | solution.py:619
  141.5 9.3 %all_to_all.94.got_ref = f32[8,1,1152]{2,1,0:T(1,128)S(1)} all-to-all(f32[8,1,1152]{2,1,0:T(1,128)S(1)} %get-tuple-element.137), channel_id=1, replica_groups=mesh['curve'=64,'split'=8] {'split'}, dimensions={0} | all-to-all | bytes 73728 | tf_op jit(solution)/shard_map/all_to_all | solution.py:621
  150.8 9.3 %all_to_all.95.got_ref = f32[8,1,1280]{2,1,0:T(1,128)S(1)} all-to-all(f32[8,1,1280]{2,1,0:T(1,128)S(1)} %get-tuple-element.139), channel_id=1, replica_groups={{0,64,128,192,256,320,384,448},{8,72,136,200,264,328,392,456},{16,80,14..., dimensions={0} | all-to-all | bytes 81920 | tf_op jit(solution)/shard_map/all_to_all | solution.py:623
  160.1 10.1 %all_to_all.96.refs_18_ = f32[8,1,1024]{2,1,0:T(1,128)S(1)} all-to-all(f32[8,1,1024]{2,1,0:T(1,128)S(1)} %get-tuple-element.141), channel_id=1, replica_groups={{0,8,16,24,32,40,48,56},{64,72,80,88,96,104,112,120},{128,136,144,152,1..., dimensions={0} | all-to-all | bytes 65536 | tf_op jit(solution)/shard_map/all_to_all | solution.py:625
  170.3 5.5 %krylov_step2.1 = (f32[16,512]{1,0:T(8,128)S(1)}, f32[8,128]{1,0:T(8,128)S(1)}, f32[48,128]{1,0:T(8,128)S(1)}, f32[16,512]{1,0:T(8,128)S(1)}, f32[64,128]{1,0:T(...) custom-call(s32[16,512]{1,0:T(8,128)S(1)} %get-tuple-element.87.slot_ref.refs_0_, ...), custom_call_target="tpu_custom_call" | custom-call | tf_op jit(solution)/shard_map/krylov_step2/pallas_call | solution.py:583
  175.8 7.8 %all_to_all.97.got_ref = f32[8,1,1152]{2,1,0:T(1,128)S(1)} all-to-all(f32[8,1,1152]{2,1,0:T(1,128)S(1)} %get-tuple-element.147), channel_id=1, replica_groups={{0,8,16,24,32,40,48,56},{64,72,80,88,96,104,112,120},{128,136,144,152,1..., dimensions={0} | all-to-all | bytes 73728 | tf_op jit(solution)/shard_map/all_to_all | solution.py:619
  183.7 9.3 %all_to_all.98.got_ref = f32[8,1,1152]{2,1,0:T(1,128)S(1)} all-to-all(f32[8,1,1152]{2,1,0:T(1,128)S(1)} %get-tuple-element.149), channel_id=1, replica_groups=mesh['curve'=64,'split'=8] {'split'}, dimensions={0} | all-to-all | bytes 73728 | tf_op jit(solution)/shard_map/all_to_all | solution.py:621
  193.0 9.3 %all_to_all.99.got_ref = f32[8,1,1280]{2,1,0:T(1,128)S(1)} all-to-all(f32[8,1,1280]{2,1,0:T(1,128)S(1)} %get-tuple-element.151), channel_id=1, replica_groups={{0,64,128,192,256,320,384,448},{8,72,136,200,264,328,392,456},{16,80,14..., dimensions={0} | all-to-all | bytes 81920 | tf_op jit(solution)/shard_map/all_to_all | solution.py:623
  202.4 10.1 %all_to_all.100.refs_18_ = f32[8,1,1024]{2,1,0:T(1,128)S(1)} all-to-all(f32[8,1,1024]{2,1,0:T(1,128)S(1)} %get-tuple-element.153), channel_id=1, replica_groups={{0,8,16,24,32,40,48,56},{64,72,80,88,96,104,112,120},{128,136,144,152,1..., dimensions={0} | all-to-all | bytes 65536 | tf_op jit(solution)/shard_map/all_to_all | solution.py:625
  212.5 3.2 %krylov_step3.1 = (f32[16,512]{1,0:T(8,128)S(1)}, f32[8,128]{1,0:T(8,128)S(1)}, f32[48,128]{1,0:T(8,128)S(1)}, f32[16,512]{1,0:T(8,128)S(1)}, f32[1,128]{1,0:T(1...) custom-call(s32[16,512]{1,0:T(8,128)S(1)} %get-tuple-element.87.slot, ...), custom_call_target="tpu_custom_call" | custom-call | tf_op jit(solution)/shard_map/krylov_step3/pallas_call | solution.py:583
  215.7 2.2 collective-permute-start.6
  219.2 2.2 collective-permute-start.8
  221.4 3.3 %collective-permute-start.9 = (f32[1,128]{1,0:T(1,128)S(1)}, f32[1,128]{1,0:T(1,128)S(1)}, u32[]{:S(2)}, u32[]{:S(2)}) collective-permute-start(f32[1,128]{1,0:T(1,128)S(1)} %get-tuple-element.166), channel_id=1, source_target_pairs={{0,8},{8,16},{16,24},{24,32},{32,40},{40,48},{48,56},{56,64},{64,7... | collective-permute-start | bytes 1544 | tf_op jit(solution)/shard_map/ppermute | solution.py:597
  224.7 1.9 collective-permute-start.10
  232.4 33.2 %all_to_all.101.refs_0_ = f32[512,1,128]{2,1,0:T(1,128)S(1)} all-to-all(f32[512,1,128]{2,1,0:T(1,128)S(1)} %get-tuple-element.169), channel_id=1, replica_groups=mesh['curve'=64,'split'=8] {'curve','split'}, dimensions={0} | all-to-all | bytes 524288 | tf_op jit(solution)/shard_map/all_to_all | solution.py:696
  (30 shorter events, 12.2 us)
Async XLA Ops:
  8.7 14.6 %collective-permute-start = (f32[24,128]{1,0:T(8,128)S(1)}, f32[24,128]{1,0:T(8,128)S(1)}, u32[]{:S(2)}, u32[]{:S(2)}) collective-permute-start(f32[24,128]{1,0:T(8,128)S(1)} %get-tuple-element.100), channel_id=1, source_target_pairs={{0,1},{1,2},{2,3},{3,4},{4,5},{5,6},{6,7},{8,9},{9,10},{10,11},{11... | collective-permute-start | bytes 36872 | tf_op jit(solution)/shard_map/ppermute | solution.py:597
  12.7 11.9 %collective-permute-start.1 = (f32[24,128]{1,0:T(8,128)S(1)}, f32[24,128]{1,0:T(8,128)S(1)}, u32[]{:S(2)}, u32[]{:S(2)}) collective-permute-start(f32[24,128]{1,0:T(8,128)S(1)} %get-tuple-element.101), channel_id=1, source_target_pairs={{1,0},{2,1},{3,2},{4,3},{5,4},{6,5},{7,6},{9,8},{10,9},{11,10},{12... | collective-permute-start | bytes 36872 | tf_op jit(solution)/shard_map/ppermute | solution.py:597
  14.0 10.6 %collective-permute-start.2 = (f32[24,128]{1,0:T(8,128)S(1)}, f32[24,128]{1,0:T(8,128)S(1)}, u32[]{:S(2)}, u32[]{:S(2)}) collective-permute-start(f32[24,128]{1,0:T(8,128)S(1)} %get-tuple-element.102), channel_id=1, source_target_pairs={{0,16},{8,24},{16,32},{24,40},{32,48},{40,56},{48,64},{56,72},{64,... | collective-permute-start | bytes 36872 | tf_op jit(solution)/shard_map/ppermute | solution.py:597
  17.2 7.5 %collective-permute-start.3 = (f32[24,128]{1,0:T(8,128)S(1)}, f32[24,128]{1,0:T(8,128)S(1)}, u32[]{:S(2)}, u32[]{:S(2)}) collective-permute-start(f32[24,128]{1,0:T(8,128)S(1)} %get-tuple-element.103), channel_id=1, source_target_pairs={{0,8},{8,16},{16,24},{24,32},{32,40},{40,48},{48,56},{56,64},{64,7... | collective-permute-start | bytes 36872 | tf_op jit(solution)/shard_map/ppermute | solution.py:597
  21.4 5.0 %collective-permute-start.4 = (f32[24,128]{1,0:T(8,128)S(1)}, f32[24,128]{1,0:T(8,128)S(1)}, u32[]{:S(2)}, u32[]{:S(2)}) collective-permute-start(f32[24,128]{1,0:T(8,128)S(1)} %get-tuple-element.104), channel_id=1, source_target_pairs={{8,0},{16,8},{24,16},{32,24},{40,32},{48,40},{56,48},{64,56},{72,6... | collective-permute-start | bytes 36872 | tf_op jit(solution)/shard_map/ppermute | solution.py:597
  23.3 4.4 %collective-permute-start.5 = (f32[24,128]{1,0:T(8,128)S(1)}, f32[24,128]{1,0:T(8,128)S(1)}, u32[]{:S(2)}, u32[]{:S(2)}) collective-permute-start(f32[24,128]{1,0:T(8,128)S(1)} %get-tuple-element.105), channel_id=1, source_target_pairs={{16,0},{24,8},{32,16},{40,24},{48,32},{56,40},{64,48},{72,56},{80,... | collective-permute-start | bytes 36872 | tf_op jit(solution)/shard_map/ppermute | solution.py:597
  215.7 10.9 %collective-permute-start.6 = (f32[1,128]{1,0:T(1,128)S(1)}, f32[1,128]{1,0:T(1,128)S(1)}, u32[]{:S(2)}, u32[]{:S(2)}) collective-permute-start(f32[1,128]{1,0:T(1,128)S(1)} %get-tuple-element.163), channel_id=1, source_target_pairs={{0,1},{1,2},{2,3},{3,4},{4,5},{5,6},{6,7},{8,9},{9,10},{10,11},{11... | collective-permute-start | bytes 1544 | tf_op jit(solution)/shard_map/ppermute | solution.py:597
  217.9 10.0 %collective-permute-start.7 = (f32[1,128]{1,0:T(1,128)S(1)}, f32[1,128]{1,0:T(1,128)S(1)}, u32[]{:S(2)}, u32[]{:S(2)}) collective-permute-start(f32[1,128]{1,0:T(1,128)S(1)} %get-tuple-element.164), channel_id=1, source_target_pairs={{1,0},{2,1},{3,2},{4,3},{5,4},{6,5},{7,6},{9,8},{10,9},{11,10},{12... | collective-permute-start | bytes 1544 | tf_op jit(solution)/shard_map/ppermute | solution.py:597
  219.2 8.8 %collective-permute-start.8 = (f32[1,128]{1,0:T(1,128)S(1)}, f32[1,128]{1,0:T(1,128)S(1)}, u32[]{:S(2)}, u32[]{:S(2)}) collective-permute-start(f32[1,128]{1,0:T(1,128)S(1)} %get-tuple-element.165), channel_id=1, source_target_pairs={{0,16},{8,24},{16,32},{24,40},{32,48},{40,56},{48,64},{56,72},{64,... | collective-permute-start | bytes 1544 | tf_op jit(solution)/shard_map/ppermute | solution.py:597
  221.4 6.6 %collective-permute-start.9 = (f32[1,128]{1,0:T(1,128)S(1)}, f32[1,128]{1,0:T(1,128)S(1)}, u32[]{:S(2)}, u32[]{:S(2)}) collective-permute-start(f32[1,128]{1,0:T(1,128)S(1)} %get-tuple-element.166), channel_id=1, source_target_pairs={{0,8},{8,16},{16,24},{24,32},{32,40},{40,48},{48,56},{56,64},{64,7... | collective-permute-start | bytes 1544 | tf_op jit(solution)/shard_map/ppermute | solution.py:597
  224.7 4.9 %collective-permute-start.10 = (f32[1,128]{1,0:T(1,128)S(1)}, f32[1,128]{1,0:T(1,128)S(1)}, u32[]{:S(2)}, u32[]{:S(2)}) collective-permute-start(f32[1,128]{1,0:T(1,128)S(1)} %get-tuple-element.167), channel_id=1, source_target_pairs={{8,0},{16,8},{24,16},{32,24},{40,32},{48,40},{56,48},{64,56},{72,6... | collective-permute-start | bytes 1544 | tf_op jit(solution)/shard_map/ppermute | solution.py:597
  226.7 4.3 %collective-permute-start.11 = (f32[1,128]{1,0:T(1,128)S(1)}, f32[1,128]{1,0:T(1,128)S(1)}, u32[]{:S(2)}, u32[]{:S(2)}) collective-permute-start(f32[1,128]{1,0:T(1,128)S(1)} %get-tuple-element.168), channel_id=1, source_target_pairs={{16,0},{24,8},{32,16},{40,24},{48,32},{56,40},{64,48},{72,56},{80,... | collective-permute-start | bytes 1544 | tf_op jit(solution)/shard_map/ppermute | solution.py:597
